TPU v7x, 32 devices: a whole 2x2x4 slice. The times are simulated.
32 devices in a mesh: dp: 8 (over y, x, core), expert: 4 (over z).
Axes of the slice: x: 2, y: 2, z: 4, core: 2. Of those that a mesh axis runs over, the one named last changes fastest.
Arguments:
- hidden_in: bfloat16 [32, 128, 2048], P(('dp', 'expert')), may hold values from -6 to 6
- out_grad: bfloat16 [32, 128, 2048], P(('dp', 'expert')), may hold values from -6 to 6
- seq_lengths: int32 [32], P('dp'), may hold values from 72 to 128, as said below
- attn_choice: int32 [32, 128, 2], P('dp'), may hold values from 0 to 3, as said below
- moe_choice: int32 [32, 128, 2], P('dp'), may hold values from 0 to 3, as said below
- attn_gain: float32 [2048], P('dp'), may hold values from 0.5 to 1.5
- moe_gain: float32 [2048], P('dp'), may hold values from 0.5 to 1.5
- attn_router: float32 [2048, 4], P('dp'), may hold values from -0.25 to 0.25
- moe_router: float32 [2048, 4], P('dp'), may hold values from -0.25 to 0.25
- key_weight: float32 [2048, 2048], P('dp'), may hold values from -0.125 to 0.125
- value_weight: float32 [2048, 2048], P('dp'), may hold values from -0.125 to 0.125
- query_weight: float32 [4, 2048, 2048], P('expert', 'dp'), may hold values from -0.125 to 0.125
- output_weight: float32 [4, 2048, 2048], P('expert', 'dp'), may hold values from -0.5 to 0.5
- gate_weight: float32 [4, 2048, 5632], P('expert', None, 'dp'), may hold values from -0.125 to 0.125
- up_weight: float32 [4, 2048, 5632], P('expert', None, 'dp'), may hold values from -0.125 to 0.125
- down_weight: float32 [4, 5632, 2048], P('expert', 'dp'), may hold values from -0.078125 to 0.078125
Outputs:
- block_out: bfloat16 [32, 128, 2048], P(('dp', 'expert'))
- input_grad: bfloat16 [32, 128, 2048], P(('dp', 'expert'))
- attn_gain_grad: float32 [2048], P(('dp', 'expert'))
- moe_gain_grad: float32 [2048], P(('dp', 'expert'))
- attn_router_grad: float32 [2048, 4], P(('dp', 'expert'))
- moe_router_grad: float32 [2048, 4], P(('dp', 'expert'))
- key_grad: float32 [2048, 2048], P(('dp', 'expert'))
- value_grad: float32 [2048, 2048], P(('dp', 'expert'))
- query_grad: float32 [4, 2048, 2048], P('expert', 'dp')
- output_grad: float32 [4, 2048, 2048], P('expert', 'dp')
- gate_grad: float32 [4, 2048, 5632], P('expert', None, 'dp')
- up_grad: float32 [4, 2048, 5632], P('expert', None, 'dp')
- down_grad: float32 [4, 5632, 2048], P('expert', 'dp')
Inputs may be any that keep to these rules, and one draw needn't show every extreme that they name: `seq_lengths`: every aligned block of 4 sequences holds one of length 128. `attn_choice`: each token names 2 different experts. Over the positions below its sequence's length, no expert is named by more than 72 tokens of one sequence, and in every aligned block of 4 sequences some expert is named by exactly 72 live tokens of each of them. Entries at padded positions carry no meaning. `moe_choice`: as for attn_choice, drawn independently.
All inputs are finite; a program needn't handle non-finite values.
Results may differ from a plain program's by a relative error of at most 0.019.
The roundings to bfloat16 on the way count: a program that leaves them out, or rounds other values in their place, can miss the bound.
Values may be sent and summed in bfloat16 or wider, within the bound.
A program may use at most 384 MiB of HBM per device.

v0:
```python
from functools import partial

import jax
import jax.numpy as jnp
from jax import lax
from jax.sharding import PartitionSpec as P

HEADS = 16
HEAD = 128


eps = 1e-06
theta = 10000.0
highest = lax.Precision.HIGHEST


def rope_tables(positions, head_size):
    half_size = head_size // 2
    frequency = theta ** (-(jnp.arange(half_size, dtype=jnp.float32) * 2.0 / head_size))
    angles = positions.astype(jnp.float32)[:, None] * frequency[None, :]
    return (jnp.cos(angles), jnp.sin(angles))


def rotate(value, cosine, sine, direction):
    half_size = value.shape[-1] // 2
    former = value[..., :half_size]
    latter = value[..., half_size:]
    cosine = cosine[:, None, :]
    sine = direction * sine[:, None, :]
    return jnp.concatenate(
        [former * cosine - latter * sine, latter * cosine + former * sine], axis=-1
    )


def norm_scale(value):
    return lax.rsqrt(jnp.mean(value * value, axis=-1, keepdims=True) + eps)


def norm_backward(grad_normed, value, scale_value, gain_value):
    scaled_grad = grad_normed * gain_value
    gain_part = jnp.sum(grad_normed * value * scale_value, axis=0)
    grad_value = scale_value * scaled_grad - value * scale_value**3 * jnp.mean(
        scaled_grad * value, axis=-1, keepdims=True
    )
    return (grad_value, gain_part)


def softmax_rows(values):
    peak = jnp.max(values, axis=-1, keepdims=True)
    powers = jnp.exp(values - peak)
    return powers / jnp.sum(powers, axis=-1, keepdims=True)


def router_gates(logits, choices, live_rows, experts):
    onehot = (choices[:, :, None] == jnp.arange(experts, dtype=jnp.int32)[None, None, :]).astype(
        jnp.float32
    )
    chosen = jnp.sum(logits[:, None, :] * onehot, axis=-1)
    shares = softmax_rows(chosen)
    dense = jnp.sum((shares * live_rows[:, None])[:, :, None] * onehot, axis=1)
    return (onehot, shares, dense)


def gates_backward(grad_dense, onehot, shares, live_rows):
    grad_shares = jnp.sum(grad_dense[:, None, :] * onehot, axis=-1) * live_rows[:, None]
    grad_chosen = shares * (grad_shares - jnp.sum(shares * grad_shares, axis=-1, keepdims=True))
    return jnp.sum(grad_chosen[:, :, None] * onehot, axis=1)


def route_table(choices, length_value, experts, capacity):
    places = jnp.arange(choices.shape[0], dtype=jnp.int32)
    living = (places < length_value).astype(jnp.int32)
    picked = (
        jnp.sum(
            (choices[:, :, None] == jnp.arange(experts, dtype=jnp.int32)[None, None, :]).astype(
                jnp.int32
            ),
            axis=1,
        )
        * living[:, None]
    )
    slot_of = jnp.cumsum(picked, axis=0) - 1
    slot_ids = jnp.arange(capacity, dtype=jnp.int32)
    return (slot_of.T[:, None, :] == slot_ids[None, :, None]) & (picked.T[:, None, :] == 1)


def on_device(
    hidden_in,
    out_grad,
    seq_lengths,
    attn_choice,
    moe_choice,
    attn_gain,
    moe_gain,
    attn_router,
    moe_router,
    key_weight,
    value_weight,
    query_weight,
    output_weight,
    gate_weight,
    up_weight,
    down_weight,
):
    experts = lax.axis_size("expert")
    groups = lax.axis_size("dp")
    mine_index = lax.axis_index("expert")
    seq_len = hidden_in.shape[1]
    model_width = hidden_in.shape[2]
    head_width = query_weight.shape[2]
    capacity = 2 * seq_len // experts + 8
    total_rows = groups * experts * capacity
    score_scale = HEAD ** (-0.5)
    places = jnp.arange(seq_len, dtype=jnp.int32)
    own_length = lax.dynamic_index_in_dim(seq_lengths, mine_index, 0, keepdims=False)
    live_rows = (places < own_length).astype(jnp.float32)
    own_attn = lax.dynamic_index_in_dim(attn_choice, mine_index, 0, keepdims=False)
    own_moe = lax.dynamic_index_in_dim(moe_choice, mine_index, 0, keepdims=False)
    tabler = partial(route_table, experts=experts, capacity=capacity)
    dense = (
        lax.all_gather(attn_gain.astype(jnp.bfloat16), "dp", axis=0, tiled=True),
        lax.all_gather(moe_gain.astype(jnp.bfloat16), "dp", axis=0, tiled=True),
        lax.all_gather(attn_router.astype(jnp.bfloat16), "dp", axis=0, tiled=True),
        lax.all_gather(moe_router.astype(jnp.bfloat16), "dp", axis=0, tiled=True),
        lax.all_gather(key_weight.astype(jnp.bfloat16), "dp", axis=0, tiled=True),
        lax.all_gather(value_weight.astype(jnp.bfloat16), "dp", axis=0, tiled=True),
        lax.all_gather(query_weight.astype(jnp.bfloat16), "dp", axis=1, tiled=True),
        lax.all_gather(output_weight.astype(jnp.bfloat16), "dp", axis=1, tiled=True),
    )
    gain_attn = dense[0].astype(jnp.float32)
    gain_moe = dense[1].astype(jnp.float32)
    router_attn = dense[2]
    router_moe = dense[3]
    key_full = dense[4]
    value_full = dense[5]
    query_full = dense[6][0]
    output_full = dense[7][0]
    gate_slice = gate_weight[0].astype(jnp.bfloat16)
    up_slice = up_weight[0].astype(jnp.bfloat16)
    down_slice = down_weight[0].astype(jnp.bfloat16)
    inputs_f = hidden_in[0].astype(jnp.float32)
    scale_one = norm_scale(inputs_f)
    normed_one = (inputs_f * scale_one * gain_attn).astype(jnp.bfloat16)
    cos_home, sin_home = rope_tables(places, HEAD)
    key_pre = jnp.dot(normed_one, key_full, preferred_element_type=jnp.float32)
    keys_home = (
        rotate(key_pre.reshape(seq_len, HEADS, HEAD), cos_home, sin_home, 1.0)
        .astype(jnp.bfloat16)
        .reshape(seq_len, head_width)
    )
    values_home = jnp.dot(normed_one, value_full, preferred_element_type=jnp.float32).astype(
        jnp.bfloat16
    )
    send_keys = jnp.broadcast_to(keys_home[None], (experts, seq_len, head_width))
    send_values = jnp.broadcast_to(values_home[None], (experts, seq_len, head_width))
    attn_logits = jnp.dot(normed_one, router_attn, preferred_element_type=jnp.float32)
    onehot_attn, shares_attn, dense_attn = router_gates(attn_logits, own_attn, live_rows, experts)
    table_attn = tabler(own_attn, own_length).astype(jnp.bfloat16)
    send_attn = jnp.einsum(
        "ect,td->ecd", table_attn, normed_one, preferred_element_type=jnp.float32
    ).astype(jnp.bfloat16)
    recv_attn, keys_recv, values_recv = (
        lax.all_to_all(send_attn, "expert", split_axis=0, concat_axis=0, tiled=True),
        lax.all_to_all(send_keys, "expert", split_axis=0, concat_axis=0, tiled=True),
        lax.all_to_all(send_values, "expert", split_axis=0, concat_axis=0, tiled=True),
    )
    keys_all = keys_recv.reshape(experts, seq_len, HEADS, HEAD)
    values_all = values_recv.reshape(experts, seq_len, HEADS, HEAD)
    source_tables = jax.vmap(tabler)(attn_choice, seq_lengths)
    mine_tables = lax.dynamic_index_in_dim(source_tables, mine_index, 1, keepdims=False)
    positions = jnp.sum(jnp.where(mine_tables, places[None, None, :], 0), axis=-1)
    rows_flat = recv_attn.reshape(experts * capacity, model_width)
    query_pre = jnp.dot(rows_flat, query_full, preferred_element_type=jnp.float32)
    cos_far, sin_far = rope_tables(positions.reshape(-1), HEAD)
    queries = (
        rotate(query_pre.reshape(-1, HEADS, HEAD), cos_far, sin_far, 1.0)
        .astype(jnp.bfloat16)
        .reshape(experts, capacity, HEADS, HEAD)
    )
    causal = places[None, None, None, :] <= positions[:, None, :, None]
    score_raw = (
        jnp.einsum("sqhd,skhd->shqk", queries, keys_all, preferred_element_type=jnp.float32)
        * score_scale
    )
    masked = jnp.where(causal, score_raw, -1e30)
    peak = jnp.max(masked, axis=-1, keepdims=True)
    powers = jnp.exp(masked - peak)
    totals = jnp.sum(powers, axis=-1, keepdims=True)
    log_total = peak + jnp.log(totals)
    attn_probs = (powers / totals).astype(jnp.bfloat16)
    mixture = (
        jnp.einsum("shqk,skhd->sqhd", attn_probs, values_all, preferred_element_type=jnp.float32)
        .astype(jnp.bfloat16)
        .reshape(experts * capacity, head_width)
    )
    attn_rows = (
        jnp.dot(mixture, output_full, preferred_element_type=jnp.float32)
        .astype(jnp.bfloat16)
        .reshape(experts, capacity, model_width)
    )
    back_attn = lax.all_to_all(attn_rows, "expert", split_axis=0, concat_axis=0, tiled=True)
    spread_attn = jnp.einsum(
        "ect,ecd->etd", table_attn, back_attn, preferred_element_type=jnp.float32
    )
    attn_sum = jnp.sum(dense_attn.T[:, :, None] * spread_attn, axis=0)
    middle = inputs_f + attn_sum
    scale_two = norm_scale(middle)
    normed_two = (middle * scale_two * gain_moe).astype(jnp.bfloat16)
    moe_logits = jnp.dot(normed_two, router_moe, preferred_element_type=jnp.float32)
    onehot_moe, shares_moe, dense_moe = router_gates(moe_logits, own_moe, live_rows, experts)
    table_moe = tabler(own_moe, own_length).astype(jnp.bfloat16)
    send_moe = jnp.einsum(
        "ect,td->ecd", table_moe, normed_two, preferred_element_type=jnp.float32
    ).astype(jnp.bfloat16)
    grad_out = out_grad[0].astype(jnp.float32) * live_rows[:, None]
    rows_moe_grad = (dense_moe.T[:, :, None] * grad_out[None]).astype(jnp.bfloat16)
    send_moe_grad = jnp.einsum(
        "ect,etd->ecd", table_moe, rows_moe_grad, preferred_element_type=jnp.float32
    ).astype(jnp.bfloat16)
    recv_moe, recv_moe_grad = (
        lax.all_to_all(send_moe, "expert", split_axis=0, concat_axis=0, tiled=True),
        lax.all_to_all(send_moe_grad, "expert", split_axis=0, concat_axis=0, tiled=True),
    )
    rows_all, grad_rows_all = (
        lax.all_gather(recv_moe, "dp", axis=0, tiled=True),
        lax.all_gather(recv_moe_grad, "dp", axis=0, tiled=True),
    )
    ffn_rows = rows_all.reshape(total_rows, model_width)
    gate_pre = jnp.dot(ffn_rows, gate_slice, preferred_element_type=jnp.float32)
    up_pre = jnp.dot(ffn_rows, up_slice, preferred_element_type=jnp.float32)
    sigmoid_gate = 1.0 / (1.0 + jnp.exp(-gate_pre))
    activated = gate_pre * sigmoid_gate
    hidden_rows = (activated * up_pre).astype(jnp.bfloat16)
    partial_out = jnp.dot(hidden_rows, down_slice, preferred_element_type=jnp.float32).reshape(
        groups, experts, capacity, model_width
    )
    summed_out = lax.psum_scatter(
        partial_out.astype(jnp.bfloat16), "dp", scatter_dimension=0, tiled=True
    ).astype(jnp.float32)
    back_moe = lax.all_to_all(
        summed_out[0].astype(jnp.bfloat16), "expert", split_axis=0, concat_axis=0, tiled=True
    )
    spread_moe = jnp.einsum("ect,ecd->etd", table_moe, back_moe, preferred_element_type=jnp.float32)
    moe_sum = jnp.sum(dense_moe.T[:, :, None] * spread_moe, axis=0)
    block_out = (live_rows[:, None] * (middle + moe_sum)).astype(jnp.bfloat16)[None]
    grad_dense_moe = jnp.sum(grad_out[None] * spread_moe, axis=-1).T
    grad_rows = grad_rows_all.reshape(total_rows, model_width)
    grad_hidden = jnp.einsum("rd,fd->rf", grad_rows, down_slice, preferred_element_type=jnp.float32)
    slope = sigmoid_gate * (1.0 + gate_pre * (1.0 - sigmoid_gate))
    grad_gate = (grad_hidden * up_pre * slope).astype(jnp.bfloat16)
    grad_up = (grad_hidden * activated).astype(jnp.bfloat16)
    grad_ffn_part = (
        jnp.einsum("rf,df->rd", grad_gate, gate_slice, preferred_element_type=jnp.float32)
        + jnp.einsum("rf,df->rd", grad_up, up_slice, preferred_element_type=jnp.float32)
    ).reshape(groups, experts, capacity, model_width)
    grad_ffn_summed = lax.psum_scatter(grad_ffn_part, "dp", scatter_dimension=0, tiled=True)
    back_moe_grad = lax.all_to_all(
        grad_ffn_summed[0].astype(jnp.bfloat16), "expert", split_axis=0, concat_axis=0, tiled=True
    )
    down_grad = jnp.einsum("rf,rd->fd", hidden_rows, grad_rows, preferred_element_type=jnp.float32)[
        None
    ]
    gate_grad = jnp.einsum("rd,rf->df", ffn_rows, grad_gate, preferred_element_type=jnp.float32)[
        None
    ]
    up_grad = jnp.einsum("rd,rf->df", ffn_rows, grad_up, preferred_element_type=jnp.float32)[None]
    grad_normed_two = jnp.einsum(
        "ect,ecd->td", table_moe, back_moe_grad, preferred_element_type=jnp.float32
    )
    grad_logits_moe = gates_backward(grad_dense_moe, onehot_moe, shares_moe, live_rows)
    grad_normed_two = grad_normed_two + jnp.dot(
        grad_logits_moe, router_moe.astype(jnp.float32).T, precision=highest
    )
    moe_router_part = jnp.dot(normed_two.astype(jnp.float32).T, grad_logits_moe, precision=highest)
    grad_middle_norm, moe_gain_part = norm_backward(grad_normed_two, middle, scale_two, gain_moe)
    grad_middle = grad_out + grad_middle_norm
    grad_dense_attn = jnp.sum(grad_middle[None] * spread_attn, axis=-1).T
    rows_attn_grad = (dense_attn.T[:, :, None] * grad_middle[None]).astype(jnp.bfloat16)
    send_attn_grad = jnp.einsum(
        "ect,etd->ecd", table_attn, rows_attn_grad, preferred_element_type=jnp.float32
    ).astype(jnp.bfloat16)
    recv_attn_grad = lax.all_to_all(
        send_attn_grad, "expert", split_axis=0, concat_axis=0, tiled=True
    )
    grad_heads_rows = recv_attn_grad.reshape(experts * capacity, model_width)
    output_grad = jnp.einsum(
        "re,rd->ed", mixture, grad_heads_rows, preferred_element_type=jnp.float32
    )
    grad_mixture = (
        jnp.einsum("rd,ed->re", grad_heads_rows, output_full, preferred_element_type=jnp.float32)
        .astype(jnp.bfloat16)
        .reshape(experts, capacity, HEADS, HEAD)
    )
    score_again = (
        jnp.einsum("sqhd,skhd->shqk", queries, keys_all, preferred_element_type=jnp.float32)
        * score_scale
    )
    probs_again = jnp.where(causal, jnp.exp(jnp.where(causal, score_again, -1e30) - log_total), 0.0)
    grad_probs = jnp.einsum(
        "sqhd,skhd->shqk", grad_mixture, values_all, preferred_element_type=jnp.float32
    )
    inner_sum = jnp.sum(probs_again * grad_probs, axis=-1, keepdims=True)
    grad_scores = (probs_again * (grad_probs - inner_sum)).astype(jnp.bfloat16)
    values_part = jnp.einsum(
        "shqk,sqhd->skhd",
        probs_again.astype(jnp.bfloat16),
        grad_mixture,
        preferred_element_type=jnp.float32,
    )
    grad_queries = (
        jnp.einsum("shqk,skhd->sqhd", grad_scores, keys_all, preferred_element_type=jnp.float32)
        * score_scale
    )
    keys_part = (
        jnp.einsum("shqk,sqhd->skhd", grad_scores, queries, preferred_element_type=jnp.float32)
        * score_scale
    )
    grad_query_pre = (
        rotate(grad_queries.reshape(-1, HEADS, HEAD), cos_far, sin_far, -1.0)
        .astype(jnp.bfloat16)
        .reshape(experts * capacity, head_width)
    )
    query_grad = jnp.einsum(
        "rd,re->de", rows_flat, grad_query_pre, preferred_element_type=jnp.float32
    )
    grad_rows_attn = (
        jnp.einsum("re,de->rd", grad_query_pre, query_full, preferred_element_type=jnp.float32)
        .astype(jnp.bfloat16)
        .astype(jnp.float32)
        .reshape(experts, capacity, model_width)
    )
    back_rows, keys_back, values_back = (
        lax.all_to_all(
            grad_rows_attn.astype(jnp.bfloat16), "expert", split_axis=0, concat_axis=0, tiled=True
        ).astype(grad_rows_attn.dtype),
        lax.all_to_all(
            keys_part.reshape(experts, seq_len, head_width).astype(jnp.bfloat16),
            "expert",
            split_axis=0,
            concat_axis=0,
            tiled=True,
        ).astype(jnp.float32),
        lax.all_to_all(
            values_part.reshape(experts, seq_len, head_width).astype(jnp.bfloat16),
            "expert",
            split_axis=0,
            concat_axis=0,
            tiled=True,
        ).astype(jnp.float32),
    )
    grad_keys = jnp.sum(keys_back, axis=0)
    grad_values = jnp.sum(values_back, axis=0).astype(jnp.bfloat16)
    grad_key_pre = (
        rotate(grad_keys.reshape(seq_len, HEADS, HEAD), cos_home, sin_home, -1.0)
        .astype(jnp.bfloat16)
        .reshape(seq_len, head_width)
    )
    key_part = jnp.einsum("td,te->de", normed_one, grad_key_pre, preferred_element_type=jnp.float32)
    value_part = jnp.einsum(
        "td,te->de", normed_one, grad_values, preferred_element_type=jnp.float32
    )
    grad_logits_attn = gates_backward(grad_dense_attn, onehot_attn, shares_attn, live_rows)
    attn_router_part = jnp.dot(
        normed_one.astype(jnp.float32).T, grad_logits_attn, precision=highest
    )
    grad_normed_one = jnp.einsum(
        "ect,ecd->td",
        table_attn,
        back_rows.astype(jnp.bfloat16),
        preferred_element_type=jnp.float32,
    )
    grad_normed_one = grad_normed_one + jnp.einsum(
        "te,de->td", grad_key_pre, key_full, preferred_element_type=jnp.float32
    )
    grad_normed_one = grad_normed_one + jnp.einsum(
        "te,de->td", grad_values, value_full, preferred_element_type=jnp.float32
    )
    grad_normed_one = grad_normed_one + jnp.dot(
        grad_logits_attn, router_attn.astype(jnp.float32).T, precision=highest
    )
    grad_inputs_norm, attn_gain_part = norm_backward(
        grad_normed_one, inputs_f, scale_one, gain_attn
    )
    input_grad = (grad_middle + grad_inputs_norm).astype(jnp.bfloat16)[None]
    shared_grads = (
        lax.psum_scatter(attn_gain_part, ("dp", "expert"), scatter_dimension=0, tiled=True),
        lax.psum_scatter(moe_gain_part, ("dp", "expert"), scatter_dimension=0, tiled=True),
        lax.psum_scatter(attn_router_part, ("dp", "expert"), scatter_dimension=0, tiled=True),
        lax.psum_scatter(moe_router_part, ("dp", "expert"), scatter_dimension=0, tiled=True),
        lax.psum_scatter(key_part, ("dp", "expert"), scatter_dimension=0, tiled=True),
        lax.psum_scatter(value_part, ("dp", "expert"), scatter_dimension=0, tiled=True),
    )
    attention_sums = (
        lax.psum_scatter(
            query_grad[None].astype(jnp.bfloat16), "dp", scatter_dimension=1, tiled=True
        ).astype(jnp.float32),
        lax.psum_scatter(
            output_grad[None].astype(jnp.bfloat16), "dp", scatter_dimension=1, tiled=True
        ).astype(jnp.float32),
    )
    return (
        block_out,
        input_grad,
        shared_grads[0],
        shared_grads[1],
        shared_grads[2],
        shared_grads[3],
        shared_grads[4],
        shared_grads[5],
        attention_sums[0],
        attention_sums[1],
        gate_grad,
        up_grad,
        down_grad,
    )


def solution(mesh):
    placed = (
        P(("dp", "expert"), None, None),
        P(("dp", "expert"), None, None),
        P("dp"),
        P("dp", None, None),
        P("dp", None, None),
        P("dp"),
        P("dp"),
        P("dp", None),
        P("dp", None),
        P("dp", None),
        P("dp", None),
        P("expert", "dp", None),
        P("expert", "dp", None),
        P("expert", None, "dp"),
        P("expert", None, "dp"),
        P("expert", "dp", None),
    )
    return jax.shard_map(
        on_device,
        mesh=mesh,
        in_specs=placed,
        out_specs=(
            P(("dp", "expert"), None, None),
            P(("dp", "expert"), None, None),
            P(("dp", "expert")),
            P(("dp", "expert")),
            P(("dp", "expert"), None),
            P(("dp", "expert"), None),
            P(("dp", "expert"), None),
            P(("dp", "expert"), None),
            P("expert", "dp", None),
            P("expert", "dp", None),
            P("expert", None, "dp"),
            P("expert", None, "dp"),
            P("expert", "dp", None),
        ),
        check_vma=False,
    )
```

profile of v0, /device:TPU:0, one launch (start us, length us, event | category | flops | bytes accessed | tf_op | source)
XLA Modules:
  0.0 1903.1 jit_solution(11162149611562344294)
XLA Ops:
  7.3 2.9 convert_element_type.335
  15.6 10.4 all-gather
  30.5 4.9 all-to-all-start.1
  36.2 31.4 %all-gather.13.cloned.1.call-done = bf16[2048,2048]{1,0:T(8,128)(2,1)} async-done(((bf16[256,2048]{1,0:T(8,128)(2,1)}), bf16[2048,2048]{1,0:T(8,128)(2,1)}) %all-gather.13.cloned.1.call-update) | async-done | bytes 8388624 | tf_op jit(solution)/shard_map/all_gather | solution.py:125
  67.6 12.4 copy.110
  80.0 5.8 fusion.89
  87.8 4.6 all-to-all-start.2
  92.4 32.1 %all-gather.9.cloned.1.call-done = bf16[2048,2048]{1,0:T(8,128)(2,1)} async-done(((bf16[256,2048]{1,0:T(8,128)(2,1)}), bf16[2048,2048]{1,0:T(8,128)(2,1)}) %all-gather.9.cloned.1.call-update) | async-done | bytes 8388624 | tf_op jit(solution)/shard_map/all_gather | solution.py:126
  124.5 5.5 convolution_convert_fusion.5
  131.3 9.7 all-to-all-done.2
  143.0 4.9 all-to-all-start
  150.2 31.2 %all-gather.11.cloned.1.call-done = bf16[1,2048,2048]{2,1,0:T(8,128)(2,1)} async-done(((bf16[1,256,2048]{2,1,0:T(8,128)(2,1)}), bf16[1,2048,2048]{2,1,0:T(8,128)(2,1)}) %all-gather.11.cloned.1.call-update) | async-done | bytes 8388624 | tf_op jit(solution)/shard_map/all_gather | solution.py:127
  181.4 12.4 copy.107
  193.8 5.4 fusion.143
  204.7 2.9 fusion.46
  208.8 29.3 %all-gather.15.cloned.1.call-done = bf16[1,2048,2048]{2,1,0:T(8,128)(2,1)} async-done(((bf16[1,256,2048]{2,1,0:T(8,128)(2,1)}), bf16[1,2048,2048]{2,1,0:T(8,128)(2,1)}) %all-gather.15.cloned.1.call-update) | async-done | bytes 8388624 | tf_op jit(solution)/shard_map/all_gather | solution.py:128
  238.1 7.4 fusion.20
  245.5 4.7 all-to-all-start.3
  250.3 8.8 all-gather.1
  260.1 7.9 all_gather.31
  270.3 9.0 all-to-all-done.3
  279.3 4.2 multiply_reduce_fusion.3
  285.1 31.4 %all_to_all.60 = bf16[4,72,2048]{2,1,0:T(8,128)(2,1)} all-to-all(bf16[4,72,2048]{2,1,0:T(8,128)(2,1)S(1)} %convolution_convert_fusion.3), channel_id=1, replica_groups=mesh['dp'=8,'expert'=4] {'expert'}, dimensions={0} | all-to-all | bytes 2359296 | tf_op jit(solution)/shard_map/all_to_all | solution.py:221
  316.6 8.9 all_gather.37
  335.4 32.5 %all_to_all.61 = bf16[4,72,2048]{2,1,0:T(8,128)(2,1)} all-to-all(bf16[4,72,2048]{2,1,0:T(8,128)(2,1)S(1)} %convolution_convert_fusion.2), channel_id=1, replica_groups=mesh['dp'=8,'expert'=4] {'expert'}, dimensions={0} | all-to-all | bytes 2359296 | tf_op jit(solution)/shard_map/all_to_all | solution.py:222
  367.9 5.7 all-gather.17.cloned.1.call-done
  373.6 14.0 fusion.11
  387.6 10.8 fusion.15
  398.4 35.8 %all-gather.19.cloned.1.call-done = bf16[32,72,2048]{2,1,0:T(8,128)(2,1)} async-done(((bf16[4,72,2048]{2,1,0:T(8,128)(2,1)}), bf16[32,72,2048]{2,1,0:T(8,128)(2,1)}) %all-gather.19.cloned.1.call-update) | async-done | bytes 9437200 | tf_op jit(solution)/shard_map/all_gather | solution.py:226
  434.2 18.6 multiply_convert_fusion
  452.8 5.6 copy.116
  458.4 13.0 convolution_convert_fusion
  471.5 16.9 fusion.13
  488.4 20.0 %convolution_add_fusion = f32[2304,2048]{1,0:T(8,128)} fusion(f32[2304,2048]{1,0:T(8,128)} %fusion.13, bf16[2304,704]{0,1:T(8,128)(2,1)S(1)} %copy-done.65, f32[1,2048,704]{1,2,0:T(8,128)} %param.30), kind=kOutput, calls=%fused_computation | convolution fusion | flops 6649937920 | bytes 46759936 | tf_op jit(solution)/shard_map/rf,df->rd/dot_general | solution.py:254
  508.5 39.7 %reduce-scatter.13.cloned.1.call-done = bf16[1,4,72,2048]{3,2,1,0:T(8,128)(2,1)} async-done(((bf16[8,4,72,2048]{3,2,1,0:T(8,128)(2,1)}), bf16[1,4,72,2048]{3,2,1,0:T(8,128)(2,1)}) %reduce-scatter.13.cloned.1.call-update) | async-done | bytes 1179664 | tf_op jit(solution)/shard_map/reduce_scatter | solution.py:237
  548.1 4.6 all-to-all-start.5
  552.7 125.2 %reduce-scatter.15.cloned.1.call-done = f32[1,4,72,2048]{3,2,1,0:T(8,128)} async-done(((f32[8,4,72,2048]{3,2,1,0:T(8,128)}), f32[1,4,72,2048]{3,2,1,0:T(8,128)}) %reduce-scatter.15.cloned.1.call-update) | async-done | bytes 2359312 | tf_op jit(solution)/shard_map/reduce_scatter | solution.py:256
  680.7 5.0 all-to-all-start.7
  685.8 3.7 multiply_reduce_fusion.1
  690.2 24.2 %all-to-all-done.7 = bf16[4,72,2048]{2,1,0:T(8,128)(2,1)} async-done(((bf16[4,72,2048]{2,1,0:T(8,128)(2,1)}), bf16[4,72,2048]{2,1,0:T(8,128)(2,1)}, u32[]{:S(2)}, u32[]{:S(2)}) %all-to-all-start.7) | async-done | bytes 1179680 | tf_op jit(solution)/shard_map/all_to_all | solution.py:257
  721.6 4.3 all-to-all-start.8
  733.2 23.7 %all-to-all-done.8 = bf16[4,72,2048]{2,1,0:T(8,128)(2,1)} async-done(((bf16[4,72,2048]{2,1,0:T(8,128)(2,1)}), bf16[4,72,2048]{2,1,0:T(8,128)(2,1)}, u32[]{:S(2)}, u32[]{:S(2)}) %all-to-all-start.8) | async-done | bytes 1179680 | tf_op jit(solution)/shard_map/all_to_all | solution.py:282
  756.9 6.4 fusion.47
  763.6 3.7 multiply_reduce_fusion.4
  773.7 7.0 convert_bitcast_fusion.1
  780.8 9.6 convert_bitcast_fusion
  790.5 3.8 multiply_convert_fusion.3
  794.3 59.2 %all_to_all.62 = bf16[4,128,2048]{1,2,0:T(8,128)(2,1)S(1)} all-to-all(bf16[4,128,2048]{1,2,0:T(8,128)(2,1)S(1)} %bitcast.283), channel_id=1, replica_groups=mesh['dp'=8,'expert'=4] {'expert'}, dimensions={0} | all-to-all | bytes 4194304 | tf_op jit(solution)/shard_map/all_to_all | solution.py:336
  854.5 8.2 fusion.91
  865.6 57.4 %all_to_all.63 = bf16[4,128,2048]{1,2,0:T(8,128)(2,1)S(1)} all-to-all(bf16[4,128,2048]{1,2,0:T(8,128)(2,1)S(1)} %bitcast.282), channel_id=1, replica_groups=mesh['dp'=8,'expert'=4] {'expert'}, dimensions={0} | all-to-all | bytes 4194304 | tf_op jit(solution)/shard_map/all_to_all | solution.py:343
  924.2 9.2 fusion.132
  933.5 12.1 convolution_bitcast_fusion.2
  945.6 11.1 convolution_bitcast_fusion
  956.8 3.8 fusion.17
  960.5 4.5 all-to-all-start.9
  965.1 12.1 convolution_bitcast_fusion.1
  979.6 34.0 %reduce-scatter.25.cloned.1.call-done = f32[64,4]{1,0:T(8,128)} async-done(((f32[2048,4]{1,0:T(8,128)}), f32[64,4]{1,0:T(8,128)}) %reduce-scatter.25.cloned.1.call-update) | async-done | bytes 1040
  1015.0 6.3 fusion.146
  1021.4 7.3 fusion.145
  1031.7 39.1 %all-reduce.2 = (f32[2048]{0:T(1024)S(1)}, f32[2048]{0:T(1024)S(1)}) all-reduce(f32[2048]{0:T(1024)S(1)} %get-tuple-element.17, f32[2048]{0:T(1024)S(1)} %copy-done.42), channel_id=4, replica_groups=mesh['dp'=8,'expert'=4] {'dp','expert'}, use_global_device_ids=true, to_apply=%region_37.38.clone | all-reduce | flops 4096 | bytes 32768
  1073.3 15.8 reduce-scatter.21.cloned.1.call-done
  1091.9 72.2 %reduce-scatter.23.cloned.1.call-done = bf16[1,256,2048]{2,1,0:T(8,128)(2,1)} async-done(((bf16[1,2048,2048]{2,1,0:T(8,128)(2,1)}), bf16[1,256,2048]{2,1,0:T(8,128)(2,1)}) %reduce-scatter.23.cloned.1.call-update) | async-done | bytes 1048592 | tf_op jit(solution)/shard_map/reduce_scatter | solution.py:397
  1167.0 364.3 %reduce-scatter.17.cloned.1.call-done = f32[64,2048]{1,0:T(8,128)} async-done(((f32[2048,2048]{1,0:T(8,128)}), f32[64,2048]{1,0:T(8,128)}) %reduce-scatter.17.cloned.1.call-update) | async-done | bytes 524304 | tf_op jit(solution)/shard_map/reduce_scatter | solution.py:390
  1531.3 364.9 %reduce-scatter.19.cloned.1.call-done = f32[64,2048]{1,0:T(8,128)} async-done(((f32[2048,2048]{1,0:T(8,128)}), f32[64,2048]{1,0:T(8,128)}) %reduce-scatter.19.cloned.1.call-update) | async-done | bytes 524304 | tf_op jit(solution)/shard_map/reduce_scatter | solution.py:391
  (285 shorter events, 84.3 us)
Async XLA Ops:
  7.2 20.0 %copy-start = (s32[4,128,2]{1,2,0:T(2,128)S(1)}, s32[4,128,2]{1,2,0:T(2,128)}, u32[]{:S(2)}) copy-start(s32[4,128,2]{1,2,0:T(2,128)} %param.20) | copy-start | bytes 12292
  7.2 3.0 copy-start.16
  7.2 60.4 %all-gather.13.cloned.1.call-start = ((), (), s32[]{:S(2)}) async-start(), calls=%async_computation.22 | async-start | bytes 9437184 | tf_op jit(solution)/shard_map/all_gather | solution.py:125
  10.1 114.4 %all-gather.9.cloned.1.call-start = ((), (), s32[]{:S(2)}) async-start(), calls=%async_computation.20 | async-start | bytes 9437184 | tf_op jit(solution)/shard_map/all_gather | solution.py:126
  11.3 3.0 copy-start.17
  11.4 170.1 %all-gather.11.cloned.1.call-start = ((), (), s32[]{:S(2)}) async-start(), calls=%async_computation.21 | async-start | bytes 9437184 | tf_op jit(solution)/shard_map/all_gather | solution.py:127
  14.3 11.6 copy-start.60
  14.3 12.9 copy-start.54
  14.3 13.8 copy-start.2
  14.3 223.8 %all-gather.15.cloned.1.call-start = ((), (), s32[]{:S(2)}) async-start(), calls=%async_computation.23 | async-start | bytes 9437184 | tf_op jit(solution)/shard_map/all_gather | solution.py:128
  27.2 3.3 copy-start.40
  27.3 241.1 %copy-start.38 = (s32[128,2]{0,1:T(2,128)}, s32[128,2]{0,1:T(2,128)S(1)}, u32[]{:S(2)}) copy-start(s32[128,2]{0,1:T(2,128)S(1)} %dynamic-slice_bitcast_fusion.1) | copy-start | bytes 3076
  27.8 2.7 copy-start.46
  28.2 690.9 %copy-start.34 = (s32[4,128]{1,0:T(4,128)}, s32[4,128]{1,0:T(4,128)S(1)}, u32[]{:S(2)}) copy-start(s32[4,128]{1,0:T(4,128)S(1)} %copy.102) | copy-start | bytes 6148
  30.5 55.5 %all-to-all-start.1 = ((bf16[4,72,2048]{2,1,0:T(8,128)(2,1)}), bf16[4,72,2048]{2,1,0:T(8,128)(2,1)S(1)}, u32[]{:S(2)}, u32[]{:S(2)}) async-start(bf16[4,72,2048]{2,1,0:T(8,128)(2,1)} %convolution_convert_fusion.4), calls=%async_computation.1 | async-start | bytes 2359296 | tf_op jit(solution)/shard_map/all_to_all | solution.py:163
  36.2 49.6 %copy-start.29 = (f32[128,64]{0,1:T(8,128)}, f32[128,64]{0,1:T(8,128)S(1)}, u32[]{:S(2)}) copy-start(f32[128,64]{0,1:T(8,128)S(1)} %get-tuple-element.47) | copy-start | bytes 98308
  87.8 53.2 %all-to-all-start.2 = ((bf16[4,128,2048]{1,2,0:T(8,128)(2,1)}), bf16[4,128,2048]{1,2,0:T(8,128)(2,1)S(1)}, u32[]{:S(2)}, u32[]{:S(2)}) async-start(bf16[4,128,2048]{1,2,0:T(8,128)(2,1)} %broadcast_in_dim.46), calls=%async_computation.2 | async-start | bytes 4194304 | tf_op jit(solution)/shard_map/all_to_all | solution.py:164
  143.0 61.7 %all-to-all-start = ((bf16[4,128,2048]{1,2,0:T(8,128)(2,1)}), bf16[4,128,2048]{1,2,0:T(8,128)(2,1)}, u32[]{:S(2)}, u32[]{:S(2)}) async-start(bf16[4,128,2048]{1,2,0:T(8,128)(2,1)} %broadcast_in_dim.38), calls=%async_computation | async-start | bytes 4194304 | tf_op jit(solution)/shard_map/all_to_all | solution.py:165
  150.2 49.0 %copy-start.19 = (f32[288,64]{1,0:T(8,128)}, f32[288,64]{1,0:T(8,128)S(1)}, u32[]{:S(2)}) copy-start(f32[288,64]{1,0:T(8,128)S(1)} %get-tuple-element.44) | copy-start | bytes 221188
  200.1 2.7 copy-start.12
  245.5 4.7 copy-start.64
  245.5 4.8 copy-start.57
  245.5 33.8 %copy-start.47 = (pred[4,128]{1,0:T(4,128)(4,1)S(1)}, pred[4,128]{1,0:T(4,128)(4,1)}, u32[]{:S(2)}) copy-start(pred[4,128]{1,0:T(4,128)(4,1)} %copy-done.46) | copy-start | bytes 1540
  245.5 33.8 %all-to-all-start.3 = ((bf16[4,72,2048]{2,1,0:T(8,128)(2,1)}), bf16[4,72,2048]{2,1,0:T(8,128)(2,1)}, u32[]{:S(2)}, u32[]{:S(2)}) async-start(bf16[4,72,2048]{2,1,0:T(8,128)(2,1)} %bitcast.302), calls=%async_computation.3 | async-start | bytes 2359296 | tf_op jit(solution)/shard_map/all_to_all | solution.py:201
  250.3 123.4 %all-gather.17.cloned.1.call-start = ((), (), s32[]{:S(2)}) async-start(), calls=%async_computation.24 | async-start | bytes 10616832 | tf_op jit(solution)/shard_map/all_gather | solution.py:225
  268.1 15.4 copy-start.32
  269.1 449.5 %copy-start.36 = (f32[128]{0:T(128)}, f32[128]{0:T(128)S(1)}, u32[]{:S(2)}) copy-start(f32[128]{0:T(128)S(1)} %compare_convert_fusion.1) | copy-start | bytes 1540
  270.3 13.2 copy-start.44
  284.3 32.2 %copy-start.55 = (f32[128]{0:T(128)}, f32[128]{0:T(128)S(1)}, u32[]{:S(2)}) copy-start(f32[128]{0:T(128)S(1)} %get-tuple-element.51) | copy-start | bytes 1540
  284.6 32.0 %copy-start.58 = (f32[256,4]{0,1:T(4,128)S(1)}, f32[256,4]{0,1:T(4,128)}, u32[]{:S(2)}) copy-start(f32[256,4]{0,1:T(4,128)} %param.24) | copy-start | bytes 12292
  316.5 117.7 %all-gather.19.cloned.1.call-start = ((), (), s32[]{:S(2)}) async-start(), calls=%async_computation.26 | async-start | bytes 10616832 | tf_op jit(solution)/shard_map/all_gather | solution.py:226
  367.9 180.3 %reduce-scatter.13.cloned.1.call-start = ((), (), s32[]{:S(2)}) async-start(), calls=%async_computation.25 | async-start | bytes 10616832 | tf_op jit(solution)/shard_map/reduce_scatter | solution.py:237
  373.6 14.0 copy-start.62
  471.5 206.4 %reduce-scatter.15.cloned.1.call-start = ((), (), s32[]{:S(2)}) async-start(), calls=%async_computation.27 | async-start | bytes 21233664 | tf_op jit(solution)/shard_map/reduce_scatter | solution.py:256
  471.5 16.9 copy-start.65
  548.1 132.6 %all-to-all-start.5 = ((bf16[4,72,2048]{2,1,0:T(8,128)(2,1)}), bf16[4,72,2048]{2,1,0:T(8,128)(2,1)}, u32[]{:S(2)}, u32[]{:S(2)}) async-start(bf16[4,72,2048]{2,1,0:T(8,128)(2,1)} %bitcast.304), calls=%async_computation.6 | async-start | bytes 2359296 | tf_op jit(solution)/shard_map/all_to_all | solution.py:240
  680.7 33.6 %all-to-all-start.7 = ((bf16[4,72,2048]{2,1,0:T(8,128)(2,1)}), bf16[4,72,2048]{2,1,0:T(8,128)(2,1)}, u32[]{:S(2)}, u32[]{:S(2)}) async-start(bf16[4,72,2048]{2,1,0:T(8,128)(2,1)} %convert_bitcast_fusion.4), calls=%async_computation.9 | async-start | bytes 2359296 | tf_op jit(solution)/shard_map/all_to_all | solution.py:257
  685.7 3.8 copy-start.41
  685.7 3.8 copy-start.51
  721.6 35.3 %all-to-all-start.8 = ((bf16[4,72,2048]{2,1,0:T(8,128)(2,1)}), bf16[4,72,2048]{2,1,0:T(8,128)(2,1)}, u32[]{:S(2)}, u32[]{:S(2)}) async-start(bf16[4,72,2048]{2,1,0:T(8,128)(2,1)} %convolution_convert_fusion.1), calls=%async_computation.10 | async-start | bytes 2359296 | tf_op jit(solution)/shard_map/all_to_all | solution.py:282
  725.9 252.3 %reduce-scatter.27.cloned.1.call-start = ((), (), s32[]{:S(2)}) async-start(), calls=%async_computation.33 | async-start | bytes 1081344
  728.4 285.2 %reduce-scatter.25.cloned.1.call-start = ((), (), s32[]{:S(2)}) async-start(), calls=%async_computation.32 | async-start | bytes 1081344
  728.4 2.9 copy-start.39
  728.4 2.9 copy-start.37
  728.4 2.9 copy-start.50
  733.2 356.0 %reduce-scatter.21.cloned.1.call-start = ((), (), s32[]{:S(2)}) async-start(), calls=%async_computation.30 | async-start | bytes 9437184 | tf_op jit(solution)/shard_map/reduce_scatter | solution.py:394
  763.6 3.7 copy-start.11
  780.8 383.4 %reduce-scatter.23.cloned.1.call-start = ((), (), s32[]{:S(2)}) async-start(), calls=%async_computation.31 | async-start | bytes 9437184 | tf_op jit(solution)/shard_map/reduce_scatter | solution.py:397
  790.4 740.8 %reduce-scatter.17.cloned.1.call-start = ((), (), s32[]{:S(2)}) async-start(), calls=%async_computation.28 | async-start | bytes 17301504 | tf_op jit(solution)/shard_map/reduce_scatter | solution.py:390
  862.8 1033.4 %reduce-scatter.19.cloned.1.call-start = ((), (), s32[]{:S(2)}) async-start(), calls=%async_computation.29 | async-start | bytes 17301504 | tf_op jit(solution)/shard_map/reduce_scatter | solution.py:391
  933.4 12.1 copy-start.66
  933.5 23.3 %slice-start = ((s8[8388608]{0:T(1024)(128)(4,1)}), s8[4194304]{0:T(1024)(128)(4,1)S(1)}, s32[]{:S(2)}) async-start(s8[8388608]{0:T(1024)(128)(4,1)} %bitcast.279), calls=%async_computation.34 | async-start | bytes 8388608
  945.6 11.2 slice-start.1
  945.6 11.2 copy-start.22
  945.6 11.2 copy-start.24
  960.5 68.1 %all-to-all-start.9 = ((bf16[4,72,2048]{2,1,0:T(8,128)(2,1)}), bf16[4,72,2048]{2,1,0:T(8,128)(2,1)}, u32[]{:S(2)}, u32[]{:S(2)}) async-start(bf16[4,72,2048]{2,1,0:T(8,128)(2,1)} %bitcast.303), calls=%async_computation.11 | async-start | bytes 2359296 | tf_op jit(solution)/shard_map/all_to_all | solution.py:333
  965.1 12.1 copy-start.5
  965.1 12.1 copy-start.27
  977.2 37.8 %copy-start.15 = (bf16[128,2048]{0,1:T(8,128)(2,1)S(1)}, bf16[128,2048]{0,1:T(8,128)(2,1)}, u32[]{:S(2)}) copy-start(bf16[128,2048]{0,1:T(8,128)(2,1)} %reduce_sum.301) | copy-start | bytes 1572868
  1021.3 7.3 copy-start.35
  1021.3 7.3 copy-start.49
  1030.7 41.3 %copy-start.10 = (f32[128,2048]{1,0:T(8,128)S(1)}, f32[128,2048]{1,0:T(8,128)}, u32[]{:S(2)}) copy-start(f32[128,2048]{1,0:T(8,128)} %copy-done.9) | copy-start | bytes 3145732
  1030.7 41.3 %copy-start.59 = (f32[128]{0:T(128)S(1)}, f32[128]{0:T(128)}, u32[]{:S(2)}) copy-start(f32[128]{0:T(128)} %get-tuple-element.48) | copy-start | bytes 1540
  1089.1 807.0 %copy-start.1 = (s32[4,128,2]{1,2,0:T(2,128)S(1)}, s32[4,128,2]{1,2,0:T(2,128)}, u32[]{:S(2)}) copy-start(s32[4,128,2]{1,2,0:T(2,128)} %param.20) | copy-start | bytes 12292
  (27 other events, 40.8 us)
Sparse Core Ops, SparseCore 0:
  10.5 57.0 all-gather.12
  70.1 54.3 all-gather.8
  127.0 54.3 all-gather.10
  183.7 54.3 all-gather.14
  316.6 56.9 all-gather.16
  375.4 58.8 all-gather.18
  471.6 76.4 reduce-scatter.12
  551.7 126.0 reduce-scatter.14
  729.0 144.1 reduce-scatter.26
  875.4 138.1 reduce-scatter.24
  1017.1 72.0 reduce-scatter.20
  1092.8 71.2 reduce-scatter.22
  1167.0 364.1 reduce-scatter.16
  1534.0 362.1 reduce-scatter.18
where the time goes:
time: 1910 us; the launch traced here: 1900 us
  waiting for transfers between devices  1250 us (65%)
  blocking collectives  256 us (13%)
  matrix products  252 us (13%)
  local copies, waits for them, and re-layouts  48.1 us (3%)
  other arithmetic  45.1 us (2%)
  starting transfers between devices  38 us (2%)
    reduce_scatter x1, waiting for transfers between devices, on_device(): lax.psum_scatter(value_part, ('dp', 'expert'), scatter_dimension=0, tiled...  365 us
    reduce_scatter x1, waiting for transfers between devices, on_device(): lax.psum_scatter(key_part, ('dp', 'expert'), scatter_dimension=0, tiled=T...  364 us
    reduce_scatter x1, waiting for transfers between devices, on_device(): lax.psum_scatter(grad_ffn_part, 'dp', scatter_dimension=0, tiled=True)  125 us
    reduce_scatter x1, waiting for transfers between devices, on_device(): lax.psum_scatter(output_grad[None].astype(jnp.bfloat16), 'dp', scatter_di...  72.2 us
    all_to_all x1, blocking collectives, on_device(): lax.all_to_all(keys_part.reshape(experts, seq_len, head_width).astype(jnp...  59.2 us
    all_to_all x1, blocking collectives, on_device(): lax.all_to_all(values_part.reshape(experts, seq_len, head_width).astype(j...  57.4 us
    reduce_scatter x1, waiting for transfers between devices, on_device(): lax.psum_scatter(partial_out.astype(jnp.bfloat16), 'dp', scatter_dimensio...  39.7 us
    unnamed x1, blocking collectives  39.1 us
  transfers between devices with their start and end apart: 22, of which 17 were waited for; matrix products, arithmetic and copies ran while one was open for 15% of the time, Pallas kernels for 0%

commit v1 on v0

v1 whole, which is shorter than its diff:
```python
from functools import partial

import jax
import jax.numpy as jnp
from jax import lax
from jax.experimental import pallas as pl
from jax.experimental.pallas import tpu as pltpu
from jax.sharding import PartitionSpec as P

HEADS = 16
HEAD = 128
MESH = pl.DeviceIdType.MESH
ANY = pl.BlockSpec(memory_space=pl.ANY)

eps = 1e-06
theta = 10000.0
highest = lax.Precision.HIGHEST
f32 = jnp.float32
bf16 = jnp.bfloat16


def rope_tables(positions, head_size):
    half_size = head_size // 2
    frequency = theta ** (-(jnp.arange(half_size, dtype=f32) * 2.0 / head_size))
    angles = positions.astype(f32)[:, None] * frequency[None, :]
    return (jnp.cos(angles), jnp.sin(angles))


def signed_tables(positions):
    cosine, sine = rope_tables(positions, HEAD)
    return (jnp.concatenate([cosine, cosine], 1), jnp.concatenate([-sine, sine], 1))


def turned_back(value, tables):
    half_size = HEAD // 2
    swapped = jnp.concatenate([value[:, half_size:], value[:, :half_size]], axis=1)
    return value * tables[0] - swapped * tables[1]


def norm_scale(value):
    return lax.rsqrt(jnp.mean(value * value, axis=-1, keepdims=True) + eps)


def norm_backward(grad_normed, value, scale_value, gain_value):
    scaled_grad = grad_normed * gain_value
    gain_part = jnp.sum(grad_normed * value * scale_value, axis=0)
    grad_value = scale_value * scaled_grad - value * scale_value**3 * jnp.mean(
        scaled_grad * value, axis=-1, keepdims=True
    )
    return (grad_value, gain_part)


def softmax_rows(values):
    peak = jnp.max(values, axis=-1, keepdims=True)
    powers = jnp.exp(values - peak)
    return powers / jnp.sum(powers, axis=-1, keepdims=True)


def router_gates(logits, choices, live_rows, experts):
    onehot = (choices[:, :, None] == jnp.arange(experts, dtype=jnp.int32)[None, None, :]).astype(
        f32
    )
    chosen = jnp.sum(logits[:, None, :] * onehot, axis=-1)
    shares = softmax_rows(chosen)
    dense = jnp.sum((shares * live_rows[:, None])[:, :, None] * onehot, axis=1)
    return (onehot, shares, dense)


def gates_backward(grad_dense, onehot, shares, live_rows):
    grad_shares = jnp.sum(grad_dense[:, None, :] * onehot, axis=-1) * live_rows[:, None]
    grad_chosen = shares * (grad_shares - jnp.sum(shares * grad_shares, axis=-1, keepdims=True))
    return jnp.sum(grad_chosen[:, :, None] * onehot, axis=1)


def route_table(choices, length_value, experts, capacity):
    places = jnp.arange(choices.shape[0], dtype=jnp.int32)
    living = (places < length_value).astype(jnp.int32)
    picked = (
        jnp.sum(
            (choices[:, :, None] == jnp.arange(experts, dtype=jnp.int32)[None, None, :]).astype(
                jnp.int32
            ),
            axis=1,
        )
        * living[:, None]
    )
    slot_of = jnp.cumsum(picked, axis=0) - 1
    slot_ids = jnp.arange(capacity, dtype=jnp.int32)
    return (slot_of.T[:, None, :] == slot_ids[None, :, None]) & (picked.T[:, None, :] == 1)


def flip(index, bit):
    return index + bit * (1 - 2 * ((index // bit) % 2))


def flips(index, mask, bits):
    for bit in bits:
        if mask & bit:
            index = flip(index, bit)
    return index


def span(bits):
    masks = [0]
    for bit in bits:
        masks = masks + [mask | bit for mask in masks]
    return masks


def bit_orders(size):
    bits = [1 << k for k in range(size.bit_length() - 1)]
    high = bits[1:]
    return (high + bits[:1], high[::-1] + bits[:1])


def barrier(targets):
    semaphore = pltpu.get_barrier_semaphore()
    for target in targets:
        pl.semaphore_signal(semaphore, inc=1, device_id=target, device_id_type=MESH)
    pl.semaphore_wait(semaphore, len(targets))


def gather_kernel(groups, experts, splits, axes, *refs):
    count = len(splits)
    shards, home = refs[:count], refs[count]
    fulls, home_all = refs[count + 1 : 2 * count + 1], refs[2 * count + 1]
    local_sem, send_sem, recv_sem, home_send, home_recv = refs[2 * count + 2 :]
    group = lax.axis_index("dp")
    mine = lax.axis_index("expert")
    orders = bit_orders(groups)
    bits = sorted(orders[0])
    others = [(mine + step) % experts for step in range(1, experts)]
    barrier([(flip(group, bit), mine) for bit in bits] + [(group, other) for other in others])

    home_copies = []
    for step, other in enumerate(others):
        copy = pltpu.make_async_remote_copy(
            src_ref=home,
            dst_ref=home_all.at[mine],
            send_sem=home_send.at[step],
            recv_sem=home_recv.at[step],
            device_id=(group, other),
            device_id_type=MESH,
        )
        copy.start()
        home_copies.append(copy)

    def part(ref, which, block, half):
        pieces, axis = splits[which], axes[which]
        extent = shards[which].shape[axis]
        size = extent // pieces
        start = half * size if block is None else block * extent + half * size
        if block is not None:
            start = pl.multiple_of(start, size)
        where = pl.ds(start, size)
        return ref.at[where] if axis == 0 else ref.at[:, where]

    stages = {}
    slot = 0
    for which in range(count):
        for half in range(splits[which]):
            order = orders[half]
            for stage, bit in enumerate(order):
                copies = []
                for mask in span(order[:stage]):
                    block = flips(group, mask, bits)
                    target = part(fulls[which], which, block, half)
                    source = part(shards[which], which, None, half) if mask == 0 else target
                    copies.append(
                        pltpu.make_async_remote_copy(
                            src_ref=source,
                            dst_ref=target,
                            send_sem=send_sem.at[slot],
                            recv_sem=recv_sem.at[slot],
                            device_id=(flip(group, bit), mine),
                            device_id_type=MESH,
                        )
                    )
                    slot += 1
                stages[which, half, stage] = copies
    keys = [(which, half) for which in range(count) for half in range(splits[which])]
    for which, half in keys:
        for copy in stages[which, half, 0]:
            copy.start()
    local = [pltpu.make_async_copy(home, home_all.at[mine], local_sem.at[count])]
    for which in range(count):
        extent = shards[which].shape[axes[which]]
        where = pl.ds(pl.multiple_of(group * extent, extent), extent)
        target = fulls[which].at[where] if axes[which] == 0 else fulls[which].at[:, where]
        local.append(pltpu.make_async_copy(shards[which], target, local_sem.at[which]))
    for copy in local:
        copy.start()
    for stage in range(len(bits)):
        for which, half in keys:
            for copy in stages[which, half, stage]:
                copy.wait_recv()
            if stage + 1 < len(bits):
                for copy in stages[which, half, stage + 1]:
                    copy.start()
    for copies in stages.values():
        for copy in copies:
            copy.wait_send()
    for copy in home_copies:
        copy.wait()
    for copy in local:
        copy.wait()


def gather_all(arrays, splits, axes, home):
    groups = lax.axis_size("dp")
    experts = lax.axis_size("expert")
    shapes = []
    for array, axis in zip(arrays, axes):
        shape = list(array.shape)
        shape[axis] *= groups
        shapes.append(jax.ShapeDtypeStruct(tuple(shape), array.dtype))
    shapes.append(jax.ShapeDtypeStruct((experts,) + home.shape, home.dtype))
    slots = sum(splits) * (groups - 1)
    return pl.pallas_call(
        partial(gather_kernel, groups, experts, splits, axes),
        out_shape=shapes,
        in_specs=[ANY] * (len(arrays) + 1),
        out_specs=[ANY] * (len(arrays) + 1),
        scratch_shapes=[
            pltpu.SemaphoreType.DMA((len(arrays) + 1,)),
            pltpu.SemaphoreType.DMA((slots,)),
            pltpu.SemaphoreType.DMA((slots,)),
            pltpu.SemaphoreType.DMA((experts - 1,)),
            pltpu.SemaphoreType.DMA((experts - 1,)),
        ],
        compiler_params=pltpu.CompilerParams(collective_id=0, has_side_effects=True),
        name="gather_all",
    )(*arrays, home)


def total_kernel(groups, experts, parts, total, held, send_sem, recv_sem):
    devices = groups * experts
    me = lax.axis_index("dp") * experts + lax.axis_index("expert")
    semaphore = pltpu.get_barrier_semaphore()

    def greet(step, carry):
        other = (me + step) % devices
        pl.semaphore_signal(
            semaphore,
            inc=1,
            device_id=(other // experts, other % experts),
            device_id_type=MESH,
        )
        return carry

    lax.fori_loop(1, devices, greet, 0)
    pl.semaphore_wait(semaphore, devices - 1)

    def copy_of(step):
        other = (me + step) % devices
        return pltpu.make_async_remote_copy(
            src_ref=parts.at[other],
            dst_ref=held.at[step],
            send_sem=send_sem.at[step],
            recv_sem=recv_sem.at[step],
            device_id=(other // experts, other % experts),
            device_id_type=MESH,
        )

    def send(step, carry):
        copy_of(step).start()
        return carry

    lax.fori_loop(1, devices, send, 0)
    held[0] = parts[me]

    def finish(step, carry):
        copy_of(step).wait()
        return carry

    lax.fori_loop(1, devices, finish, 0)
    total[...] = jnp.sum(held[...], axis=0)


def total_small(rows):
    groups = lax.axis_size("dp")
    experts = lax.axis_size("expert")
    devices = groups * experts
    kinds, width = rows.shape
    share = width // devices
    packed = rows.reshape(kinds, devices, share).transpose(1, 0, 2).reshape(devices, kinds * share)
    room = -(-kinds * share // 1024) * 1024
    packed = jnp.pad(packed, ((0, 0), (0, room - kinds * share))).reshape(
        devices, room // 128, 128
    )
    summed = pl.pallas_call(
        partial(total_kernel, groups, experts),
        out_shape=jax.ShapeDtypeStruct((room // 128, 128), f32),
        in_specs=[pl.BlockSpec(memory_space=pltpu.VMEM)],
        out_specs=pl.BlockSpec(memory_space=pltpu.VMEM),
        scratch_shapes=[
            pltpu.VMEM((devices, room // 128, 128), f32),
            pltpu.SemaphoreType.DMA((devices,)),
            pltpu.SemaphoreType.DMA((devices,)),
        ],
        compiler_params=pltpu.CompilerParams(collective_id=1, has_side_effects=True),
        name="total_small",
    )(packed)
    return summed.reshape(-1)[: kinds * share].reshape(kinds, share)


def turn(value, cosine, sine):
    return value * cosine + pltpu.roll(value, HEAD // 2, 1) * sine


def softmax_all(scores, seen):
    masked = jnp.where(seen, scores * (HEAD ** (-0.5)), -1e30)
    powers = jnp.exp(masked - jnp.max(masked, axis=-1, keepdims=True))
    return powers / jnp.sum(powers, axis=-1, keepdims=True)


def blocks_of(experts, rows, tokens, width):
    capacity, seq_len = rows // experts, tokens // experts
    return [
        (
            slice(seq * capacity, (seq + 1) * capacity),
            slice(seq * seq_len, (seq + 1) * seq_len),
            slice(head * HEAD, (head + 1) * HEAD),
        )
        for head in range(width // HEAD)
        for seq in range(experts)
    ]


def attend_kernel(
    experts,
    inputs_ref,
    small_ref,
    table_ref,
    place_ref,
    cos_far,
    sin_far,
    cos_near,
    sin_near,
    query_weight,
    key_weight,
    value_weight,
    normed_out,
    rows_out,
    query_out,
    key_out,
    value_out,
    mixture_out,
    query_hold,
):
    @pl.when(pl.program_id(0) == 0)
    def _():
        gain = small_ref[0:1].astype(f32)

        def norm_part(step, carry):
            at = pl.ds(pl.multiple_of(step * 32, 32), 32)
            value = inputs_ref[at].astype(f32)
            normed_out[at] = (value * norm_scale(value) * gain).astype(bf16)
            return carry

        lax.fori_loop(0, inputs_ref.shape[0] // 32, norm_part, 0)
        rows_out[...] = jnp.dot(
            table_ref[...], normed_out[...], preferred_element_type=f32
        ).astype(bf16)

    capacity = rows_out.shape[0] // experts
    seq_len = normed_out.shape[0] // experts
    width = key_out.shape[1]
    key = jnp.dot(normed_out[...], key_weight[...], preferred_element_type=f32)
    value_out[...] = jnp.dot(
        normed_out[...], value_weight[...], preferred_element_type=f32
    ).astype(bf16)
    query = jnp.dot(rows_out[...], query_weight[...], preferred_element_type=f32)
    for head in range(width // HEAD):
        cut = slice(head * HEAD, (head + 1) * HEAD)
        key_out[:, cut] = turn(key[:, cut], cos_near[...], sin_near[...]).astype(bf16)
        query_hold[:, cut] = turn(query[:, cut], cos_far[...], sin_far[...])
    query_out[...] = query_hold[...].astype(bf16)
    blocks = blocks_of(experts, rows_out.shape[0], normed_out.shape[0], width)
    contract = (((1,), (1,)), ((), ()))
    scores = jnp.concatenate(
        [
            lax.dot_general(
                query_hold[rows, cut].astype(bf16),
                key_out[keys, cut],
                contract,
                preferred_element_type=f32,
            )
            for rows, keys, cut in blocks
        ],
        axis=0,
    )
    spots = lax.broadcasted_iota(jnp.int32, (rows_out.shape[0], seq_len), 1)
    seen = spots <= place_ref[...]
    probs = softmax_all(scores, jnp.concatenate([seen] * (width // HEAD), axis=0))
    for number, (rows, keys, cut) in enumerate(blocks):
        query_hold[rows, cut] = jnp.dot(
            probs[number * capacity : (number + 1) * capacity].astype(bf16),
            value_out[keys, cut],
            preferred_element_type=f32,
        )
    mixture_out[...] = query_hold[...].astype(bf16)


def attend(experts, inputs, small, table, places, far, near, query_w, key_w, value_w):
    tokens, depth = inputs.shape
    rows = table.shape[0]
    heads_width = query_w.shape[1]
    tile = 256

    def full(shape):
        return pl.BlockSpec(shape, lambda step: (0, 0))

    def cut(height):
        return pl.BlockSpec((height, tile), lambda step: (0, step))

    def shaped(height, width):
        return jax.ShapeDtypeStruct((height, width), bf16)

    return pl.pallas_call(
        partial(attend_kernel, experts),
        grid=(heads_width // tile,),
        out_shape=[
            shaped(tokens, depth),
            shaped(rows, depth),
            shaped(rows, heads_width),
            shaped(tokens, heads_width),
            shaped(tokens, heads_width),
            shaped(rows, heads_width),
        ],
        in_specs=[
            full((tokens, depth)),
            full(small.shape),
            full(table.shape),
            full(places.shape),
            full((rows, HEAD)),
            full((rows, HEAD)),
            full((tokens, HEAD)),
            full((tokens, HEAD)),
            cut(depth),
            cut(depth),
            cut(depth),
        ],
        out_specs=[
            full((tokens, depth)),
            full((rows, depth)),
            cut(rows),
            cut(tokens),
            cut(tokens),
            cut(rows),
        ],
        scratch_shapes=[pltpu.VMEM((rows, tile), f32)],
        compiler_params=pltpu.CompilerParams(vmem_limit_bytes=48 * 1024 * 1024),
        cost_estimate=pl.CostEstimate(
            flops=2 * depth * heads_width * (2 * tokens + rows),
            bytes_accessed=6 * depth * heads_width + 8 * tokens * depth,
            transcendentals=rows * heads_width,
        ),
        name="attend",
    )(inputs, small, table, places, *far, *near, query_w, key_w, value_w)


def attend_back_kernel(
    experts,
    grad_ref,
    place_ref,
    cos_far,
    sin_far,
    weight_ref,
    query_ref,
    key_ref,
    value_ref,
    mixture_ref,
    query_out,
    key_out,
    value_out,
    output_out,
    grad_hold,
    query_hold,
    back_hold,
):
    contract = (((1,), (1,)), ((), ()))
    stack = (((0,), (0,)), ((), ()))
    rows_all = grad_ref.shape[0]
    capacity = rows_all // experts
    width = query_ref.shape[1]
    seq_len = key_ref.shape[0] // experts
    scale = HEAD ** (-0.5)
    grad_hold[...] = (
        lax.dot_general(grad_ref[...], weight_ref[...], contract, preferred_element_type=f32)
        .astype(bf16)
        .astype(f32)
    )
    output_out[...] = lax.dot_general(
        mixture_ref[...], grad_ref[...], stack, preferred_element_type=f32
    ).astype(bf16)
    query_hold[...] = query_ref[...].astype(f32)
    blocks = blocks_of(experts, rows_all, key_ref.shape[0], width)
    queries = [query_hold[rows, cut].astype(bf16) for rows, keys, cut in blocks]
    grads = [grad_hold[rows, cut].astype(bf16) for rows, keys, cut in blocks]
    scores = jnp.concatenate(
        [
            lax.dot_general(query, key_ref[keys, cut], contract, preferred_element_type=f32)
            for query, (rows, keys, cut) in zip(queries, blocks)
        ],
        axis=0,
    )
    grad_probs = jnp.concatenate(
        [
            lax.dot_general(grad, value_ref[keys, cut], contract, preferred_element_type=f32)
            for grad, (rows, keys, cut) in zip(grads, blocks)
        ],
        axis=0,
    )
    spots = lax.broadcasted_iota(jnp.int32, (rows_all, seq_len), 1)
    seen = spots <= place_ref[...]
    probs = softmax_all(scores, jnp.concatenate([seen] * (width // HEAD), axis=0))
    inner = jnp.sum(probs * grad_probs, axis=-1, keepdims=True)
    slopes = probs * (grad_probs - inner)
    for number, (rows, keys, cut) in enumerate(blocks):
        own = slice(number * capacity, (number + 1) * capacity)
        slope = slopes[own].astype(bf16)
        value_out[0, keys, cut] = lax.dot_general(
            probs[own].astype(bf16), grads[number], stack, preferred_element_type=f32
        ).astype(bf16)
        key_out[0, keys, cut] = (
            lax.dot_general(slope, queries[number], stack, preferred_element_type=f32) * scale
        ).astype(bf16)
        back_hold[rows, cut] = (
            jnp.dot(slope, key_ref[keys, cut], preferred_element_type=f32) * scale
        )
    for head in range(width // HEAD):
        cut = slice(head * HEAD, (head + 1) * HEAD)
        query_out[:, cut] = turn(back_hold[:, cut], cos_far[...], -sin_far[...]).astype(bf16)


def attend_back(experts, grad_rows, places, far, output_w, query, key, value, mixture):
    rows, depth = grad_rows.shape
    tokens, heads_width = key.shape
    tile = 256
    own_width = heads_width // experts
    steps = own_width // tile

    def full(shape):
        return pl.BlockSpec(shape, lambda step: (0, 0))

    def cut(height):
        return pl.BlockSpec((height, tile), lambda step: (0, step))

    by_heads = pl.BlockSpec((1, tokens, tile), lambda step: (step // steps, 0, step % steps))
    return pl.pallas_call(
        partial(attend_back_kernel, experts),
        grid=(heads_width // tile,),
        out_shape=[
            jax.ShapeDtypeStruct((rows, heads_width), bf16),
            jax.ShapeDtypeStruct((experts, tokens, own_width), bf16),
            jax.ShapeDtypeStruct((experts, tokens, own_width), bf16),
            jax.ShapeDtypeStruct((heads_width, depth), bf16),
        ],
        in_specs=[
            full((rows, depth)),
            full(places.shape),
            full((rows, HEAD)),
            full((rows, HEAD)),
            pl.BlockSpec((tile, depth), lambda step: (step, 0)),
            cut(rows),
            cut(tokens),
            cut(tokens),
            cut(rows),
        ],
        out_specs=[
            cut(rows),
            by_heads,
            by_heads,
            pl.BlockSpec((tile, depth), lambda step: (step, 0)),
        ],
        scratch_shapes=[pltpu.VMEM((rows, tile), f32)] * 3,
        compiler_params=pltpu.CompilerParams(vmem_limit_bytes=48 * 1024 * 1024),
        cost_estimate=pl.CostEstimate(
            flops=4 * rows * depth * heads_width,
            bytes_accessed=4 * depth * heads_width + 8 * tokens * heads_width,
            transcendentals=rows * heads_width,
        ),
        name="attend_back",
    )(grad_rows, places, *far, output_w, query, key, value, mixture)


def halves(ref, block, rows, half):
    size = rows // 2
    return ref.at[pl.ds(pl.multiple_of(block * rows + half * size, size), size)]


def whole(ref, block, rows):
    return ref.at[pl.ds(pl.multiple_of(block * rows, rows), rows)]


def ffn_kernel(
    rows,
    own_ref,
    slope_ref,
    pick_ref,
    router_ref,
    gate_ref,
    up_ref,
    down_ref,
    rows_out,
    hidden_out,
    grad_gate_out,
    grad_up_out,
    out_out,
    grad_out,
    held,
    pulled,
    hidden,
    scaled,
    grad_gate,
    grad_up,
    made,
    grads,
    near,
    far,
    dense,
    dense_far,
    dense_hold,
    far_send,
    far_recv,
    near_send,
    near_recv,
    sum_send,
    sum_recv,
    dense_send,
    dense_recv,
    load_sem,
    save_sem,
):
    group = lax.axis_index("dp")
    mine = lax.axis_index("expert")
    depth = held.shape[1]
    width = hidden.shape[1]
    pair = 2 * rows
    bits = (1, 2, 4)
    peers = {mask: (flips(group, mask, bits), mine) for mask in range(1, 8)}
    barrier([peers[mask] for mask in range(1, 8)])

    def remote(source, target, send, recv, mask):
        return pltpu.make_async_remote_copy(
            src_ref=source,
            dst_ref=target,
            send_sem=send,
            recv_sem=recv,
            device_id=peers[mask],
            device_id_type=MESH,
        )

    def own_half(half):
        size = rows // 2
        return own_ref.at[pl.ds(half * size, size)]

    sends = {}
    for slot, (mask, half) in enumerate(((2, 0), (4, 1), (2, 1), (4, 0))):
        sends[mask, half] = remote(
            own_half(half),
            halves(held, mask, rows, half),
            far_send.at[slot],
            far_recv.at[slot],
            mask,
        )
    sends[6, 0] = remote(
        halves(held, 2, rows, 0), halves(held, 6, rows, 0), far_send.at[4], far_recv.at[4], 4
    )
    sends[6, 1] = remote(
        halves(held, 4, rows, 1), halves(held, 6, rows, 1), far_send.at[5], far_recv.at[5], 2
    )
    across = {}
    for chip in range(4):
        across[chip] = remote(
            own_ref if chip == 0 else whole(held, 2 * chip, rows),
            whole(held, 2 * chip + 1, rows),
            near_send.at[chip],
            near_recv.at[chip],
            1,
        )
    sends[2, 0].start()
    sends[4, 1].start()
    across[0].start()
    sends[2, 1].start()
    sends[4, 0].start()
    seat = pltpu.make_async_copy(own_ref, whole(held, 0, rows), load_sem.at[2])
    seat.start()

    def pull(chip, slot, which):
        block = group_of(2 * chip + which)
        return pltpu.make_async_copy(
            slope_ref.at[block], whole(pulled, 2 * slot + which, rows), load_sem.at[which]
        )

    def group_of(index):
        result = group
        for bit in bits:
            on = (index // bit) % 2
            turned = bit * (1 - 2 * ((group // bit) % 2))
            result = result + on * turned
        return result

    def saves(chip):
        copies = []
        for which in range(2):
            block = group_of(2 * chip + which)
            for number, (source, target) in enumerate(
                (
                    (whole(held, 2 * chip + which, rows), rows_out.at[block]),
                    (whole(scaled, which, rows), hidden_out.at[block]),
                    (whole(grad_gate, which, rows), grad_gate_out.at[block]),
                    (whole(grad_up, which, rows), grad_up_out.at[block]),
                    (whole(made, which, rows), out_out.at[block]),
                )
            ):
                copies.append(
                    pltpu.make_async_copy(source, target, save_sem.at[5 * which + number])
                )
        return copies

    def across_sum(chip):
        return remote(
            whole(grads, 2 * chip + 1, rows),
            whole(near, chip, rows),
            near_send.at[4 + chip],
            near_recv.at[4 + chip],
            1,
        )

    hops = {}
    for slot, (key, block, half, mask) in enumerate(
        (
            ("x2", 2, 0, 2),
            ("x6", 6, 0, 2),
            ("y4", 4, 1, 4),
            ("y6", 6, 1, 4),
            ("then_y", 4, 0, 4),
            ("then_x", 2, 1, 2),
        )
    ):
        size = rows // 2
        hops[key] = remote(
            halves(grads, block, rows, half),
            far.at[pl.ds(slot * size, size)],
            sum_send.at[slot],
            sum_recv.at[slot],
            mask,
        )
    far_slots = {"x2": 0, "x6": 1, "y4": 2, "y6": 3, "then_y": 4, "then_x": 5}

    def dense_hop(mask):
        return remote(
            dense.at[mask],
            dense_far.at[mask],
            dense_send.at[mask],
            dense_recv.at[mask],
            mask,
        )

    def join(chip):
        across_sum(chip).wait_recv()
        block = 2 * chip

        def add(step, carry):
            at = pl.ds(pl.multiple_of(block * rows + step * 48, 16), 48)
            other = pl.ds(pl.multiple_of(chip * rows + step * 48, 16), 48)
            grads[at] = (grads[at].astype(f32) + near[other].astype(f32)).astype(bf16)
            return carry

        lax.fori_loop(0, rows // 48, add, 0)

    def add_far(block, half, key):
        size = rows // 2
        hops[key].wait_recv()

        def add(step, carry):
            at = pl.ds(pl.multiple_of(block * rows + half * size + step * 48, 16), 48)
            other = pl.ds(far_slots[key] * size + pl.multiple_of(step * 48, 16), 48)
            grads[at] = (grads[at].astype(f32) + far[other].astype(f32)).astype(bf16)
            return carry

        lax.fori_loop(0, size // 48, add, 0)

    for which in range(2):
        pull(0, 0, which).start()
    seat.wait()

    def step(chip, carry):
        @pl.when(chip == 0)
        def _():
            across[0].wait_recv()

        @pl.when(chip == 1)
        def _():
            sends[2, 0].wait_recv()
            sends[6, 0].start()
            sends[4, 1].wait_recv()
            sends[6, 1].start()
            sends[2, 1].wait_recv()
            across[1].start()
            sends[4, 0].wait_recv()
            across[2].start()
            across[1].wait_recv()

        @pl.when(chip == 2)
        def _():
            sends[6, 0].wait_recv()
            sends[6, 1].wait_recv()
            across[3].start()
            across[2].wait_recv()

        @pl.when(chip == 3)
        def _():
            across[3].wait_recv()

        slot = chip % 2
        for which in range(2):
            pull(chip, slot, which).wait()

        @pl.when(chip < 3)
        def _():
            for which in range(2):
                pull(chip + 1, 1 - slot, which).start()

        @pl.when(chip > 0)
        def _():
            for copy in saves(chip - 1):
                copy.wait()

        base = pl.multiple_of(chip * pair, pair)
        at = pl.ds(base, pair)
        logits = lax.dot_general(
            held[at], router_ref[...], (((1,), (1,)), ((), ())), preferred_element_type=f32
        )
        apart = []
        for which in range(2):
            block = group_of(2 * chip + which)
            picks = pick_ref[pl.ds(pl.multiple_of(block * rows, rows), rows)]
            apart.append(
                jnp.sum(
                    logits[which * rows : (which + 1) * rows] * picks, axis=-1, keepdims=True
                )
            )
        weight = 1.0 / (1.0 + jnp.exp(jnp.concatenate(apart, axis=0)))
        loads = pl.ds(pl.multiple_of(slot * pair, pair), pair)
        tile = 256
        partial_dense = jnp.zeros((pair, 128), f32)

        def units(number, total):
            cut = pl.ds(pl.multiple_of(number * tile, tile), tile)
            contract = (((1,), (1,)), ((), ()))
            gate = lax.dot_general(
                held[at], gate_ref[cut], contract, preferred_element_type=f32
            )
            up = lax.dot_general(held[at], up_ref[cut], contract, preferred_element_type=f32)
            sigmoid = 1.0 / (1.0 + jnp.exp(-gate))
            active = gate * sigmoid
            value = (active * up).astype(bf16)
            wide = value.astype(f32)
            plain = pulled[loads, cut]
            hidden[:, cut] = value
            scaled[:, cut] = (weight * wide).astype(bf16)
            inner = weight * plain
            grad_gate[:, cut] = (inner * up * (sigmoid * (1.0 + gate * (1.0 - sigmoid)))).astype(
                bf16
            )
            grad_up[:, cut] = (inner * active).astype(bf16)
            both = wide * plain
            return total + both[:, :128] + both[:, 128:]

        partial_dense = lax.fori_loop(0, width // tile, units, partial_dense)
        ones = jnp.ones((8, 128), f32)
        for which in range(2):
            dense[2 * chip + which] = lax.dot_general(
                ones,
                partial_dense[which * rows : (which + 1) * rows],
                (((1,), (1,)), ((), ())),
                precision=highest,
                preferred_element_type=f32,
            )

        @pl.when(chip == 1)
        def _():
            join(0)

        @pl.when(chip == 2)
        def _():
            join(1)
            hops["x2"].start()

        @pl.when(chip == 3)
        def _():
            join(2)
            hops["y4"].start()

        def columns(number, carry):
            cut = pl.ds(pl.multiple_of(number * tile, tile), tile)
            made[:, cut] = jnp.dot(
                hidden[...], down_ref[:, cut], preferred_element_type=f32
            ).astype(bf16)
            grads[at, cut] = (
                jnp.dot(grad_gate[...], gate_ref[:, cut], preferred_element_type=f32)
                + jnp.dot(grad_up[...], up_ref[:, cut], preferred_element_type=f32)
            ).astype(bf16)
            return carry

        lax.fori_loop(0, depth // tile, columns, 0)
        across_sum(chip).start()
        for copy in saves(chip):
            copy.start()
        return carry

    lax.fori_loop(0, 4, step, 0)
    join(3)
    hops["x6"].start()
    hops["y6"].start()
    for mask in range(1, 8):
        dense_hop(mask).start()
    add_far(0, 0, "x2")
    add_far(0, 1, "y4")
    add_far(4, 0, "x6")
    hops["then_y"].start()
    add_far(2, 1, "y6")
    hops["then_x"].start()
    total = dense[0]
    for mask in range(1, 8):
        dense_hop(mask).wait_recv()
        total = total + dense_far[mask]
    for copy in saves(3):
        copy.wait()
    pick = (lax.broadcasted_iota(jnp.int32, (8, 128), 0) == 0).astype(f32)
    column = lax.dot_general(
        total, pick, (((0,), (0,)), ((), ())), precision=highest, preferred_element_type=f32
    )
    upper = column.astype(bf16)
    lower = (column - upper.astype(f32)).astype(bf16)
    lane = lax.broadcasted_iota(jnp.int32, column.shape, 1)
    dense_hold[...] = jnp.where(lane == 0, upper, jnp.where(lane == 1, lower, 0.0)).astype(bf16)
    add_far(0, 0, "then_y")
    add_far(0, 1, "then_x")
    tail = pltpu.make_async_copy(dense_hold, grad_out.at[:, pl.ds(depth, 128)], load_sem.at[0])
    tail.start()
    last = pltpu.make_async_copy(
        whole(grads, 0, rows), grad_out.at[:, pl.ds(0, depth)], load_sem.at[2]
    )
    last.start()
    for copy in list(sends.values()) + list(across.values()) + list(hops.values()):
        copy.wait_send()
    for chip in range(4):
        across_sum(chip).wait_send()
    for mask in range(1, 8):
        dense_hop(mask).wait_send()
    last.wait()
    tail.wait()


def ffn_call(own, slopes, picks, router, gate, up, down):
    rows, depth = own.shape
    width = gate.shape[0]
    vmem = pl.BlockSpec(memory_space=pltpu.VMEM)
    return pl.pallas_call(
        partial(ffn_kernel, rows),
        out_shape=[
            jax.ShapeDtypeStruct((8, rows, depth), bf16),
            jax.ShapeDtypeStruct((8, rows, width), bf16),
            jax.ShapeDtypeStruct((8, rows, width), bf16),
            jax.ShapeDtypeStruct((8, rows, width), bf16),
            jax.ShapeDtypeStruct((8, rows, depth), bf16),
            jax.ShapeDtypeStruct((rows, depth + 128), bf16),
        ],
        in_specs=[ANY, ANY, vmem, vmem, vmem, vmem, vmem],
        out_specs=[ANY] * 6,
        scratch_shapes=[
            pltpu.VMEM((8 * rows, depth), bf16),
            pltpu.VMEM((4 * rows, width), f32),
            pltpu.VMEM((2 * rows, width), bf16),
            pltpu.VMEM((2 * rows, width), bf16),
            pltpu.VMEM((2 * rows, width), bf16),
            pltpu.VMEM((2 * rows, width), bf16),
            pltpu.VMEM((2 * rows, depth), bf16),
            pltpu.VMEM((8 * rows, depth), bf16),
            pltpu.VMEM((4 * rows, depth), bf16),
            pltpu.VMEM((3 * rows, depth), bf16),
            pltpu.VMEM((8, 8, rows), f32),
            pltpu.VMEM((8, 8, rows), f32),
            pltpu.VMEM((rows, 128), bf16),
            pltpu.SemaphoreType.DMA((6,)),
            pltpu.SemaphoreType.DMA((6,)),
            pltpu.SemaphoreType.DMA((8,)),
            pltpu.SemaphoreType.DMA((8,)),
            pltpu.SemaphoreType.DMA((6,)),
            pltpu.SemaphoreType.DMA((6,)),
            pltpu.SemaphoreType.DMA((8,)),
            pltpu.SemaphoreType.DMA((8,)),
            pltpu.SemaphoreType.DMA((3,)),
            pltpu.SemaphoreType.DMA((10,)),
        ],
        compiler_params=pltpu.CompilerParams(
            collective_id=2, has_side_effects=True, vmem_limit_bytes=61 * 1024 * 1024
        ),
        name="ffn",
    )(own, slopes, picks, router, gate, up, down)


class ChipSums:
    def __init__(self, remote, blocks, near, far, sems, rows):
        self.blocks, self.near, self.far, self.rows = blocks, near, far, rows
        self.remote = remote
        self.near_send, self.near_recv, self.sum_send, self.sum_recv = sems
        self.hops = {}
        size = rows // 2
        for slot, (key, block, half, mask) in enumerate(
            (
                ("x2", 2, 0, 2),
                ("x6", 6, 0, 2),
                ("y4", 4, 1, 4),
                ("y6", 6, 1, 4),
                ("then_y", 4, 0, 4),
                ("then_x", 2, 1, 2),
            )
        ):
            self.hops[key] = (
                remote(
                    halves(blocks, block, rows, half),
                    far.at[pl.ds(slot * size, size)],
                    self.sum_send.at[slot],
                    self.sum_recv.at[slot],
                    mask,
                ),
                slot * size,
            )

    def across(self, chip):
        return self.remote(
            whole(self.blocks, 2 * chip + 1, self.rows),
            whole(self.near, chip, self.rows),
            self.near_send.at[chip],
            self.near_recv.at[chip],
            1,
        )

    def add(self, start, other, other_start, count):
        piece = 48 if count % 48 == 0 else 32

        def one(step, carry):
            at = pl.ds(pl.multiple_of(start + step * piece, 16), piece)
            have = pl.ds(pl.multiple_of(other_start + step * piece, 16), piece)
            self.blocks[at] = (self.blocks[at].astype(f32) + other[have].astype(f32)).astype(bf16)
            return carry

        lax.fori_loop(0, count // piece, one, 0)

    def join(self, chip):
        self.across(chip).wait_recv()
        self.add(2 * chip * self.rows, self.near, chip * self.rows, self.rows)

    def begin(self, key):
        self.hops[key][0].start()

    def settle(self, chip):
        self.join(chip)

        @pl.when(chip == 1)
        def _():
            self.begin("x2")

        @pl.when(chip == 2)
        def _():
            self.begin("y4")

        @pl.when(chip == 3)
        def _():
            self.begin("x6")
            self.begin("y6")

    def add_far(self, block, half, key):
        size = self.rows // 2
        copy, place = self.hops[key]
        copy.wait_recv()
        self.add(block * self.rows + half * size, self.far, place, size)

    def cross(self):
        self.add_far(4, 0, "x6")
        self.begin("then_y")
        self.add_far(2, 1, "y6")
        self.begin("then_x")
        self.add_far(0, 0, "x2")
        self.add_far(0, 1, "y4")

    def close(self):
        self.add_far(0, 0, "then_y")
        self.add_far(0, 1, "then_x")

    def drain(self):
        for copy, place in self.hops.values():
            copy.wait_send()
        for chip in range(4):
            self.across(chip).wait_send()


def turned_pair(index, other, bits):
    result = index
    for bit in bits:
        on = (other // bit) % 2
        result = result + on * bit * (1 - 2 * ((index // bit) % 2))
    return result


def back_kernel(
    grad_ref,
    rows_ref,
    place_ref,
    cos_far,
    sin_far,
    cos_near,
    sin_near,
    weight_ref,
    query_ref,
    key_ref,
    value_ref,
    mixture_ref,
    query_out,
    key_out,
    value_out,
    output_sum,
    query_sum,
    grad_hold,
    query_hold,
    back_hold,
    weights,
    key_part,
    value_part,
    key_got,
    value_got,
    key_pass,
    value_pass,
    total_hold,
    output_blocks,
    output_near,
    output_far,
    query_blocks,
    query_near,
    query_far,
    output_near_send,
    output_near_recv,
    output_sum_send,
    output_sum_recv,
    query_near_send,
    query_near_recv,
    query_sum_send,
    query_sum_recv,
    got_send,
    got_recv,
    pass_send,
    pass_recv,
    load_sem,
):
    group = lax.axis_index("dp")
    mine = lax.axis_index("expert")
    experts = 4
    side = mine // 2
    edge = ((mine + 1) % experts) // 2 == 0
    bits = (1, 2, 4)
    peers = {mask: (flips(group, mask, bits), mine) for mask in (1, 2, 4)}
    barrier(
        [peers[mask] for mask in (1, 2, 4)]
        + [(group, (mine + step) % experts) for step in range(1, experts)]
    )

    def remote(source, target, send, recv, mask):
        return pltpu.make_async_remote_copy(
            src_ref=source,
            dst_ref=target,
            send_sem=send,
            recv_sem=recv,
            device_id=peers[mask],
            device_id_type=MESH,
        )

    rows_all, depth = grad_ref.shape
    tokens = key_ref.shape[0]
    capacity = rows_all // experts
    seq_len = tokens // experts
    tile = 256
    contract = (((1,), (1,)), ((), ()))
    stack = (((0,), (0,)), ((), ()))
    scale = HEAD ** (-0.5)
    outputs = ChipSums(
        remote,
        output_blocks,
        output_near,
        output_far,
        (output_near_send, output_near_recv, output_sum_send, output_sum_recv),
        tile,
    )
    queries_sum = ChipSums(
        remote,
        query_blocks,
        query_near,
        query_far,
        (query_near_send, query_near_recv, query_sum_send, query_sum_recv),
        tile,
    )

    def owner_of(number):
        return jnp.where(
            number == 0,
            2 - side,
            jnp.where(number == 1, 3 - 3 * side, jnp.where(number == 2, 1 + 4 * side - mine, mine)),
        )

    def chip_of(owner):
        return turned_pair(owner, group // 2, (1, 2))

    def load(step):
        at = pl.multiple_of((2 * owner_of(step // 2) + step % 2) * tile, tile)
        return pltpu.make_async_copy(
            weight_ref.at[pl.ds(at, tile)], weights.at[step % 2], load_sem.at[step % 2]
        )

    def part_at(owner):
        return pl.ds(pl.multiple_of(owner * tokens, tokens), tokens)

    def give(owner):
        return [
            pltpu.make_async_remote_copy(
                src_ref=part.at[part_at(owner)],
                dst_ref=got.at[part_at(mine)],
                send_sem=got_send.at[owner, number],
                recv_sem=got_recv.at[mine, number],
                device_id=(group, owner),
                device_id_type=MESH,
            )
            for number, (part, got) in enumerate(
                ((key_part, key_got), (value_part, value_got))
            )
        ]

    def got_from(source):
        return [
            pltpu.make_async_remote_copy(
                src_ref=part.at[part_at(source)],
                dst_ref=got.at[part_at(source)],
                send_sem=got_send.at[source, number],
                recv_sem=got_recv.at[source, number],
                device_id=(group, source),
                device_id_type=MESH,
            )
            for number, (part, got) in enumerate(
                ((key_part, key_got), (value_part, value_got))
            )
        ]

    def hand_on(target):
        return [
            pltpu.make_async_remote_copy(
                src_ref=part.at[part_at(2 - side)],
                dst_ref=pile,
                send_sem=pass_send.at[number],
                recv_sem=pass_recv.at[number],
                device_id=(group, target),
                device_id_type=MESH,
            )
            for number, (part, pile) in enumerate(
                ((key_part, key_pass), (value_part, value_pass))
            )
        ]

    load(0).start()
    block_slices = blocks_of(experts, rows_all, tokens, tile)
    spots = lax.broadcasted_iota(jnp.int32, (rows_all, seq_len), 1)

    def one(step, carry):
        owner = owner_of(step // 2)
        parity = step % 2
        number = 2 * owner + parity
        chip = chip_of(owner)
        load(step).wait()

        @pl.when(step < 7)
        def _():
            load(step + 1).start()

        columns = pl.ds(pl.multiple_of(number * tile, tile), tile)
        block = turned_pair(number, group, bits)
        block_at = pl.ds(pl.multiple_of(block * tile, tile), tile)
        grad_hold[...] = (
            lax.dot_general(
                grad_ref[...], weights[parity], contract, preferred_element_type=f32
            )
            .astype(bf16)
            .astype(f32)
        )
        output_blocks[block_at] = lax.dot_general(
            mixture_ref[:, columns], grad_ref[...], stack, preferred_element_type=f32
        ).astype(bf16)

        @pl.when((parity == 1) & (step > 1))
        def _():
            outputs.settle(chip_of(owner_of(step // 2 - 1)))

        query_hold[...] = query_ref[:, columns].astype(f32)
        keys_tile = key_ref[:, columns]
        values_tile = value_ref[:, columns]
        queries = [query_hold[rows, cut].astype(bf16) for rows, keys, cut in block_slices]
        grads = [grad_hold[rows, cut].astype(bf16) for rows, keys, cut in block_slices]
        scores = jnp.concatenate(
            [
                lax.dot_general(query, keys_tile[keys, cut], contract, preferred_element_type=f32)
                for query, (rows, keys, cut) in zip(queries, block_slices)
            ],
            axis=0,
        )
        grad_probs = jnp.concatenate(
            [
                lax.dot_general(grad, values_tile[keys, cut], contract, preferred_element_type=f32)
                for grad, (rows, keys, cut) in zip(grads, block_slices)
            ],
            axis=0,
        )
        seen = spots <= place_ref[...]
        probs = softmax_all(scores, jnp.concatenate([seen] * (tile // HEAD), axis=0))
        inner = jnp.sum(probs * grad_probs, axis=-1, keepdims=True)
        slopes = probs * (grad_probs - inner)
        for count, (rows, keys, cut) in enumerate(block_slices):
            own = slice(count * capacity, (count + 1) * capacity)
            slope = slopes[own].astype(bf16)
            token_at = pl.ds(
                pl.multiple_of(owner * tokens + keys.start, seq_len), seq_len
            )
            lanes = pl.ds(pl.multiple_of(parity * tile + cut.start, HEAD), HEAD)
            value_part[token_at, lanes] = lax.dot_general(
                probs[own].astype(bf16), grads[count], stack, preferred_element_type=f32
            ).astype(bf16)
            key_part[token_at, lanes] = (
                lax.dot_general(slope, queries[count], stack, preferred_element_type=f32) * scale
            ).astype(bf16)
            back_hold[rows, cut] = (
                jnp.dot(slope, keys_tile[keys, cut], preferred_element_type=f32) * scale
            )
        for head in range(tile // HEAD):
            cut = slice(head * HEAD, (head + 1) * HEAD)
            lanes = pl.ds(pl.multiple_of(number * tile + head * HEAD, HEAD), HEAD)
            query_out[:, lanes] = turn(back_hold[:, cut], cos_far[...], -sin_far[...]).astype(bf16)

        @pl.when(parity == 1)
        def _():
            outputs.across(chip).start()

            @pl.when(step == 1)
            def _():
                @pl.when(edge)
                def _():
                    for copy in hand_on(1 + side):
                        copy.start()

            @pl.when((step == 3) | (step == 5))
            def _():
                for copy in give(owner):
                    copy.start()

        return carry

    lax.fori_loop(0, 8, one, 0)

    def project(block, carry):
        number = turned_pair(block, group, bits)
        columns = pl.ds(pl.multiple_of(number * tile, tile), tile)
        block_at = pl.ds(pl.multiple_of(block * tile, tile), tile)
        query_blocks[block_at] = lax.dot_general(
            rows_ref[:, columns], query_out[...], stack, preferred_element_type=f32
        ).astype(bf16)

        @pl.when(block % 2 == 1)
        def _():
            queries_sum.across(block // 2).start()

        return carry

    lax.fori_loop(0, 8, project, 0)
    outputs.settle(chip_of(mine))
    piece = 32

    @pl.when(jnp.logical_not(edge))
    def _():
        for (part, pile), copy in zip(
            ((key_part, key_pass), (value_part, value_pass)), hand_on(1 + side)
        ):
            copy.wait_recv()

            def add(step, carry):
                at = pl.ds(pl.multiple_of((2 - side) * tokens + step * piece, piece), piece)
                other = pl.ds(pl.multiple_of(step * piece, piece), piece)
                part[at] = (part[at].astype(f32) + pile[other].astype(f32)).astype(bf16)
                return carry

            lax.fori_loop(0, tokens // piece, add, 0)
        for copy in give(2 - side):
            copy.start()

    for chip in range(4):
        queries_sum.settle(chip)
    outputs.cross()
    outputs.close()
    result = pltpu.make_async_copy(whole(output_blocks, 0, tile), output_sum, load_sem.at[0])
    result.start()
    queries_sum.cross()
    queries_sum.close()
    second = pltpu.make_async_copy(whole(query_blocks, 0, tile), query_sum, load_sem.at[1])
    second.start()

    def expected(source):
        far_end = (mine + 2) % experts
        middle = ((mine + 1) % experts) // 2 == 1
        return jnp.logical_not(middle & (source == far_end))

    def gather(number, part, got):
        def first(step, carry):
            at = pl.ds(pl.multiple_of(mine * tokens + step * piece, piece), piece)
            where = pl.ds(pl.multiple_of(step * piece, piece), piece)
            total_hold[where] = part[at].astype(f32)
            return carry

        lax.fori_loop(0, tokens // piece, first, 0)
        for hop in range(1, experts):
            source = (mine + hop) % experts

            @pl.when(expected(source))
            def _():
                got_from(source)[number].wait_recv()

                def add(step, carry):
                    at = pl.ds(pl.multiple_of(source * tokens + step * piece, piece), piece)
                    where = pl.ds(pl.multiple_of(step * piece, piece), piece)
                    total_hold[where] = total_hold[where] + got[at].astype(f32)
                    return carry

                lax.fori_loop(0, tokens // piece, add, 0)

    gather(1, value_part, value_got)
    value_out[...] = total_hold[...].astype(bf16)
    gather(0, key_part, key_got)
    for head in range(key_out.shape[1] // HEAD):
        cut = slice(head * HEAD, (head + 1) * HEAD)
        key_out[:, cut] = turn(total_hold[:, cut], cos_near[...], -sin_near[...]).astype(bf16)

    @pl.when(edge)
    def _():
        for copy in hand_on(1 + side):
            copy.wait_send()

    @pl.when(jnp.logical_not(edge))
    def _():
        for copy in give(2 - side):
            copy.wait_send()

    for number in (1, 2):
        for copy in give(owner_of(number)):
            copy.wait_send()
    outputs.drain()
    queries_sum.drain()
    result.wait()
    second.wait()


def back_call(grad_rows, rows_flat, places, far, near, output_w, query, key, value, mixture):
    rows, depth = grad_rows.shape
    tokens, heads_width = key.shape
    own = heads_width // 4
    tile = 256
    vmem = pl.BlockSpec(memory_space=pltpu.VMEM)

    def dma(*shape):
        return pltpu.SemaphoreType.DMA(shape)

    def blocks(count):
        return pltpu.VMEM((count * tile, depth), bf16)

    return pl.pallas_call(
        back_kernel,
        out_shape=[
            jax.ShapeDtypeStruct((rows, heads_width), bf16),
            jax.ShapeDtypeStruct((tokens, own), bf16),
            jax.ShapeDtypeStruct((tokens, own), bf16),
            jax.ShapeDtypeStruct((tile, depth), bf16),
            jax.ShapeDtypeStruct((tile, depth), bf16),
        ],
        in_specs=[vmem] * 7 + [ANY] + [vmem] * 4,
        out_specs=[vmem] * 3 + [ANY] * 2,
        scratch_shapes=[
            pltpu.VMEM((rows, tile), f32),
            pltpu.VMEM((rows, tile), f32),
            pltpu.VMEM((rows, tile), f32),
            pltpu.VMEM((2, tile, depth), bf16),
            pltpu.VMEM((4 * tokens, own), bf16),
            pltpu.VMEM((4 * tokens, own), bf16),
            pltpu.VMEM((4 * tokens, own), bf16),
            pltpu.VMEM((4 * tokens, own), bf16),
            pltpu.VMEM((tokens, own), bf16),
            pltpu.VMEM((tokens, own), bf16),
            pltpu.VMEM((tokens, own), f32),
            blocks(8),
            blocks(4),
            blocks(3),
            blocks(8),
            blocks(4),
            blocks(3),
            dma(4),
            dma(4),
            dma(6),
            dma(6),
            dma(4),
            dma(4),
            dma(6),
            dma(6),
            dma(4, 2),
            dma(4, 2),
            dma(2),
            dma(2),
            dma(2),
        ],
        compiler_params=pltpu.CompilerParams(
            collective_id=3, has_side_effects=True, vmem_limit_bytes=61 * 1024 * 1024
        ),
        cost_estimate=pl.CostEstimate(
            flops=60_000_000_000, bytes_accessed=200_000_000, transcendentals=0
        ),
        name="attend_back_sums",
    )(grad_rows, rows_flat, places, *far, *near, output_w, query, key, value, mixture)


def start_kernel(
    home,
    attn_gain,
    moe_gain,
    attn_router,
    moe_router,
    attn_choice,
    moe_choice,
    lengths,
    cos_home,
    sin_home,
    given,
    value_shard,
    key_shard,
    query_shard,
    output_shard,
    small_full,
    told_full,
    table_out,
    place_out,
    cos_far,
    sin_far,
    attn_table,
    moe_table,
    normed_out,
    rows_out,
    query_out,
    key_out,
    value_out,
    mixture_out,
    branch_out,
    value_own,
    key_own,
    query_full,
    output_full,
    given_out,
    inputs,
    small_own,
    told_own,
    small_hold,
    normed,
    rows_hold,
    query_hold,
    query_low,
    keys,
    values,
    chances,
    mixture,
    branch,
    given_hold,
    value_stage,
    key_stage,
    query_stage,
    output_stage,
    value_buf,
    key_buf,
    query_buf,
    output_buf,
    load_sem,
    far_send,
    far_recv,
    near_send,
    near_recv,
    home_send,
    home_recv,
    small_send,
    small_recv,
    told_send,
    told_recv,
    heads_send,
    heads_recv,
    given_send,
    given_recv,
    save_sem,
):
    group = lax.axis_index("dp")
    mine = lax.axis_index("expert")
    experts = 4
    bits = (1, 2, 4)
    peers = {mask: (flips(group, mask, bits), mine) for mask in range(1, 8)}
    others = [(mine + hop) % experts for hop in range(1, experts)]
    seq_len, depth = home.shape
    expert_rows = rows_out.shape[0]
    capacity = expert_rows // experts
    tokens = experts * seq_len
    extent = key_shard.shape[0]
    half_extent = extent // 2
    own_width = value_buf.shape[1]
    heads_width = key_buf.shape[1]
    tile = 256
    shards = (value_shard, key_shard, query_shard, output_shard)
    stages = (value_stage, key_stage, query_stage, output_stage)
    buffers = (value_buf, key_buf, query_buf, output_buf)
    loads = []
    for which in range(4):
        source = shards[which]
        if which == 0:
            source = source.at[:, pl.ds(pl.multiple_of(mine * own_width, own_width), own_width)]
        loads.append(pltpu.make_async_copy(source, stages[which], load_sem.at[which]))
    seat = pltpu.make_async_copy(home, inputs.at[mine], load_sem.at[4])
    for copy in loads:
        copy.start()
    seat.start()

    small_hold[...] = jnp.zeros_like(small_hold)
    small_hold[0:1] = attn_gain[...]
    small_hold[1:2] = moe_gain[...]
    small_hold[2 : 2 + experts] = attn_router[...]
    small_hold[2 + experts : 2 + 2 * experts] = moe_router[...]
    small_own[...] = small_hold[...].astype(bf16)
    lane = lax.broadcasted_iota(jnp.int32, (experts, seq_len), 1)
    live = lane < lengths[...]
    told_own[0:experts] = jnp.where(live, moe_choice[0], -1).astype(f32)
    told_own[experts : 2 * experts] = jnp.where(live, moe_choice[1], -1).astype(f32)
    barrier([peers[mask] for mask in range(1, 8)] + [(group, other) for other in others])

    def remote(source, target, send, recv, device):
        return pltpu.make_async_remote_copy(
            src_ref=source,
            dst_ref=target,
            send_sem=send,
            recv_sem=recv,
            device_id=device,
            device_id_type=MESH,
        )

    small_at = pl.ds(pl.multiple_of(group * extent, extent), extent)
    told_at = pl.ds(pl.multiple_of(group * 2 * experts, 2 * experts), 2 * experts)
    smalls = []
    for mask in range(1, 8):
        smalls.append(
            remote(
                small_own,
                small_full.at[:, small_at],
                small_send.at[mask],
                small_recv.at[mask],
                peers[mask],
            )
        )
        smalls.append(
            remote(
                told_own,
                told_full.at[told_at],
                told_send.at[mask],
                told_recv.at[mask],
                peers[mask],
            )
        )
    homes = [
        remote(home, inputs.at[mine], home_send.at[hop], home_recv.at[hop], (group, other))
        for hop, other in enumerate(others)
    ]
    for copy in smalls + homes:
        copy.start()
    small_full[:, small_at] = small_own[...]
    told_full[told_at] = told_own[...]

    def piece(which, mask, half):
        start = flips(group, mask, bits) * extent + half * half_extent
        return buffers[which].at[pl.ds(pl.multiple_of(start, half_extent), half_extent)]

    def block(which, mask):
        start = flips(group, mask, bits) * extent
        return buffers[which].at[pl.ds(pl.multiple_of(start, extent), extent)]

    far = {}
    near = {}
    for which in range(4):
        for slot, (mask, half, towards) in enumerate(
            ((0, 0, 2), (0, 1, 2), (0, 1, 4), (0, 0, 4), (2, 0, 4), (4, 1, 2))
        ):
            far[which, slot] = remote(
                piece(which, mask, half),
                piece(which, mask, half),
                far_send.at[which, slot],
                far_recv.at[which, slot],
                peers[towards],
            )
        for chip in range(4):
            near[which, chip] = remote(
                block(which, 2 * chip),
                block(which, 2 * chip),
                near_send.at[which, chip],
                near_recv.at[which, chip],
                peers[1],
            )

    def convert(which):
        loads[which].wait()
        count = 32

        def one(step, carry):
            at = pl.ds(pl.multiple_of(step * count, count), count)
            to = pl.ds(pl.multiple_of(group * extent + step * count, count), count)
            buffers[which][to] = stages[which][at].astype(bf16)
            return carry

        lax.fori_loop(0, extent // count, one, 0)

    def leave(which):
        for slot in (0, 2, 1, 3):
            far[which, slot].start()
        near[which, 0].start()

    def pass_on(which):
        far[which, 0].wait_recv()
        far[which, 4].start()
        far[which, 2].wait_recv()
        far[which, 5].start()

    def spread(which):
        far[which, 1].wait_recv()
        near[which, 1].start()
        far[which, 3].wait_recv()
        near[which, 2].start()
        far[which, 4].wait_recv()
        far[which, 5].wait_recv()
        near[which, 3].start()

    def complete(which):
        for chip in range(4):
            near[which, chip].wait_recv()

    convert(0)
    leave(0)
    convert(1)
    leave(1)

    chosen = ((attn_choice[0] == mine) | (attn_choice[1] == mine)) & live
    picked = chosen.astype(f32)
    early = lax.broadcasted_iota(jnp.int32, (seq_len, seq_len), 0)
    late = lax.broadcasted_iota(jnp.int32, (seq_len, seq_len), 1)
    until = (early <= late).astype(f32)
    seats = lax.broadcasted_iota(jnp.int32, (capacity, seq_len), 0).astype(f32) + 1.0
    spot = lax.broadcasted_iota(jnp.int32, (capacity, seq_len), 1).astype(f32)

    def seated(taken):
        slot_of = jnp.dot(taken, until, preferred_element_type=f32)
        return [
            ((slot_of[row : row + 1] == seats) & (taken[row : row + 1] > 0.0)).astype(f32)
            for row in range(experts)
        ]

    tables = seated(picked)
    row_of = lax.broadcasted_iota(jnp.int32, (experts, seq_len), 0)

    def own_row(value):
        return jnp.sum(jnp.where(row_of == mine, value, 0), axis=0, keepdims=True)

    own_live = lane < own_row(jnp.broadcast_to(lengths[...], (experts, seq_len)))
    for choice, table_ref in ((attn_choice, attn_table), (moe_choice, moe_table)):
        goes = ((own_row(choice[0]) == row_of) | (own_row(choice[1]) == row_of)) & own_live
        table_ref[...] = jnp.concatenate(seated(goes.astype(f32)), axis=0).astype(bf16)
    for other in range(experts):
        given_hold[other] = jnp.dot(
            moe_table[other * capacity : (other + 1) * capacity],
            given[...],
            preferred_element_type=f32,
        ).astype(bf16)
    empty = jnp.zeros((capacity, seq_len), f32)
    table_out[...] = jnp.concatenate(
        [
            jnp.concatenate(
                [tables[seq] if seq == other else empty for other in range(experts)], axis=1
            )
            for seq in range(experts)
        ],
        axis=0,
    ).astype(bf16)
    place_out[...] = jnp.concatenate(
        [jnp.sum(table * spot, axis=1, keepdims=True) for table in tables], axis=0
    ).astype(jnp.int32)
    stacked = jnp.concatenate(tables, axis=0)
    vacant = 1.0 - jnp.sum(stacked, axis=1, keepdims=True)
    cos_far[...] = vacant + jnp.dot(
        stacked, cos_home[...], precision=highest, preferred_element_type=f32
    )
    sin_far[...] = jnp.dot(stacked, sin_home[...], precision=highest, preferred_element_type=f32)

    pass_on(0)
    convert(2)
    pass_on(1)
    leave(2)
    convert(3)
    spread(0)
    complete(0)
    spread(1)

    seat.wait()
    for copy in smalls:
        copy.wait_recv()
    gain = small_full[0:1].astype(f32)
    for hop in range(experts):
        source = (mine + experts - hop) % experts
        if hop > 0:
            homes[hop - 1].wait_recv()
        count = 32

        def one(step, carry):
            at = pl.ds(pl.multiple_of(step * count, count), count)
            to = pl.ds(pl.multiple_of(source * seq_len + step * count, count), count)
            value = inputs[source, at].astype(f32)
            normed[to] = (value * norm_scale(value) * gain).astype(bf16)
            return carry

        lax.fori_loop(0, seq_len // count, one, 0)
    own_at = pl.ds(pl.multiple_of(mine * own_width, own_width), own_width)
    values[:, own_at] = jnp.dot(
        normed[...], value_buf[...], preferred_element_type=f32
    ).astype(bf16)
    heads = [
        remote(
            values.at[:, own_at],
            values.at[:, own_at],
            heads_send.at[hop],
            heads_recv.at[hop],
            (group, other),
        )
        for hop, other in enumerate(others)
    ]
    for copy in heads:
        copy.start()
    rows_hold[...] = jnp.dot(table_out[...], normed[...], preferred_element_type=f32).astype(bf16)
    saves = [
        pltpu.make_async_copy(normed, normed_out, save_sem.at[0]),
        pltpu.make_async_copy(rows_hold, rows_out, save_sem.at[1]),
        pltpu.make_async_copy(value_buf, value_own, save_sem.at[2]),
    ]
    for copy in saves:
        copy.start()

    def save(source, target, number):
        copy = pltpu.make_async_copy(source, target, save_sem.at[number])
        copy.start()
        saves.append(copy)

    complete(1)
    save(key_buf.at[:, own_at], key_own, 3)

    def make_keys(step, carry):
        cut = pl.ds(pl.multiple_of(step * tile, tile), tile)
        made = jnp.dot(normed[...], key_buf[:, cut], preferred_element_type=f32)
        for head in range(tile // HEAD):
            lanes = pl.ds(pl.multiple_of(step * tile + head * HEAD, HEAD), HEAD)
            part = made[:, head * HEAD : (head + 1) * HEAD]
            for seq in range(experts):
                rows = slice(seq * seq_len, (seq + 1) * seq_len)
                keys[rows, lanes] = turn(part[rows], cos_home[...], sin_home[...]).astype(bf16)
        return carry

    lax.fori_loop(0, heads_width // tile, make_keys, 0)
    save(keys, key_out, 4)
    pass_on(2)
    leave(3)
    spread(2)
    complete(2)
    save(query_buf, query_full, 5)

    blocks = blocks_of(experts, expert_rows, tokens, tile)
    contract = (((1,), (1,)), ((), ()))
    spots = lax.broadcasted_iota(jnp.int32, (expert_rows, seq_len), 1)
    span_rows = len(blocks) * capacity

    def make_chances(step, carry):
        cut = pl.ds(pl.multiple_of(step * tile, tile), tile)
        made = jnp.dot(rows_hold[...], query_buf[:, cut], preferred_element_type=f32)
        for head in range(tile // HEAD):
            part = slice(head * HEAD, (head + 1) * HEAD)
            query_hold[:, part] = turn(made[:, part], cos_far[...], sin_far[...])
        query_low[:, cut] = query_hold[...].astype(bf16)
        tile_keys = keys[:, cut]
        scores = jnp.concatenate(
            [
                lax.dot_general(
                    query_hold[rows, lanes].astype(bf16),
                    tile_keys[spans, lanes],
                    contract,
                    preferred_element_type=f32,
                )
                for rows, spans, lanes in blocks
            ],
            axis=0,
        )
        seen = spots <= place_out[...]
        probs = softmax_all(scores, jnp.concatenate([seen] * (tile // HEAD), axis=0))
        chances[pl.ds(pl.multiple_of(step * span_rows, 64), span_rows)] = probs.astype(bf16)
        return carry

    lax.fori_loop(0, heads_width // tile, make_chances, 0)
    save(query_low, query_out, 6)
    pass_on(3)
    for copy in heads:
        copy.wait_recv()
    givens = [
        remote(
            given_hold.at[other],
            given_out.at[mine],
            given_send.at[hop],
            given_recv.at[hop],
            (group, other),
        )
        for hop, other in enumerate(others)
    ]
    for copy in givens:
        copy.start()
    save(given_hold.at[mine], given_out.at[mine], 11)
    save(values, value_out, 7)

    def mix(step, carry):
        cut = pl.ds(pl.multiple_of(step * tile, tile), tile)
        tile_values = values[:, cut]
        probs = chances[pl.ds(pl.multiple_of(step * span_rows, 64), span_rows)].astype(f32)
        for count, (rows, spans, lanes) in enumerate(blocks):
            query_hold[rows, lanes] = jnp.dot(
                probs[count * capacity : (count + 1) * capacity].astype(bf16),
                tile_values[spans, lanes],
                preferred_element_type=f32,
            )
        mixture[:, cut] = query_hold[...].astype(bf16)
        return carry

    lax.fori_loop(0, heads_width // tile, mix, 0)
    save(mixture, mixture_out, 8)
    spread(3)
    complete(3)
    save(output_buf, output_full, 9)

    def project(step, carry):
        cut = pl.ds(pl.multiple_of(step * tile, tile), tile)
        branch[:, cut] = jnp.dot(
            mixture[...], output_buf[:, cut], preferred_element_type=f32
        ).astype(bf16)
        return carry

    lax.fori_loop(0, depth // tile, project, 0)
    save(branch, branch_out, 10)
    for copy in givens:
        copy.wait_recv()
    for copy in smalls + homes + heads + givens + list(far.values()) + list(near.values()):
        copy.wait_send()
    for copy in saves:
        copy.wait()


def start_call(
    home,
    attn_gain,
    moe_gain,
    attn_router,
    moe_router,
    attn_choice,
    moe_choice,
    lengths,
    near,
    given,
    value_weight,
    key_weight,
    query_weight,
    output_weight,
):
    experts = 4
    groups = 8
    seq_len, depth = home.shape
    extent, heads_width = key_weight.shape
    capacity = 2 * seq_len // experts + 8
    rows = experts * capacity
    tokens = experts * seq_len
    own_width = heads_width // experts
    small_room = -(-(2 + 2 * experts) // 16) * 16
    vmem = pl.BlockSpec(memory_space=pltpu.VMEM)

    def shaped(*shape, kind=bf16):
        return jax.ShapeDtypeStruct(shape, kind)

    def dma(*shape):
        return pltpu.SemaphoreType.DMA(shape)

    return pl.pallas_call(
        start_kernel,
        out_shape=[
            shaped(small_room, depth),
            shaped(groups * 2 * experts, seq_len, kind=f32),
            shaped(rows, tokens),
            shaped(rows, 1, kind=jnp.int32),
            shaped(rows, HEAD, kind=f32),
            shaped(rows, HEAD, kind=f32),
            shaped(rows, seq_len),
            shaped(rows, seq_len),
            shaped(tokens, depth),
            shaped(rows, depth),
            shaped(rows, heads_width),
            shaped(tokens, heads_width),
            shaped(tokens, heads_width),
            shaped(rows, heads_width),
            shaped(rows, depth),
            shaped(depth, own_width),
            shaped(depth, own_width),
            shaped(depth, heads_width),
            shaped(heads_width, depth),
            shaped(experts, capacity, depth),
        ],
        in_specs=[ANY] + [vmem] * 10 + [ANY] * 4,
        out_specs=[vmem] * 8 + [ANY] * 12,
        scratch_shapes=[
            pltpu.VMEM((experts, seq_len, depth), bf16),
            pltpu.VMEM((small_room, extent), bf16),
            pltpu.VMEM((2 * experts, seq_len), f32),
            pltpu.VMEM((small_room, extent), f32),
            pltpu.VMEM((tokens, depth), bf16),
            pltpu.VMEM((rows, depth), bf16),
            pltpu.VMEM((rows, 256), f32),
            pltpu.VMEM((rows, heads_width), bf16),
            pltpu.VMEM((tokens, heads_width), bf16),
            pltpu.VMEM((tokens, heads_width), bf16),
            pltpu.VMEM((rows * heads_width // HEAD, seq_len), bf16),
            pltpu.VMEM((rows, heads_width), bf16),
            pltpu.VMEM((rows, depth), bf16),
            pltpu.VMEM((experts, capacity, depth), bf16),
            pltpu.VMEM((extent, own_width), f32),
            pltpu.VMEM((extent, heads_width), f32),
            pltpu.VMEM((extent, heads_width), f32),
            pltpu.VMEM((extent, depth), f32),
            pltpu.VMEM((depth, own_width), bf16),
            pltpu.VMEM((depth, heads_width), bf16),
            pltpu.VMEM((depth, heads_width), bf16),
            pltpu.VMEM((heads_width, depth), bf16),
            dma(5),
            dma(4, 6),
            dma(4, 6),
            dma(4, 4),
            dma(4, 4),
            dma(3),
            dma(3),
            dma(8),
            dma(8),
            dma(8),
            dma(8),
            dma(3),
            dma(3),
            dma(3),
            dma(3),
            dma(12),
        ],
        compiler_params=pltpu.CompilerParams(
            collective_id=4, has_side_effects=True, vmem_limit_bytes=61 * 1024 * 1024
        ),
        cost_estimate=pl.CostEstimate(
            flops=100_000_000_000, bytes_accessed=300_000_000, transcendentals=0
        ),
        name="attend_start",
    )(
        home,
        attn_gain,
        moe_gain,
        attn_router,
        moe_router,
        attn_choice,
        moe_choice,
        lengths,
        *near,
        given,
        value_weight,
        key_weight,
        query_weight,
        output_weight,
    )


def start_plain(
    home,
    attn_gain,
    moe_gain,
    attn_router,
    moe_router,
    attn_choice,
    moe_choice,
    lengths,
    near,
    given,
    value_weight,
    key_weight,
    query_weight,
    output_weight,
):
    experts = lax.axis_size("expert")
    mine = lax.axis_index("expert")
    seq_len, depth = home.shape
    heads_width = key_weight.shape[1]
    own_width = heads_width // experts
    capacity = 2 * seq_len // experts + 8
    rows = experts * capacity
    kinds = 2 + 2 * experts
    small_own = jnp.concatenate(
        [
            attn_gain,
            moe_gain,
            attn_router,
            moe_router,
            jnp.zeros((-kinds % 16, attn_gain.shape[1]), f32),
        ]
    ).astype(bf16)
    places = jnp.arange(seq_len, dtype=jnp.int32)
    live = places[None] < lengths
    told = jnp.where(live, moe_choice, -1).astype(f32).reshape(2 * experts, seq_len)
    key_full, value_full, query_full, output_full, small_full, told_full, inputs = gather_all(
        [
            key_weight.astype(bf16),
            value_weight.astype(bf16),
            query_weight.astype(bf16),
            output_weight.astype(bf16),
            small_own,
            told,
        ],
        (2, 2, 2, 2, 1, 1),
        (0, 0, 0, 0, 1, 0),
        home,
    )

    def tables_of(choice):
        return jax.vmap(partial(route_table, experts=experts, capacity=capacity))(
            choice.transpose(1, 2, 0), lengths[:, 0]
        )

    attn_all, moe_all = tables_of(attn_choice), tables_of(moe_choice)
    group_table = lax.dynamic_index_in_dim(attn_all, mine, 1, keepdims=False)
    own_attn = lax.dynamic_index_in_dim(attn_all, mine, 0, keepdims=False).astype(bf16)
    own_moe = lax.dynamic_index_in_dim(moe_all, mine, 0, keepdims=False).astype(bf16)
    row_places = jnp.sum(jnp.where(group_table, places, 0), axis=-1).reshape(rows, 1)
    same = jnp.eye(experts, dtype=bool)[:, None, :, None]
    table = (group_table[:, :, None, :] & same).astype(bf16).reshape(rows, experts * seq_len)
    far = signed_tables(row_places[:, 0])
    all_near = tuple(jnp.tile(part, (experts, 1)) for part in near)
    normed, rows_flat, queries, keys, values, mixture = attend(
        experts,
        inputs.reshape(experts * seq_len, depth),
        small_full,
        table,
        row_places,
        far,
        all_near,
        query_full,
        key_full,
        value_full,
    )
    branch = jnp.dot(mixture, output_full, preferred_element_type=f32).astype(bf16)
    given_rows = jnp.einsum("ect,td->ecd", own_moe, given, preferred_element_type=f32)

    def own_heads(weight):
        return lax.dynamic_slice_in_dim(weight, mine * own_width, own_width, 1)

    return (
        small_full,
        told_full,
        table,
        row_places,
        *far,
        own_attn.reshape(rows, seq_len),
        own_moe.reshape(rows, seq_len),
        normed,
        rows_flat,
        queries,
        keys,
        values,
        mixture,
        branch,
        own_heads(value_full),
        own_heads(key_full),
        query_full,
        output_full,
        exchange(given_rows.astype(bf16)),
    )


def ffn_plain(own, slopes, picks, router, gate, up, down):
    groups, rows, width = slopes.shape
    depth = own.shape[1]
    held = lax.all_gather(own, "dp", axis=0, tiled=True)
    logits = jnp.einsum("rd,ed->re", held, router, preferred_element_type=f32)
    weight = 1.0 / (1.0 + jnp.exp(jnp.sum(logits * picks, axis=-1, keepdims=True)))
    plain = slopes.reshape(groups * rows, width)
    gate_pre = jnp.einsum("rd,fd->rf", held, gate, preferred_element_type=f32)
    up_pre = jnp.einsum("rd,fd->rf", held, up, preferred_element_type=f32)
    sigmoid = 1.0 / (1.0 + jnp.exp(-gate_pre))
    active = gate_pre * sigmoid
    hidden = (active * up_pre).astype(bf16)
    wide = hidden.astype(f32)
    inner = weight * plain
    grad_gate = (inner * up_pre * (sigmoid * (1.0 + gate_pre * (1.0 - sigmoid)))).astype(bf16)
    grad_up = (inner * active).astype(bf16)
    made = jnp.dot(hidden, down, preferred_element_type=f32).astype(bf16)
    grads = (
        jnp.dot(grad_gate, gate, preferred_element_type=f32)
        + jnp.dot(grad_up, up, preferred_element_type=f32)
    ).astype(bf16)
    grads = lax.psum_scatter(
        grads.reshape(groups, rows, depth), "dp", scatter_dimension=0, tiled=True
    )[0]
    dense = lax.psum_scatter(
        jnp.sum(wide * plain, axis=-1).reshape(groups, rows),
        "dp",
        scatter_dimension=0,
        tiled=True,
    )

    def split(value):
        return value.reshape(groups, rows, value.shape[-1])

    upper = dense[0][:, None].astype(bf16)
    lower = (dense[0][:, None] - upper.astype(f32)).astype(bf16)
    grads = jnp.concatenate([grads, upper, lower, jnp.zeros((rows, 126), bf16)], axis=1)
    scaled = (weight * wide).astype(bf16)
    return (
        split(held),
        split(scaled),
        split(grad_gate),
        split(grad_up),
        split(made),
        grads,
    )


def back_plain(grad_rows, rows_flat, places, far, near, output_w, query, key, value, mixture):
    experts = lax.axis_size("expert")
    grad_query, keys_part, values_part, output_part = attend_back(
        experts, grad_rows, places, far, output_w, query, key, value, mixture
    )
    output_sum = lax.psum_scatter(output_part, "dp", scatter_dimension=0, tiled=True)
    grad_values = jnp.sum(exchange(values_part).astype(f32), axis=0).astype(bf16)
    grad_keys = jnp.sum(exchange(keys_part).astype(f32), axis=0)
    grad_keys = jnp.concatenate(
        [
            turned_back(grad_keys[:, start : start + HEAD], near)
            for start in range(0, grad_keys.shape[1], HEAD)
        ],
        axis=1,
    ).astype(bf16)
    query_part = jnp.einsum("rd,re->de", rows_flat, grad_query, preferred_element_type=f32)
    query_sum = lax.psum_scatter(
        query_part.astype(bf16), "dp", scatter_dimension=0, tiled=True
    )
    return grad_query, grad_keys, grad_values, output_sum, query_sum


def exchange(value):
    return lax.all_to_all(value, "expert", split_axis=0, concat_axis=0, tiled=True)


def on_device(
    hidden_in,
    out_grad,
    seq_lengths,
    attn_choice,
    moe_choice,
    attn_gain,
    moe_gain,
    attn_router,
    moe_router,
    key_weight,
    value_weight,
    query_weight,
    output_weight,
    gate_weight,
    up_weight,
    down_weight,
):
    experts = lax.axis_size("expert")
    groups = lax.axis_size("dp")
    mine_index = lax.axis_index("expert")
    seq_len = hidden_in.shape[1]
    model_width = hidden_in.shape[2]
    head_width = query_weight.shape[2]
    own_width = head_width // experts
    capacity = 2 * seq_len // experts + 8
    expert_rows = experts * capacity
    total_rows = groups * expert_rows
    score_scale = HEAD ** (-0.5)
    places = jnp.arange(seq_len, dtype=jnp.int32)
    own_length = lax.dynamic_index_in_dim(seq_lengths, mine_index, 0, keepdims=False)
    live_rows = (places < own_length).astype(f32)
    own_attn = lax.dynamic_index_in_dim(attn_choice, mine_index, 0, keepdims=False)
    own_moe = lax.dynamic_index_in_dim(moe_choice, mine_index, 0, keepdims=False)
    kinds = 2 + 2 * experts
    ready = groups == 8 and experts == 4
    near_home = signed_tables(places)
    (
        small_full,
        told_full,
        spread_table,
        row_places,
        cos_far,
        sin_far,
        table_attn,
        table_moe,
        normed_group,
        rows_flat,
        queries,
        keys_all,
        values_all,
        mixture,
        attn_rows,
        value_own,
        key_own,
        query_full,
        output_full,
        given_rows,
    ) = (start_call if ready else start_plain)(
        hidden_in[0],
        attn_gain[None],
        moe_gain[None],
        attn_router.T,
        moe_router.T,
        attn_choice.transpose(2, 0, 1),
        moe_choice.transpose(2, 0, 1),
        seq_lengths[:, None],
        near_home,
        out_grad[0],
        value_weight,
        key_weight,
        query_weight[0],
        output_weight[0],
    )
    far = (cos_far, sin_far)
    near = tuple(jnp.tile(part, (experts, 1)) for part in near_home)
    table_attn = table_attn.reshape(experts, capacity, seq_len)
    table_moe = table_moe.reshape(experts, capacity, seq_len)
    given_all = lax.all_gather(
        given_rows.reshape(expert_rows, model_width), "dp", axis=0, tiled=True
    )
    attn_rows = attn_rows.reshape(experts, capacity, model_width)

    gain_attn = small_full[0].astype(f32)
    gain_moe = small_full[1].astype(f32)
    router_attn = small_full[2 : 2 + experts]
    router_moe = small_full[2 + experts : kinds]
    inputs_f = hidden_in[0].astype(f32)
    scale_one = norm_scale(inputs_f)
    normed_one = (inputs_f * scale_one * gain_attn).astype(bf16)
    attn_logits = jnp.einsum("td,ed->te", normed_one, router_attn, preferred_element_type=f32)
    onehot_attn, shares_attn, dense_attn = router_gates(attn_logits, own_attn, live_rows, experts)

    told = told_full.reshape(groups, 2, experts, seq_len).transpose(1, 0, 2, 3)
    told = told.reshape(2, groups * experts, seq_len).astype(jnp.int32)
    comes = (told[0] == mine_index) | (told[1] == mine_index)
    order = jnp.cumsum(comes.astype(jnp.int32), axis=1) - 1
    slots = jnp.arange(capacity, dtype=jnp.int32)[None, :, None]
    rivals = jnp.sum(
        jnp.where(
            (order[:, None, :] == slots) & comes[:, None, :],
            (told[0] + told[1] - mine_index)[:, None, :],
            0,
        ),
        axis=-1,
    ).reshape(total_rows, 1)
    back_attn = exchange(attn_rows)
    spread_attn = jnp.einsum("ect,ecd->etd", table_attn, back_attn, preferred_element_type=f32)
    attn_sum = jnp.sum(dense_attn.T[:, :, None] * spread_attn, axis=0)
    middle = inputs_f + attn_sum
    scale_two = norm_scale(middle)
    normed_two = (middle * scale_two * gain_moe).astype(bf16)
    moe_logits = jnp.einsum("td,ed->te", normed_two, router_moe, preferred_element_type=f32)
    onehot_moe, shares_moe, dense_moe = router_gates(moe_logits, own_moe, live_rows, experts)
    send_moe = jnp.einsum(
        "ect,td->ecd", table_moe, normed_two, preferred_element_type=f32
    ).astype(bf16)
    rows_moe = exchange(send_moe).reshape(expert_rows, model_width)

    units = gate_weight.shape[2]
    room = -(-units // 256) * 256
    gate_slice = jnp.pad(gate_weight[0].T.astype(bf16), ((0, room - units), (0, 0)))
    up_slice = jnp.pad(up_weight[0].T.astype(bf16), ((0, room - units), (0, 0)))
    down_slice = jnp.pad(down_weight[0].astype(bf16), ((0, room - units), (0, 0)))
    slopes = jnp.einsum("rd,fd->rf", given_all, down_slice, preferred_element_type=f32)
    expert_ids = jnp.arange(16, dtype=jnp.int32)[None, :]
    picks = (expert_ids == rivals).astype(f32) - (
        expert_ids == mine_index
    ).astype(f32)
    router_rows = jnp.pad(router_moe, ((0, 16 - experts), (0, 0)))
    feed = ffn_call if groups == 8 and expert_rows % 96 == 0 else ffn_plain
    ffn_rows, scaled, grad_gate, grad_up, partial_out, grad_ffn = feed(
        rows_moe,
        slopes.reshape(groups, expert_rows, room),
        picks,
        router_rows,
        gate_slice,
        up_slice,
        down_slice,
    )
    back_moe_grad = exchange(grad_ffn.reshape(experts, capacity, model_width + 128))
    summed_out = lax.psum_scatter(partial_out, "dp", scatter_dimension=0, tiled=True)
    ffn_rows = ffn_rows.reshape(total_rows, model_width)
    down_grad = jnp.einsum(
        "rf,rd->fd",
        scaled.reshape(total_rows, room)[:, :units],
        given_all,
        preferred_element_type=f32,
    )[None]
    gate_grad = jnp.einsum(
        "rd,rf->df",
        ffn_rows,
        grad_gate.reshape(total_rows, room)[:, :units],
        preferred_element_type=f32,
    )[None]
    up_grad = jnp.einsum(
        "rd,rf->df",
        ffn_rows,
        grad_up.reshape(total_rows, room)[:, :units],
        preferred_element_type=f32,
    )[None]
    back_moe_grad, down_grad, gate_grad = lax.optimization_barrier(
        (back_moe_grad, down_grad, gate_grad)
    )
    back_dense = jnp.sum(back_moe_grad[:, :, model_width:].astype(f32), axis=-1)
    back_moe_grad = back_moe_grad[:, :, :model_width]

    grad_out = out_grad[0].astype(f32) * live_rows[:, None]
    grad_dense_moe = jnp.sum(table_moe.astype(f32) * back_dense[:, :, None], axis=1).T
    grad_normed_two = jnp.einsum(
        "ect,ecd->td", table_moe, back_moe_grad, preferred_element_type=f32
    )
    grad_logits_moe = gates_backward(grad_dense_moe, onehot_moe, shares_moe, live_rows)
    grad_normed_two = grad_normed_two + jnp.dot(
        grad_logits_moe, router_moe.astype(f32), precision=highest
    )
    moe_router_part = jnp.dot(grad_logits_moe.T, normed_two.astype(f32), precision=highest)
    grad_middle_norm, moe_gain_part = norm_backward(grad_normed_two, middle, scale_two, gain_moe)
    grad_middle = grad_out + grad_middle_norm
    grad_dense_attn = jnp.sum(grad_middle[None] * spread_attn, axis=-1).T
    rows_attn_grad = (dense_attn.T[:, :, None] * grad_middle[None]).astype(bf16)
    send_attn_grad = jnp.einsum(
        "ect,etd->ecd", table_attn, rows_attn_grad, preferred_element_type=f32
    ).astype(bf16)
    recv_attn_grad = exchange(send_attn_grad)
    recv_attn_grad, up_grad, summed_out = lax.optimization_barrier(
        (recv_attn_grad, up_grad, summed_out)
    )

    back_moe = exchange(summed_out[0].reshape(experts, capacity, model_width))
    backward = back_call if ready else back_plain
    grad_query_pre, grad_key_pre, grad_values, output_out, query_out = backward(
        recv_attn_grad.reshape(expert_rows, model_width),
        rows_flat,
        row_places,
        far,
        near,
        output_full,
        queries,
        keys_all,
        values_all,
        mixture,
    )
    grad_query_pre, back_moe = lax.optimization_barrier((grad_query_pre, back_moe))
    grad_rows_attn = jnp.einsum(
        "re,de->rd", grad_query_pre, query_full, preferred_element_type=f32
    ).astype(bf16)
    grad_normed_part = (
        jnp.einsum("rt,rd->td", spread_table, grad_rows_attn, preferred_element_type=f32)
        + jnp.einsum("te,de->td", grad_key_pre, key_own, preferred_element_type=f32)
        + jnp.einsum("te,de->td", grad_values, value_own, preferred_element_type=f32)
    ).astype(bf16)
    grad_normed_part, grad_key_pre, grad_values = lax.optimization_barrier(
        (grad_normed_part, grad_key_pre, grad_values)
    )
    normed_got = exchange(grad_normed_part.reshape(experts, seq_len, model_width))
    both_part = jnp.einsum(
        "td,te->de",
        normed_group,
        jnp.concatenate([grad_key_pre, grad_values], axis=1),
        preferred_element_type=f32,
    ).astype(bf16)
    both_own = lax.psum_scatter(both_part, "dp", scatter_dimension=0, tiled=True)
    normed_got, both_part = lax.optimization_barrier((normed_got, both_part))
    grad_normed_one = jnp.sum(normed_got.astype(f32), axis=0)
    both_own = exchange(both_own.reshape(experts, -1, 2 * own_width))
    both_own = both_own.reshape(experts, -1, 2, own_width).transpose(2, 1, 0, 3).astype(f32)
    key_grad = both_own[0].reshape(-1, head_width)
    value_grad = both_own[1].reshape(-1, head_width)

    spread_moe = jnp.einsum("ect,ecd->etd", table_moe, back_moe, preferred_element_type=f32)
    moe_sum = jnp.sum(dense_moe.T[:, :, None] * spread_moe, axis=0)
    block_out = (live_rows[:, None] * (middle + moe_sum)).astype(bf16)[None]
    grad_logits_attn = gates_backward(grad_dense_attn, onehot_attn, shares_attn, live_rows)
    attn_router_part = jnp.dot(grad_logits_attn.T, normed_one.astype(f32), precision=highest)
    grad_normed_one = grad_normed_one + jnp.dot(
        grad_logits_attn, router_attn.astype(f32), precision=highest
    )
    grad_inputs_norm, attn_gain_part = norm_backward(
        grad_normed_one, inputs_f, scale_one, gain_attn
    )
    input_grad = (grad_middle + grad_inputs_norm).astype(bf16)[None]
    smalls = total_small(
        jnp.concatenate(
            [attn_gain_part[None], moe_gain_part[None], attn_router_part, moe_router_part]
        )
    )
    return (
        block_out,
        input_grad,
        smalls[0],
        smalls[1],
        smalls[2 : 2 + experts].T,
        smalls[2 + experts : kinds].T,
        key_grad,
        value_grad,
        query_out.astype(f32)[None],
        output_out.astype(f32)[None],
        gate_grad,
        up_grad,
        down_grad,
    )


def solution(mesh):
    placed = (
        P(("dp", "expert"), None, None),
        P(("dp", "expert"), None, None),
        P("dp"),
        P("dp", None, None),
        P("dp", None, None),
        P("dp"),
        P("dp"),
        P("dp", None),
        P("dp", None),
        P("dp", None),
        P("dp", None),
        P("expert", "dp", None),
        P("expert", "dp", None),
        P("expert", None, "dp"),
        P("expert", None, "dp"),
        P("expert", "dp", None),
    )
    return jax.shard_map(
        on_device,
        mesh=mesh,
        in_specs=placed,
        out_specs=(
            P(("dp", "expert"), None, None),
            P(("dp", "expert"), None, None),
            P(("dp", "expert")),
            P(("dp", "expert")),
            P(("dp", "expert"), None),
            P(("dp", "expert"), None),
            P(("dp", "expert"), None),
            P(("dp", "expert"), None),
            P("expert", "dp", None),
            P("expert", "dp", None),
            P("expert", None, "dp"),
            P("expert", None, "dp"),
            P("expert", "dp", None),
        ),
        check_vma=False,
    )
```

time: 1910 us -> 644 us (0.34)
  waiting for transfers between devices: 1250 us -> 74.9 us
  Pallas kernels: 0 us -> 364 us
  blocking collectives: 256 us -> 0 us
  matrix products: 252 us -> 90.4 us
  local copies, waits for them, and re-layouts: 48.1 us -> 24.8 us
    reduce_scatter x6 -> x2, waiting for transfers between devices: 982 us -> 1.95 us  [the longest x1 1.93 us: on_device(): lax.psum_scatter(partial_out, 'dp', scatter_dimension=0, tiled=True)]
    pallas_call x0 -> x4, Pallas kernels: none -> 364 us  [the longest x1 127 us: start_call(): pl.pallas_call(start_kernel, out_shape=[shaped(small_room, depth), shaped...]
    all_to_all x4 -> x0, blocking collectives: 181 us -> none  [the longest x1 59.2 us: on_device(): lax.all_to_all(keys_part.reshape(experts, seq_len, head_width).astype(jnp...]
    dot_general x36 -> x16, matrix products: 241 us -> 84.2 us  [the longest x1 13.5 us: on_device(): jnp.einsum('rf,rd->fd', scaled.reshape(total_rows, room)[:, :units], give...]
    all_gather x6 -> x1, waiting for transfers between devices: 165 us -> 12.2 us  [on_device(): lax.all_gather(given_rows.reshape(expert_rows, model_width), 'dp', axis=0...]
    unnamed x1 -> x0, blocking collectives: 39.1 us -> none
    all_gather x4 -> x0, blocking collectives: 36 us -> none  [the longest x1 10.4 us: on_device(): lax.all_gather(attn_gain.astype(jnp.bfloat16), 'dp', axis=0, tiled=True)]
    unnamed x16 -> x3, waiting for transfers between devices: 34.2 us -> 0.05 us
  transfers between devices with their start and end apart: 22 -> 10, of which waited for: 17 -> 6; matrix products, arithmetic and copies ran while one was open for 15% -> 19% of each run, Pallas kernels for 0% -> 18%
where the time goes in v1:
time: 644 us; the launch traced here: 634 us
  Pallas kernels  364 us (57%)
  matrix products  90.4 us (14%)
  waiting for transfers between devices  74.9 us (12%)
  starting transfers between devices  32.7 us (5%)
  other arithmetic  32.6 us (5%)
  local copies, waits for them, and re-layouts  24.8 us (4%)
  between operations  14.5 us (2%)
    pallas_call x1, Pallas kernels, start_call(): pl.pallas_call(start_kernel, out_shape=[shaped(small_room, depth), shaped...  127 us
    pallas_call x1, Pallas kernels, ffn_call(): pl.pallas_call(partial(ffn_kernel, rows), out_shape=[jax.ShapeDtypeStruct...  120 us
    pallas_call x1, Pallas kernels, back_call(): pl.pallas_call(back_kernel, out_shape=[jax.ShapeDtypeStruct((rows, heads_...  100 us
    all_to_all x7, waiting for transfers between devices, exchange(): lax.all_to_all(value, 'expert', split_axis=0, concat_axis=0, tiled=True)  60.8 us
    all_to_all x7, starting transfers between devices, exchange(): lax.all_to_all(value, 'expert', split_axis=0, concat_axis=0, tiled=True)  32.5 us
    pallas_call x1, Pallas kernels, total_small(): pl.pallas_call(partial(total_kernel, groups, experts), out_shape=jax.Shap...  16.2 us
    dot_general x1, matrix products, on_device(): jnp.einsum('rf,rd->fd', scaled.reshape(total_rows, room)[:, :units], give...  13.5 us
  transfers between devices with their start and end apart: 10, of which 6 were waited for; matrix products, arithmetic and copies ran while one was open for 19% of the time, Pallas kernels for 18%

profile of v1, /device:TPU:0, one launch (start us, length us, event | category | flops | bytes accessed | tf_op | source)
XLA Modules:
  0.0 634.0 jit_solution(17769015567882605992)
XLA Ops:
  7.2 1.3 copy.67.lengths
  8.6 1.3 copy_bitcast_fusion.1
  10.2 0.8 pad_maximum_fusion
  10.9 127.5 %attend_start.1 = (bf16[16,2048]{1,0:T(8,128)(2,1)}, f32[64,128]{1,0:T(8,128)}, bf16[288,512]{1,0:T(8,128)(2,1)}, s32[288,1]{1,0:T(8,128)}, f32[288,128]{1,0:T(8...) custom-call(bf16[128,2048]{1,0:T(8,128)(2,1)} %bitcast.159, ...), custom_call_target="tpu_custom_call" | custom-call | flops 99999997952 | bytes 300000000 | tf_op jit(solution)/shard_map/attend_start/pallas_call | solution.py:2011
  138.5 6.0 all-to-all-start
  146.7 3.9 convert_bitcast_fusion.2
  150.6 5.7 convert_bitcast_fusion.1
  156.4 2.0 convert_bitcast_fusion
  158.4 1.3 dynamic-slice_bitcast_fusion
  160.3 0.7 eq.114
  161.6 4.1 pad.20.gate_ref
  165.7 2.1 pad.21.up_ref
  167.8 2.0 pad.18.down_ref
  170.2 0.7 compare_convert_fusion.1
  171.4 0.7 select_reduce_fusion.7
  172.1 2.4 convert_subtract_fusion.pick_ref
  174.6 4.1 multiply_reduce_fusion.2
  178.9 0.8 copy-done.2
  179.7 1.6 convolution_convert_fusion.1
  181.3 5.2 all-to-all-start.1
  186.7 12.2 %all-gather.2.cloned.1.call-done = bf16[2304,2048]{1,0:T(8,128)(2,1)} async-done(((bf16[288,2048]{1,0:T(8,128)(2,1)}), bf16[2304,2048]{1,0:T(8,128)(2,1)}) %all-gather.2.cloned.1.call-update) | async-done | bytes 9437200 | tf_op jit(solution)/shard_map/all_gather | solution.py:2359
  198.9 12.8 %fusion.51 = f32[2304,768]{1,0:T(8,128)} fusion(bf16[2304,2048]{1,0:T(8,128)(2,1)} %all-gather.2.cloned.1.call-done, bf16[704,2048]{1,0:T(8,128)(2,1)} %copy-done.4), kind=kOutput, calls=%fused_computation.135 | convolution fusion | flops 7247757312 | bytes 19398656 | tf_op jit(solution)/shard_map/rd,fd->rf/dot_general | solution.py:2405
  211.6 3.2 all-to-all-done.1
  214.8 120.3 %ffn.1 = (bf16[8,288,2048]{2,1,0:T(8,128)(2,1)}, bf16[8,288,768]{2,1,0:T(8,128)(2,1)}, bf16[8,288,768]{2,1,0:T(8,128)(2,1)}, bf16[8,288,768]{2,1,0:T(8,128)(2,1)...) custom-call(bf16[288,2048]{1,0:T(8,128)(2,1)} %bitcast.24.own_ref, f32[8,288,768]{2,1,0:T(8,128)} %bitcast.160, ...), custom_call_target="tpu_custom_call" | custom-call | tf_op jit(solution)/shard_map/ffn/pallas_call | solution.py:963
  335.4 3.8 all-to-all-start.2
  339.3 13.5 %convolution_bitcast_fusion.2 = f32[1,704,2048]{2,1,0:T(8,128)} fusion(bf16[2304,2048]{1,0:T(8,128)(2,1)} %all-gather.2.cloned.1.call-done, bf16[2304,768]{1,0:T(8,128)(2,1)} %bitcast.211), kind=kOutput, calls=%fused_computation.10 | convolution fusion | flops 6643777536 | bytes 18743296 | tf_op jit(solution)/shard_map/rf,rd->fd/dot_general | solution.py:2424
  352.8 11.2 %convolution_bitcast_fusion.1 = f32[1,2048,704]{1,2,0:T(8,128)} fusion(bf16[2304,2048]{1,0:T(8,128)(2,1)} %bitcast.207, bf16[2304,768]{1,0:T(8,128)(2,1)S(1)} %bitcast.210), kind=kOutput, calls=%fused_computation.9 | convolution fusion | flops 6643777536 | bytes 18743296 | tf_op jit(solution)/shard_map/rd,rf->df/dot_general | solution.py:2430
  364.0 6.0 all-to-all-done.2
  370.7 0.9 multiply_reduce_fusion.3
  371.6 1.6 fusion.50
  373.2 1.6 convolution_convert_fusion.3
  374.8 4.8 all-to-all-start.3
  379.6 12.3 %convolution_bitcast_fusion = f32[1,2048,704]{1,2,0:T(8,128)} fusion(bf16[2304,2048]{1,0:T(8,128)(2,1)} %bitcast.208, bf16[2304,768]{1,0:T(8,128)(2,1)} %bitcast.209), kind=kOutput, calls=%fused_computation.8 | convolution fusion | flops 6643777536 | bytes 18743296 | tf_op jit(solution)/shard_map/rd,rf->df/dot_general | solution.py:2436
  391.9 16.1 %all-to-all-done.3 = bf16[4,72,2048]{2,1,0:T(8,128)(2,1)} async-done(((bf16[4,72,2048]{2,1,0:T(8,128)(2,1)}), bf16[4,72,2048]{2,1,0:T(8,128)(2,1)}, u32[]{:S(2)}, u32[]{:S(2)}) %all-to-all-start.3) | async-done | bytes 1179680 | tf_op jit(solution)/shard_map/all_to_all | solution.py:2278
  408.0 1.9 reduce-scatter.3.cloned.1.call-done
  409.9 4.6 all-to-all-start.4
  414.5 0.7 tile.8
  415.2 0.7 tile.20
  416.0 100.2 %attend_back_sums.1 = (bf16[288,2048]{1,0:T(8,128)(2,1)}, bf16[512,512]{1,0:T(8,128)(2,1)}, bf16[512,512]{1,0:T(8,128)(2,1)}, bf16[256,2048]{1,0:T(8,128)(2,1)}, bf16[256,2048]{1,0:T(8,128)(2,1)}) custom-call(bf16[288,2048]{1,0:T(8,128)(2,1)} %bitcast.47.grad_ref, bf16[288,2048]{1,0:T(8,128)(2,1)} %get-tuple-element.70.rows_ref, ...), custom_call_target="tpu_custom_call" | custom-call | flops 60000002048 | bytes 200000000 | tf_op jit(solution)/shard_map/attend_back_sums/pallas_call | solution.py:1481
  516.2 5.2 fusion.60
  521.4 3.3 fusion.59
  524.6 11.3 %add_convert_fusion = bf16[512,2048]{1,0:T(8,128)(2,1)} fusion(f32[512,2048]{1,0:T(8,128)} %fusion.60, f32[512,2048]{1,0:T(8,128)} %fusion.59, bf16[288,512]{1,0:T(8,128)(2,1)S(1)} %copy-done.28, bf16[288,2048]{1,0:T(8,128)(2,1)} %get-tuple-element.83, bf16[2048,2048]{1,0:T(8,128)(2,1)} %get-tuple-element.84), kind=kOutput, calls=%fused_computation.3 | convolution fusion | flops 3023634432 | bytes 20348928 | tf_op jit(solution)/shard_map/rt,rd->td/dot_general | solution.py:2489
  535.9 5.9 convolution_convert_fusion
  541.8 4.7 all-to-all-start.5
  546.9 3.2 multiply_reduce_fusion
  550.1 1.3 fusion.37
  551.4 1.6 bitcast_convert_fusion.1
  553.0 1.6 bitcast_convert_fusion
  554.6 2.1 multiply_reduce_fusion.1
  556.8 1.0 fusion.23
  557.8 35.5 %all-to-all-done.5 = bf16[4,128,2048]{2,1,0:T(8,128)(2,1)} async-done(((bf16[4,128,2048]{2,1,0:T(8,128)(2,1)}), bf16[4,128,2048]{2,1,0:T(8,128)(2,1)}, u32[]{:S(2)}, u32[]{:S(2)}) %all-to-all-start.5) | async-done | bytes 2097184 | tf_op jit(solution)/shard_map/all_to_all | solution.py:2278
  593.3 2.1 convert_reduce_fusion
  595.4 1.0 fusion.18
  596.4 1.5 fusion.30
  598.2 3.5 all-to-all-start.6
  601.7 1.3 fusion.39
  603.3 0.7 copy.72
  604.0 16.2 %total_small.1 = f32[8,128]{1,0:T(8,128)} custom-call(f32[32,8,128]{2,1,0:T(8,128)} %bitcast.176), custom_call_target="tpu_custom_call" | custom-call | tf_op jit(solution)/shard_map/total_small/pallas_call | solution.py:291
  620.2 0.8 reshape.503
  621.0 0.8 fusion.56
  623.6 1.0 reshape.509
  624.6 0.7 copy.78
  625.4 1.0 copy.73
  626.3 1.0 copy.74
  (122 shorter events, 9.4 us)
Async XLA Ops:
  7.2 191.7 %all-gather.2.cloned.1.call-start = ((), (), s32[]{:S(2)}) async-start(), calls=%async_computation.9 | async-start | bytes 10616832 | tf_op jit(solution)/shard_map/all_gather | solution.py:2359
  138.4 6.0 copy-start.18
  138.4 6.3 copy-start
  138.4 7.7 %copy-start.13 = (bf16[16,2048]{1,0:T(8,128)(2,1)S(1)}, bf16[16,2048]{1,0:T(8,128)(2,1)}, u32[]{:S(2)}) copy-start(bf16[16,2048]{1,0:T(8,128)(2,1)} %get-tuple-element.56) | copy-start | bytes 196612
  138.5 36.1 %all-to-all-start = ((bf16[4,72,2048]{2,1,0:T(8,128)(2,1)}), bf16[4,72,2048]{2,1,0:T(8,128)(2,1)}, u32[]{:S(2)}, u32[]{:S(2)}) async-start(bf16[4,72,2048]{2,1,0:T(8,128)(2,1)} %bitcast.172), calls=%async_computation | async-start | bytes 2359296 | tf_op jit(solution)/shard_map/all_to_all | solution.py:2278
  146.7 9.6 %slice-start = ((s8[5767168]{0:T(1024)(128)(4,1)}), s8[4194304]{0:T(1024)(128)(4,1)S(1)}, s32[]{:S(2)}) async-start(s8[5767168]{0:T(1024)(128)(4,1)} %bitcast.161), calls=%async_computation.12 | async-start | bytes 8388608
  150.6 17.2 %copy-start.4 = (bf16[704,2048]{1,0:T(8,128)(2,1)}, bf16[704,2048]{1,0:T(8,128)(2,1)S(1)}, u32[]{:S(2)}) copy-start(bf16[704,2048]{1,0:T(8,128)(2,1)S(1)} %convert_bitcast_fusion.2) | copy-start | bytes 8650756
  150.6 5.7 slice-start.1
  156.4 3.3 copy-start.26
  161.6 4.1 copy-start.5
  167.8 2.0 copy-start.16
  167.8 2.0 copy-start.23
  167.8 2.3 copy-start.19
  167.8 6.8 %copy-start.12 = (bf16[288,128]{1,0:T(8,128)(2,1)S(1)}, bf16[288,128]{1,0:T(8,128)(2,1)}, u32[]{:S(2)}) copy-start(bf16[288,128]{1,0:T(8,128)(2,1)} %get-tuple-element.57) | copy-start | bytes 221188
  174.6 5.1 copy-start.11
  178.7 1.0 copy-start.2
  181.3 33.5 %all-to-all-start.1 = ((bf16[4,72,2048]{2,1,0:T(8,128)(2,1)}), bf16[4,72,2048]{2,1,0:T(8,128)(2,1)}, u32[]{:S(2)}, u32[]{:S(2)}) async-start(bf16[4,72,2048]{2,1,0:T(8,128)(2,1)} %convolution_convert_fusion.1), calls=%async_computation.1 | async-start | bytes 2359296 | tf_op jit(solution)/shard_map/all_to_all | solution.py:2278
  186.5 223.4 %reduce-scatter.3.cloned.1.call-start = ((), (), s32[]{:S(2)}) async-start(), calls=%async_computation.10 | async-start | bytes 10616832 | tf_op jit(solution)/shard_map/reduce_scatter | solution.py:2422
  335.4 34.6 %all-to-all-start.2 = ((bf16[4,72,2176]{2,1,0:T(8,128)(2,1)}), bf16[4,72,2176]{2,1,0:T(8,128)(2,1)S(1)}, u32[]{:S(2)}, u32[]{:S(2)}) async-start(bf16[4,72,2176]{2,1,0:T(8,128)(2,1)} %bitcast.169), calls=%async_computation.2 | async-start | bytes 2506752 | tf_op jit(solution)/shard_map/all_to_all | solution.py:2278
  339.2 13.6 %copy-start.27 = (bf16[8,288,768]{2,1,0:T(8,128)(2,1)S(1)}, bf16[8,288,768]{2,1,0:T(8,128)(2,1)}, u32[]{:S(2)}) copy-start(bf16[8,288,768]{2,1,0:T(8,128)(2,1)} %get-tuple-element.65) | copy-start | bytes 10616836
  352.8 17.3 %copy-start.21 = (s32[128,2]{0,1:T(2,128)S(1)}, s32[128,2]{0,1:T(2,128)}, u32[]{:S(2)}) copy-start(s32[128,2]{0,1:T(2,128)} %get-tuple-element.142) | copy-start | bytes 3076
  374.8 33.2 %all-to-all-start.3 = ((bf16[4,72,2048]{2,1,0:T(8,128)(2,1)}), bf16[4,72,2048]{2,1,0:T(8,128)(2,1)}, u32[]{:S(2)}, u32[]{:S(2)}) async-start(bf16[4,72,2048]{2,1,0:T(8,128)(2,1)} %convolution_convert_fusion.3), calls=%async_computation.3 | async-start | bytes 2359296 | tf_op jit(solution)/shard_map/all_to_all | solution.py:2278
  379.5 35.0 %copy-start.15 = (f32[128,128]{1,0:T(8,128)S(1)}, f32[128,128]{1,0:T(8,128)}, u32[]{:S(2)}) copy-start(f32[128,128]{1,0:T(8,128)} %get-tuple-element.138.cos_home) | copy-start | bytes 196612
  379.5 35.7 %copy-start.14 = (f32[128,128]{1,0:T(8,128)S(1)}, f32[128,128]{1,0:T(8,128)}, u32[]{:S(2)}) copy-start(f32[128,128]{1,0:T(8,128)} %get-tuple-element.139.sin_home) | copy-start | bytes 196612
  409.9 114.7 %all-to-all-start.4 = ((bf16[4,72,2048]{2,1,0:T(8,128)(2,1)}), bf16[4,72,2048]{2,1,0:T(8,128)(2,1)}, u32[]{:S(2)}, u32[]{:S(2)}) async-start(bf16[4,72,2048]{2,1,0:T(8,128)(2,1)} %bitcast.171), calls=%async_computation.5 | async-start | bytes 2359296 | tf_op jit(solution)/shard_map/all_to_all | solution.py:2278
  414.5 183.7 %reduce-scatter.5.cloned.1.call-start = ((), (), s32[]{:S(2)}) async-start(), calls=%async_computation.11 | async-start | bytes 4718592 | tf_op jit(solution)/shard_map/reduce_scatter | solution.py:2503
  516.2 5.2 copy-start.6
  516.2 5.2 copy-start.7
  521.3 3.3 copy-start.28
  524.6 11.3 %copy-start.8 = (bf16[512,512]{1,0:T(8,128)(2,1)S(1)}, bf16[512,512]{1,0:T(8,128)(2,1)}, u32[]{:S(2)}) copy-start(bf16[512,512]{1,0:T(8,128)(2,1)} %get-tuple-element.92) | copy-start | bytes 1572868
  541.8 51.5 %all-to-all-start.5 = ((bf16[4,128,2048]{2,1,0:T(8,128)(2,1)}), bf16[4,128,2048]{2,1,0:T(8,128)(2,1)}, u32[]{:S(2)}, u32[]{:S(2)}) async-start(bf16[4,128,2048]{2,1,0:T(8,128)(2,1)} %bitcast.164), calls=%async_computation.6 | async-start | bytes 4194304 | tf_op jit(solution)/shard_map/all_to_all | solution.py:2278
  546.8 3.3 copy-start.20
  546.8 3.3 copy-start.22
  546.9 4.6 copy-start.10
  550.0 3.0 copy-start.9
  553.0 3.7 copy-start.1
  553.0 3.7 copy-start.3
  556.8 38.6 %copy-start.17 = (f32[1,2048]{1,0:T(1,128)S(1)}, f32[1,2048]{1,0:T(1,128)}, u32[]{:S(2)}) copy-start(f32[1,2048]{1,0:T(1,128)} %get-tuple-element.120) | copy-start | bytes 24580
  556.8 38.6 %copy-start.24 = (f32[128]{0:T(128)S(1)}, f32[128]{0:T(128)}, u32[]{:S(2)}) copy-start(f32[128]{0:T(128)} %get-tuple-element.131) | copy-start | bytes 1540
  557.8 38.6 %copy-start.25 = (f32[128]{0:T(128)S(1)}, f32[128]{0:T(128)}, u32[]{:S(2)}) copy-start(f32[128]{0:T(128)} %get-tuple-element.130) | copy-start | bytes 1540
  598.2 25.4 %all-to-all-start.6 = ((bf16[4,64,1024]{2,1,0:T(8,128)(2,1)}), bf16[4,64,1024]{2,1,0:T(8,128)(2,1)S(1)}, u32[]{:S(2)}, u32[]{:S(2)}) async-start(bf16[4,64,1024]{2,1,0:T(8,128)(2,1)} %bitcast.173), calls=%async_computation.8 | async-start | bytes 1048576 | tf_op jit(solution)/shard_map/all_to_all | solution.py:2278
Sparse Core Ops, SparseCore 0:
  138.6 60.2 all-gather.1
  335.2 74.6 reduce-scatter.2
  541.9 49.7 reduce-scatter.4

commit v2 on v1

--- a/solution.py
+++ b/solution.py
@@ -845,7 +845,8 @@
             )
         weight = 1.0 / (1.0 + jnp.exp(jnp.concatenate(apart, axis=0)))
         loads = pl.ds(pl.multiple_of(slot * pair, pair), pair)
-        tile = 256
+        tile = width
+        wide = 1024
         partial_dense = jnp.zeros((pair, 128), f32)
 
         def units(number, total):
@@ -858,17 +859,19 @@
             sigmoid = 1.0 / (1.0 + jnp.exp(-gate))
             active = gate * sigmoid
             value = (active * up).astype(bf16)
-            wide = value.astype(f32)
+            exact = value.astype(f32)
             plain = pulled[loads, cut]
             hidden[:, cut] = value
-            scaled[:, cut] = (weight * wide).astype(bf16)
+            scaled[:, cut] = (weight * exact).astype(bf16)
             inner = weight * plain
             grad_gate[:, cut] = (inner * up * (sigmoid * (1.0 + gate * (1.0 - sigmoid)))).astype(
                 bf16
             )
             grad_up[:, cut] = (inner * active).astype(bf16)
-            both = wide * plain
-            return total + both[:, :128] + both[:, 128:]
+            both = exact * plain
+            for start in range(0, tile, 128):
+                total = total + both[:, start : start + 128]
+            return total
 
         partial_dense = lax.fori_loop(0, width // tile, units, partial_dense)
         ones = jnp.ones((8, 128), f32)
@@ -896,7 +899,7 @@
             hops["y4"].start()
 
         def columns(number, carry):
-            cut = pl.ds(pl.multiple_of(number * tile, tile), tile)
+            cut = pl.ds(pl.multiple_of(number * wide, wide), wide)
             made[:, cut] = jnp.dot(
                 hidden[...], down_ref[:, cut], preferred_element_type=f32
             ).astype(bf16)
@@ -906,7 +909,7 @@
             ).astype(bf16)
             return carry
 
-        lax.fori_loop(0, depth // tile, columns, 0)
+        lax.fori_loop(0, depth // wide, columns, 0)
         across_sum(chip).start()
         for copy in saves(chip):
             copy.start()
@@ -1121,11 +1124,13 @@
     key_ref,
     value_ref,
     mixture_ref,
-    query_out,
+    query_weight,
+    back_out,
     key_out,
     value_out,
     output_sum,
     query_sum,
+    query_out,
     grad_hold,
     query_hold,
     back_hold,
@@ -1381,6 +1386,29 @@
 
     lax.fori_loop(0, 8, project, 0)
     outputs.settle(chip_of(mine))
+
+    def stream(step):
+        at = pl.multiple_of(step * tile, tile)
+        return pltpu.make_async_copy(
+            query_weight.at[pl.ds(at, tile)], weights.at[step % 2], load_sem.at[step % 2]
+        )
+
+    stream(0).start()
+
+    def rows_back(step, carry):
+        stream(step).wait()
+
+        @pl.when(step < depth // tile - 1)
+        def _():
+            stream(step + 1).start()
+
+        cut = pl.ds(pl.multiple_of(step * tile, tile), tile)
+        back_out[:, cut] = lax.dot_general(
+            query_out[...], weights[step % 2], contract, preferred_element_type=f32
+        ).astype(bf16)
+        return carry
+
+    lax.fori_loop(0, depth // tile, rows_back, 0)
     piece = 32
 
     @pl.when(jnp.logical_not(edge))
@@ -1465,7 +1493,9 @@
     second.wait()
 
 
-def back_call(grad_rows, rows_flat, places, far, near, output_w, query, key, value, mixture):
+def back_call(
+    grad_rows, rows_flat, places, far, near, output_w, query, key, value, mixture, query_w
+):
     rows, depth = grad_rows.shape
     tokens, heads_width = key.shape
     own = heads_width // 4
@@ -1481,15 +1511,16 @@
     return pl.pallas_call(
         back_kernel,
         out_shape=[
-            jax.ShapeDtypeStruct((rows, heads_width), bf16),
+            jax.ShapeDtypeStruct((rows, depth), bf16),
             jax.ShapeDtypeStruct((tokens, own), bf16),
             jax.ShapeDtypeStruct((tokens, own), bf16),
             jax.ShapeDtypeStruct((tile, depth), bf16),
             jax.ShapeDtypeStruct((tile, depth), bf16),
         ],
-        in_specs=[vmem] * 7 + [ANY] + [vmem] * 4,
+        in_specs=[vmem] * 7 + [ANY] + [vmem] * 4 + [ANY],
         out_specs=[vmem] * 3 + [ANY] * 2,
         scratch_shapes=[
+            pltpu.VMEM((rows, heads_width), bf16),
             pltpu.VMEM((rows, tile), f32),
             pltpu.VMEM((rows, tile), f32),
             pltpu.VMEM((rows, tile), f32),
@@ -1528,7 +1559,19 @@
             flops=60_000_000_000, bytes_accessed=200_000_000, transcendentals=0
         ),
         name="attend_back_sums",
-    )(grad_rows, rows_flat, places, *far, *near, output_w, query, key, value, mixture)
+    )(
+        grad_rows,
+        rows_flat,
+        places,
+        *far,
+        *near,
+        output_w,
+        query,
+        key,
+        value,
+        mixture,
+        query_w,
+    )
 
 
 def start_kernel(
@@ -2204,6 +2247,288 @@
     )
 
 
+def last_kernel(
+    rows_back,
+    table_ref,
+    key_own,
+    value_own,
+    grad_keys,
+    grad_values,
+    normed_ref,
+    home_out,
+    key_out,
+    value_out,
+    part,
+    got,
+    pile,
+    blocks,
+    near,
+    far,
+    swapped,
+    near_send,
+    near_recv,
+    sum_send,
+    sum_recv,
+    got_send,
+    got_recv,
+    pass_send,
+    pass_recv,
+    swap_send,
+    swap_recv,
+):
+    group = lax.axis_index("dp")
+    mine = lax.axis_index("expert")
+    experts = 4
+    side = mine // 2
+    edge = ((mine + 1) % experts) // 2 == 0
+    bits = (1, 2, 4)
+    peers = {mask: (flips(group, mask, bits), mine) for mask in (1, 2, 4)}
+    others = [(mine + hop) % experts for hop in range(1, experts)]
+    barrier([peers[mask] for mask in (1, 2, 4)] + [(group, other) for other in others])
+
+    def send_to(device, source, target, send, recv):
+        return pltpu.make_async_remote_copy(
+            src_ref=source,
+            dst_ref=target,
+            send_sem=send,
+            recv_sem=recv,
+            device_id=device,
+            device_id_type=MESH,
+        )
+
+    def remote(source, target, send, recv, mask):
+        return send_to(peers[mask], source, target, send, recv)
+
+    seq_len, depth = home_out.shape
+    own_width = grad_keys.shape[1]
+    tile = depth // 8
+    contract = (((1,), (1,)), ((), ()))
+    stack = (((0,), (0,)), ((), ()))
+    sums = ChipSums(
+        remote, blocks, near, far, (near_send, near_recv, sum_send, sum_recv), tile
+    )
+
+    def owner_of(number):
+        return jnp.where(
+            number == 0,
+            2 - side,
+            jnp.where(number == 1, 3 - 3 * side, jnp.where(number == 2, 1 + 4 * side - mine, mine)),
+        )
+
+    def give(owner):
+        return send_to(
+            (group, owner), part.at[owner], got.at[mine], got_send.at[owner], got_recv.at[mine]
+        )
+
+    def got_from(source):
+        return send_to(
+            (group, source),
+            part.at[source],
+            got.at[source],
+            got_send.at[source],
+            got_recv.at[source],
+        )
+
+    hand_on = send_to(
+        (group, 1 + side), part.at[2 - side], pile, pass_send.at[0], pass_recv.at[0]
+    )
+
+    def one(step, carry):
+        owner = owner_of(step)
+        at = pl.ds(pl.multiple_of(owner * seq_len, seq_len), seq_len)
+        part[owner] = (
+            lax.dot_general(
+                table_ref[:, at], rows_back[...], stack, preferred_element_type=f32
+            )
+            + lax.dot_general(
+                grad_keys[at], key_own[...], contract, preferred_element_type=f32
+            )
+            + lax.dot_general(
+                grad_values[at], value_own[...], contract, preferred_element_type=f32
+            )
+        ).astype(bf16)
+
+        @pl.when((step == 0) & edge)
+        def _():
+            hand_on.start()
+
+        @pl.when((step == 1) | (step == 2))
+        def _():
+            give(owner).start()
+
+        return carry
+
+    lax.fori_loop(0, experts, one, 0)
+
+    def project(block, carry):
+        number = turned_pair(block, group, bits)
+        columns = pl.ds(pl.multiple_of(number * tile, tile), tile)
+        block_at = pl.ds(pl.multiple_of(block * tile, tile), tile)
+        for half, value in enumerate((grad_keys, grad_values)):
+            blocks[block_at, half * own_width : (half + 1) * own_width] = lax.dot_general(
+                normed_ref[:, columns], value[...], stack, preferred_element_type=f32
+            ).astype(bf16)
+
+        @pl.when(block % 2 == 1)
+        def _():
+            sums.across(block // 2).start()
+
+        return carry
+
+    lax.fori_loop(0, 8, project, 0)
+    piece = 32
+
+    def add_rows(target, start, source, other_start, count):
+        def add(step, carry):
+            at = pl.ds(pl.multiple_of(start + step * piece, piece), piece)
+            have = pl.ds(pl.multiple_of(other_start + step * piece, piece), piece)
+            target[at] = (target[at].astype(f32) + source[have].astype(f32)).astype(target.dtype)
+            return carry
+
+        lax.fori_loop(0, count // piece, add, 0)
+
+    for chip in range(4):
+        sums.settle(chip)
+
+    @pl.when(jnp.logical_not(edge))
+    def _():
+        hand_on.wait_recv()
+        add_rows(part.at[2 - side], 0, pile, 0, seq_len)
+        give(2 - side).start()
+
+    sums.cross()
+    sums.close()
+    share = tile // experts
+    swaps = [
+        send_to(
+            (group, other),
+            blocks.at[pl.ds(pl.multiple_of(other * share, share), share)],
+            swapped.at[mine],
+            swap_send.at[hop],
+            swap_recv.at[hop],
+        )
+        for hop, other in enumerate(others)
+    ]
+    for copy in swaps:
+        copy.start()
+
+    def hand_out(source, value):
+        at = pl.ds(pl.multiple_of(source * own_width, own_width), own_width)
+        key_out[:, at] = value[:, :own_width].astype(f32)
+        value_out[:, at] = value[:, own_width:].astype(f32)
+
+    hand_out(mine, blocks[pl.ds(pl.multiple_of(mine * share, share), share)])
+    for hop in range(1, experts):
+        source = (mine + experts - hop) % experts
+        swaps[hop - 1].wait_recv()
+        hand_out(source, swapped[source])
+
+    home_out[...] = part[mine].astype(f32)
+    for hop in range(1, experts):
+        source = (mine + hop) % experts
+        middle = ((mine + 1) % experts) // 2 == 1
+
+        @pl.when(jnp.logical_not(middle & (source == (mine + 2) % experts)))
+        def _():
+            got_from(source).wait_recv()
+
+            def add(step, carry):
+                at = pl.ds(pl.multiple_of(step * piece, piece), piece)
+                home_out[at] = home_out[at] + got[source, at].astype(f32)
+                return carry
+
+            lax.fori_loop(0, seq_len // piece, add, 0)
+
+    @pl.when(edge)
+    def _():
+        hand_on.wait_send()
+
+    @pl.when(jnp.logical_not(edge))
+    def _():
+        give(2 - side).wait_send()
+
+    for number in (1, 2):
+        give(owner_of(number)).wait_send()
+    for copy in swaps:
+        copy.wait_send()
+    sums.drain()
+
+
+def last_call(rows_back, table, key_own, value_own, grad_keys, grad_values, normed):
+    tokens, own = grad_keys.shape
+    depth = normed.shape[1]
+    experts = 4
+    heads_width = own * experts
+    seq_len = tokens // experts
+    tile = depth // 8
+    share = tile // experts
+    vmem = pl.BlockSpec(memory_space=pltpu.VMEM)
+
+    def dma(*shape):
+        return pltpu.SemaphoreType.DMA(shape)
+
+    def blocks(count):
+        return pltpu.VMEM((count * tile, 2 * own), bf16)
+
+    return pl.pallas_call(
+        last_kernel,
+        out_shape=[
+            jax.ShapeDtypeStruct((seq_len, depth), f32),
+            jax.ShapeDtypeStruct((share, heads_width), f32),
+            jax.ShapeDtypeStruct((share, heads_width), f32),
+        ],
+        in_specs=[vmem] * 7,
+        out_specs=[vmem] * 3,
+        scratch_shapes=[
+            pltpu.VMEM((experts, seq_len, depth), bf16),
+            pltpu.VMEM((experts, seq_len, depth), bf16),
+            pltpu.VMEM((seq_len, depth), bf16),
+            blocks(8),
+            blocks(4),
+            blocks(3),
+            pltpu.VMEM((experts, share, 2 * own), bf16),
+            dma(4),
+            dma(4),
+            dma(6),
+            dma(6),
+            dma(4),
+            dma(4),
+            dma(1),
+            dma(1),
+            dma(3),
+            dma(3),
+        ],
+        compiler_params=pltpu.CompilerParams(
+            collective_id=5, has_side_effects=True, vmem_limit_bytes=56 * 1024 * 1024
+        ),
+        name="attend_last",
+    )(rows_back, table, key_own, value_own, grad_keys, grad_values, normed)
+
+
+def last_plain(rows_back, table, key_own, value_own, grad_keys, grad_values, normed):
+    experts = lax.axis_size("expert")
+    own_width = grad_keys.shape[1]
+    depth = normed.shape[1]
+    part = (
+        jnp.einsum("rt,rd->td", table, rows_back, preferred_element_type=f32)
+        + jnp.einsum("te,de->td", grad_keys, key_own, preferred_element_type=f32)
+        + jnp.einsum("te,de->td", grad_values, value_own, preferred_element_type=f32)
+    ).astype(bf16)
+    home = jnp.sum(exchange(part.reshape(experts, -1, depth)).astype(f32), axis=0)
+    both = jnp.einsum(
+        "td,te->de",
+        normed,
+        jnp.concatenate([grad_keys, grad_values], axis=1),
+        preferred_element_type=f32,
+    ).astype(bf16)
+    both = lax.psum_scatter(both, "dp", scatter_dimension=0, tiled=True)
+    both = exchange(both.reshape(experts, -1, 2 * own_width))
+    both = both.reshape(experts, -1, 2, own_width).transpose(2, 1, 0, 3).astype(f32)
+    return home, both[0].reshape(-1, experts * own_width), both[1].reshape(
+        -1, experts * own_width
+    )
+
+
 def ffn_plain(own, slopes, picks, router, gate, up, down):
     groups, rows, width = slopes.shape
     depth = own.shape[1]
@@ -2252,7 +2577,9 @@
     )
 
 
-def back_plain(grad_rows, rows_flat, places, far, near, output_w, query, key, value, mixture):
+def back_plain(
+    grad_rows, rows_flat, places, far, near, output_w, query, key, value, mixture, query_w
+):
     experts = lax.axis_size("expert")
     grad_query, keys_part, values_part, output_part = attend_back(
         experts, grad_rows, places, far, output_w, query, key, value, mixture
@@ -2271,7 +2598,8 @@
     query_sum = lax.psum_scatter(
         query_part.astype(bf16), "dp", scatter_dimension=0, tiled=True
     )
-    return grad_query, grad_keys, grad_values, output_sum, query_sum
+    rows_back = jnp.einsum("re,de->rd", grad_query, query_w, preferred_element_type=f32)
+    return rows_back.astype(bf16), grad_keys, grad_values, output_sum, query_sum
 
 
 def exchange(value):
@@ -2469,7 +2797,7 @@
 
     back_moe = exchange(summed_out[0].reshape(experts, capacity, model_width))
     backward = back_call if ready else back_plain
-    grad_query_pre, grad_key_pre, grad_values, output_out, query_out = backward(
+    rows_back, grad_keys, grad_values, output_out, query_out = backward(
         recv_attn_grad.reshape(expert_rows, model_width),
         rows_flat,
         row_places,
@@ -2480,34 +2808,12 @@
         keys_all,
         values_all,
         mixture,
-    )
-    grad_query_pre, back_moe = lax.optimization_barrier((grad_query_pre, back_moe))
-    grad_rows_attn = jnp.einsum(
-        "re,de->rd", grad_query_pre, query_full, preferred_element_type=f32
-    ).astype(bf16)
-    grad_normed_part = (
-        jnp.einsum("rt,rd->td", spread_table, grad_rows_attn, preferred_element_type=f32)
-        + jnp.einsum("te,de->td", grad_key_pre, key_own, preferred_element_type=f32)
-        + jnp.einsum("te,de->td", grad_values, value_own, preferred_element_type=f32)
-    ).astype(bf16)
-    grad_normed_part, grad_key_pre, grad_values = lax.optimization_barrier(
-        (grad_normed_part, grad_key_pre, grad_values)
-    )
-    normed_got = exchange(grad_normed_part.reshape(experts, seq_len, model_width))
-    both_part = jnp.einsum(
-        "td,te->de",
-        normed_group,
-        jnp.concatenate([grad_key_pre, grad_values], axis=1),
-        preferred_element_type=f32,
-    ).astype(bf16)
-    both_own = lax.psum_scatter(both_part, "dp", scatter_dimension=0, tiled=True)
-    normed_got, both_part = lax.optimization_barrier((normed_got, both_part))
-    grad_normed_one = jnp.sum(normed_got.astype(f32), axis=0)
-    both_own = exchange(both_own.reshape(experts, -1, 2 * own_width))
-    both_own = both_own.reshape(experts, -1, 2, own_width).transpose(2, 1, 0, 3).astype(f32)
-    key_grad = both_own[0].reshape(-1, head_width)
-    value_grad = both_own[1].reshape(-1, head_width)
-
+        query_full,
+    )
+    rows_back, back_moe = lax.optimization_barrier((rows_back, back_moe))
+    grad_normed_one, key_grad, value_grad = (last_call if ready else last_plain)(
+        rows_back, spread_table, key_own, value_own, grad_keys, grad_values, normed_group
+    )
     spread_moe = jnp.einsum("ect,ecd->etd", table_moe, back_moe, preferred_element_type=f32)
     moe_sum = jnp.sum(dense_moe.T[:, :, None] * spread_moe, axis=0)
     block_out = (live_rows[:, None] * (middle + moe_sum)).astype(bf16)[None]

time: 644 us -> 613 us (0.952)
  waiting for transfers between devices: 74.9 us -> 30.8 us
  Pallas kernels: 364 us -> 408 us
  matrix products: 90.4 us -> 67.8 us
  starting transfers between devices: 32.7 us -> 24.8 us
    pallas_call x1 -> x2, Pallas kernels: 100 us -> 154 us  [the longest x1 100 us: back_call(): pl.pallas_call(back_kernel, out_shape=[jax.ShapeDtypeStruct((rows, depth)...]
    all_to_all x7 -> x5, waiting for transfers between devices: 60.8 us -> 17.1 us  [exchange(): lax.all_to_all(value, 'expert', split_axis=0, concat_axis=0, tiled=True)]
    dot_general x4 -> x0, matrix products: 25.6 us -> none  [the longest x1 11.3 us: on_device(): jnp.einsum('rt,rd->td', spread_table, grad_rows_attn, preferred_element_t...]
    all_to_all x7 -> x5, starting transfers between devices: 32.5 us -> 24.6 us  [exchange(): lax.all_to_all(value, 'expert', split_axis=0, concat_axis=0, tiled=True)]
  transfers between devices with their start and end apart: 10 -> 7, of which waited for: 6 -> 4; matrix products, arithmetic and copies ran while one was open for 19% -> 18% of each run, Pallas kernels for 18% -> 17%
where the time goes in v2:
time: 613 us; the launch traced here: 603 us
  Pallas kernels  408 us (67%)
  matrix products  67.8 us (11%)
  other arithmetic  33.3 us (5%)
  waiting for transfers between devices  30.8 us (5%)
  starting transfers between devices  24.8 us (4%)
  local copies, waits for them, and re-layouts  23.7 us (4%)
  between operations  14.7 us (2%)
    pallas_call x1, Pallas kernels, start_call(): pl.pallas_call(start_kernel, out_shape=[shaped(small_room, depth), shaped...  127 us
    pallas_call x1, Pallas kernels, ffn_call(): pl.pallas_call(partial(ffn_kernel, rows), out_shape=[jax.ShapeDtypeStruct...  115 us
    pallas_call x1, Pallas kernels, back_call(): pl.pallas_call(back_kernel, out_shape=[jax.ShapeDtypeStruct((rows, depth)...  100 us
    pallas_call x1, Pallas kernels, last_call(): pl.pallas_call(last_kernel, out_shape=[jax.ShapeDtypeStruct((seq_len, dep...  53.7 us
    all_to_all x5, starting transfers between devices, exchange(): lax.all_to_all(value, 'expert', split_axis=0, concat_axis=0, tiled=True)  24.6 us
    all_to_all x5, waiting for transfers between devices, exchange(): lax.all_to_all(value, 'expert', split_axis=0, concat_axis=0, tiled=True)  17.1 us
    dot_general x1, matrix products, on_device(): jnp.einsum('rf,rd->fd', scaled.reshape(total_rows, room)[:, :units], give...  14.1 us
    all_gather x1, waiting for transfers between devices, on_device(): lax.all_gather(given_rows.reshape(expert_rows, model_width), 'dp', axis=0...  13.6 us
  transfers between devices with their start and end apart: 7, of which 4 were waited for; matrix products, arithmetic and copies ran while one was open for 18% of the time, Pallas kernels for 17%

profile of v2, /device:TPU:0, one launch (start us, length us, event | category | flops | bytes accessed | tf_op | source)
XLA Modules:
  0.0 603.3 jit_solution(6228051993969338918)
XLA Ops:
  7.2 1.3 copy.63.lengths
  8.6 1.3 copy_bitcast_fusion
  10.2 0.8 pad_maximum_fusion
  10.9 127.5 %attend_start.1 = (bf16[16,2048]{1,0:T(8,128)(2,1)}, f32[64,128]{1,0:T(8,128)}, bf16[288,512]{1,0:T(8,128)(2,1)}, s32[288,1]{1,0:T(8,128)}, f32[288,128]{1,0:T(8...) custom-call(bf16[128,2048]{1,0:T(8,128)(2,1)} %bitcast.140, ...), custom_call_target="tpu_custom_call" | custom-call | flops 99999997952 | bytes 300000000 | tf_op jit(solution)/shard_map/attend_start/pallas_call | solution.py:2054
  138.5 6.0 all-to-all-start
  145.0 0.6 select_reduce_fusion
  145.6 0.5 multiply_multiply_fusion
  146.1 0.6 slice_convert_fusion
  146.7 3.9 convert_bitcast_fusion.2
  150.6 5.7 convert_bitcast_fusion.1
  156.4 2.0 convert_bitcast_fusion
  158.4 1.3 dynamic-slice_bitcast_fusion
  159.6 0.6 dynamic_slice.11
  160.2 0.7 eq.114
  160.9 0.6 pad.19.router_ref
  161.6 4.1 pad.20.gate_ref
  165.7 2.1 pad.21.up_ref
  167.8 2.0 pad.18.down_ref
  170.2 0.7 compare_convert_fusion.1
  170.9 0.7 select_reduce_fusion.7
  171.6 2.4 convert_subtract_fusion.pick_ref
  174.0 4.1 multiply_reduce_fusion.2
  178.4 1.6 convolution_convert_fusion
  179.9 5.2 all-to-all-start.1
  185.3 13.6 %all-gather.2.cloned.1.call-done = bf16[2304,2048]{1,0:T(8,128)(2,1)} async-done(((bf16[288,2048]{1,0:T(8,128)(2,1)}), bf16[2304,2048]{1,0:T(8,128)(2,1)}) %all-gather.2.cloned.1.call-update) | async-done | bytes 9437200 | tf_op jit(solution)/shard_map/all_gather | solution.py:2687
  198.9 12.8 %fusion.47 = f32[2304,768]{1,0:T(8,128)} fusion(bf16[2304,2048]{1,0:T(8,128)(2,1)} %all-gather.2.cloned.1.call-done, bf16[704,2048]{1,0:T(8,128)(2,1)} %copy-done.2), kind=kOutput, calls=%fused_computation.126 | convolution fusion | flops 7247757312 | bytes 19398656 | tf_op jit(solution)/shard_map/rd,fd->rf/dot_general | solution.py:2733
  211.6 1.8 all-to-all-done.1
  213.4 115.3 %ffn.1 = (bf16[8,288,2048]{2,1,0:T(8,128)(2,1)}, bf16[8,288,768]{2,1,0:T(8,128)(2,1)}, bf16[8,288,768]{2,1,0:T(8,128)(2,1)}, bf16[8,288,768]{2,1,0:T(8,128)(2,1)...) custom-call(bf16[288,2048]{1,0:T(8,128)(2,1)} %bitcast.24.own_ref, f32[8,288,768]{2,1,0:T(8,128)} %bitcast.141, ...), custom_call_target="tpu_custom_call" | custom-call | tf_op jit(solution)/shard_map/ffn/pallas_call | solution.py:966
  329.1 4.7 all-to-all-start.2
  333.8 14.1 %convolution_bitcast_fusion.2 = f32[1,704,2048]{2,1,0:T(8,128)} fusion(bf16[2304,2048]{1,0:T(8,128)(2,1)} %all-gather.2.cloned.1.call-done, bf16[2304,768]{1,0:T(8,128)(2,1)} %bitcast.185), kind=kOutput, calls=%fused_computation.7 | convolution fusion | flops 6643777536 | bytes 18743296 | tf_op jit(solution)/shard_map/rf,rd->fd/dot_general | solution.py:2752
  347.9 11.2 %convolution_bitcast_fusion.1 = f32[1,2048,704]{1,2,0:T(8,128)} fusion(bf16[2304,2048]{1,0:T(8,128)(2,1)} %bitcast.181, bf16[2304,768]{1,0:T(8,128)(2,1)S(1)} %bitcast.184), kind=kOutput, calls=%fused_computation.6 | convolution fusion | flops 6643777536 | bytes 18743296 | tf_op jit(solution)/shard_map/rd,rf->df/dot_general | solution.py:2758
  359.1 5.4 all-to-all-done.2
  364.5 1.0 fusion.52
  365.6 0.6 select_reduce_fusion.5
  366.2 1.7 convolution_bitcast_fusion.3
  368.0 0.9 multiply_reduce_fusion.3
  368.9 2.7 fusion.46
  371.6 1.6 convolution_convert_fusion.1
  373.1 4.4 all-to-all-start.3
  377.6 12.3 %convolution_bitcast_fusion = f32[1,2048,704]{1,2,0:T(8,128)} fusion(bf16[2304,2048]{1,0:T(8,128)(2,1)} %bitcast.182, bf16[2304,768]{1,0:T(8,128)(2,1)} %bitcast.183), kind=kOutput, calls=%fused_computation.5 | convolution fusion | flops 6643777536 | bytes 18743296 | tf_op jit(solution)/shard_map/rd,rf->df/dot_general | solution.py:2764
  389.9 2.0 copy.66
  392.0 2.7 multiply_reduce_fusion
  394.8 1.3 fusion.34
  396.1 10.0 %all-to-all-done.3 = bf16[4,72,2048]{2,1,0:T(8,128)(2,1)} async-done(((bf16[4,72,2048]{2,1,0:T(8,128)(2,1)}), bf16[4,72,2048]{2,1,0:T(8,128)(2,1)}, u32[]{:S(2)}, u32[]{:S(2)}) %all-to-all-start.3) | async-done | bytes 1179680 | tf_op jit(solution)/shard_map/all_to_all | solution.py:2606
  406.0 4.3 all-to-all-start.4
  410.3 0.7 tile.8
  411.0 0.7 tile.20
  411.8 100.0 %attend_back_sums.1 = (bf16[288,2048]{1,0:T(8,128)(2,1)}, bf16[512,512]{1,0:T(8,128)(2,1)}, bf16[512,512]{1,0:T(8,128)(2,1)}, bf16[256,2048]{1,0:T(8,128)(2,1)}, bf16[256,2048]{1,0:T(8,128)(2,1)}) custom-call(bf16[288,2048]{1,0:T(8,128)(2,1)} %bitcast.47.grad_ref, bf16[288,2048]{1,0:T(8,128)(2,1)} %get-tuple-element.69.rows_ref, ...), custom_call_target="tpu_custom_call" | custom-call | flops 60000002048 | bytes 200000000 | tf_op jit(solution)/shard_map/attend_back_sums/pallas_call | solution.py:1511
  511.8 2.9 bitcast_convert_fusion.1
  514.7 1.6 bitcast_convert_fusion
  516.2 2.1 multiply_reduce_fusion.1
  518.4 1.0 fusion.20
  519.4 53.7 %attend_last.1 = (f32[128,2048]{1,0:T(8,128)}, f32[64,2048]{1,0:T(8,128)}, f32[64,2048]{1,0:T(8,128)}) custom-call(bf16[288,2048]{1,0:T(8,128)(2,1)} %get-tuple-element.82.rows_back, bf16[288,512]{1,0:T(8,128)(2,1)} %get-tuple-element.83.table_ref, bf16[2048,512]{1,0:T(8,128)(2,1)} %get-tuple-element.84.key_own, ...), custom_call_target="tpu_custom_call" | custom-call | tf_op jit(solution)/shard_map/attend_last/pallas_call | solution.py:2473
  573.1 2.2 fusion.18
  575.3 1.5 fusion.27
  577.1 1.3 fusion.36
  578.7 0.7 copy.67
  579.4 11.9 %total_small.1 = f32[8,128]{1,0:T(8,128)} custom-call(f32[32,8,128]{2,1,0:T(8,128)} %bitcast.150), custom_call_target="tpu_custom_call" | custom-call | tf_op jit(solution)/shard_map/total_small/pallas_call | solution.py:291
  591.3 0.8 fusion.51
  592.0 0.8 reshape.493
  593.3 0.7 slice.76
  594.0 0.7 slice.78
  594.6 0.8 copy.72
  595.4 0.8 copy.73
  (100 shorter events, 3.5 us)
Async XLA Ops:
  7.2 191.7 %all-gather.2.cloned.1.call-start = ((), (), s32[]{:S(2)}) async-start(), calls=%async_computation.6 | async-start | bytes 10616832 | tf_op jit(solution)/shard_map/all_gather | solution.py:2687
  138.4 6.0 copy-start.15
  138.4 6.3 %copy-start = (bf16[1,128,2048]{2,1,0:T(8,128)(2,1)S(1)}, bf16[1,128,2048]{2,1,0:T(8,128)(2,1)}, u32[]{:S(2)}) copy-start(bf16[1,128,2048]{2,1,0:T(8,128)(2,1)} %param.16) | copy-start | bytes 1572868
  138.4 7.7 %copy-start.10 = (bf16[16,2048]{1,0:T(8,128)(2,1)S(1)}, bf16[16,2048]{1,0:T(8,128)(2,1)}, u32[]{:S(2)}) copy-start(bf16[16,2048]{1,0:T(8,128)(2,1)} %get-tuple-element.55) | copy-start | bytes 196612
  138.5 35.6 %all-to-all-start = ((bf16[4,72,2048]{2,1,0:T(8,128)(2,1)}), bf16[4,72,2048]{2,1,0:T(8,128)(2,1)}, u32[]{:S(2)}, u32[]{:S(2)}) async-start(bf16[4,72,2048]{2,1,0:T(8,128)(2,1)} %bitcast.149), calls=%async_computation | async-start | bytes 2359296 | tf_op jit(solution)/shard_map/all_to_all | solution.py:2606
  146.7 9.6 %slice-start = ((s8[5767168]{0:T(1024)(128)(4,1)}), s8[4194304]{0:T(1024)(128)(4,1)S(1)}, s32[]{:S(2)}) async-start(s8[5767168]{0:T(1024)(128)(4,1)} %bitcast.142), calls=%async_computation.8 | async-start | bytes 8388608
  150.6 17.2 %copy-start.2 = (bf16[704,2048]{1,0:T(8,128)(2,1)}, bf16[704,2048]{1,0:T(8,128)(2,1)S(1)}, u32[]{:S(2)}) copy-start(bf16[704,2048]{1,0:T(8,128)(2,1)S(1)} %convert_bitcast_fusion.2) | copy-start | bytes 8650756
  150.6 5.7 slice-start.1
  156.4 3.3 copy-start.23
  161.6 4.1 copy-start.3
  167.8 2.0 copy-start.13
  167.8 2.0 copy-start.20
  167.8 2.3 copy-start.16
  167.8 6.2 %copy-start.9 = (bf16[288,128]{1,0:T(8,128)(2,1)S(1)}, bf16[288,128]{1,0:T(8,128)(2,1)}, u32[]{:S(2)}) copy-start(bf16[288,128]{1,0:T(8,128)(2,1)} %get-tuple-element.56) | copy-start | bytes 221188
  174.0 4.3 copy-start.8
  178.3 189.6 %copy-start.1 = (f32[128,2048]{1,0:T(8,128)}, f32[128,2048]{1,0:T(8,128)S(1)}, u32[]{:S(2)}) copy-start(f32[128,2048]{1,0:T(8,128)S(1)} %get-tuple-element.108) | copy-start | bytes 3145732
  179.9 33.5 %all-to-all-start.1 = ((bf16[4,72,2048]{2,1,0:T(8,128)(2,1)}), bf16[4,72,2048]{2,1,0:T(8,128)(2,1)}, u32[]{:S(2)}, u32[]{:S(2)}) async-start(bf16[4,72,2048]{2,1,0:T(8,128)(2,1)} %convolution_convert_fusion), calls=%async_computation.1 | async-start | bytes 2359296 | tf_op jit(solution)/shard_map/all_to_all | solution.py:2606
  185.1 220.9 %reduce-scatter.2.cloned.1.call-start = ((), (), s32[]{:S(2)}) async-start(), calls=%async_computation.7 | async-start | bytes 10616832 | tf_op jit(solution)/shard_map/reduce_scatter | solution.py:2750
  329.1 35.5 %all-to-all-start.2 = ((bf16[4,72,2176]{2,1,0:T(8,128)(2,1)}), bf16[4,72,2176]{2,1,0:T(8,128)(2,1)}, u32[]{:S(2)}, u32[]{:S(2)}) async-start(bf16[4,72,2176]{2,1,0:T(8,128)(2,1)} %bitcast.146), calls=%async_computation.2 | async-start | bytes 2506752 | tf_op jit(solution)/shard_map/all_to_all | solution.py:2606
  333.8 14.1 %copy-start.24 = (bf16[8,288,768]{2,1,0:T(8,128)(2,1)S(1)}, bf16[8,288,768]{2,1,0:T(8,128)(2,1)}, u32[]{:S(2)}) copy-start(bf16[8,288,768]{2,1,0:T(8,128)(2,1)} %get-tuple-element.64) | copy-start | bytes 10616836
  347.9 17.6 %copy-start.18 = (s32[128,2]{0,1:T(2,128)S(1)}, s32[128,2]{0,1:T(2,128)}, u32[]{:S(2)}) copy-start(s32[128,2]{0,1:T(2,128)} %get-tuple-element.138) | copy-start | bytes 3076
  373.1 32.9 %all-to-all-start.3 = ((bf16[4,72,2048]{2,1,0:T(8,128)(2,1)}), bf16[4,72,2048]{2,1,0:T(8,128)(2,1)}, u32[]{:S(2)}, u32[]{:S(2)}) async-start(bf16[4,72,2048]{2,1,0:T(8,128)(2,1)} %convolution_convert_fusion.1), calls=%async_computation.3 | async-start | bytes 2359296 | tf_op jit(solution)/shard_map/all_to_all | solution.py:2606
  391.9 2.8 copy-start.17
  392.0 2.8 copy-start.4
  392.0 18.3 %copy-start.12 = (f32[128,128]{1,0:T(8,128)S(1)}, f32[128,128]{1,0:T(8,128)}, u32[]{:S(2)}) copy-start(f32[128,128]{1,0:T(8,128)} %get-tuple-element.134.cos_home) | copy-start | bytes 196612
  394.7 16.4 %copy-start.11 = (f32[128,128]{1,0:T(8,128)S(1)}, f32[128,128]{1,0:T(8,128)}, u32[]{:S(2)}) copy-start(f32[128,128]{1,0:T(8,128)} %get-tuple-element.135.sin_home) | copy-start | bytes 196612
  406.0 110.2 %all-to-all-start.4 = ((bf16[4,72,2048]{2,1,0:T(8,128)(2,1)}), bf16[4,72,2048]{2,1,0:T(8,128)(2,1)}, u32[]{:S(2)}, u32[]{:S(2)}) async-start(bf16[4,72,2048]{2,1,0:T(8,128)(2,1)} %bitcast.147), calls=%async_computation.5 | async-start | bytes 2359296 | tf_op jit(solution)/shard_map/all_to_all | solution.py:2606
  511.8 2.9 copy-start.5
  511.8 4.5 copy-start.19
  519.4 53.7 %copy-start.14 = (f32[1,2048]{1,0:T(1,128)S(1)}, f32[1,2048]{1,0:T(1,128)}, u32[]{:S(2)}) copy-start(f32[1,2048]{1,0:T(1,128)} %get-tuple-element.116) | copy-start | bytes 24580
  519.4 53.7 %copy-start.21 = (f32[128]{0:T(128)S(1)}, f32[128]{0:T(128)}, u32[]{:S(2)}) copy-start(f32[128]{0:T(128)} %get-tuple-element.127) | copy-start | bytes 1540
  519.4 55.9 %copy-start.22 = (f32[128]{0:T(128)S(1)}, f32[128]{0:T(128)}, u32[]{:S(2)}) copy-start(f32[128]{0:T(128)} %get-tuple-element.126) | copy-start | bytes 1540
  576.8 17.8 %copy-start.7 = (f32[64,2048]{1,0:T(8,128)S(1)}, f32[64,2048]{1,0:T(8,128)}, u32[]{:S(2)}) copy-start(f32[64,2048]{1,0:T(8,128)} %get-tuple-element.159) | copy-start | bytes 1572868
  576.8 18.6 %copy-start.6 = (f32[64,2048]{1,0:T(8,128)S(1)}, f32[64,2048]{1,0:T(8,128)}, u32[]{:S(2)}) copy-start(f32[64,2048]{1,0:T(8,128)} %get-tuple-element.160) | copy-start | bytes 1572868
Sparse Core Ops, SparseCore 0:
  138.6 60.2 all-gather.1
  328.9 74.3 reduce-scatter.1

commit v3 on v2

--- a/solution.py
+++ b/solution.py
@@ -251,10 +251,15 @@
     lax.fori_loop(1, devices, greet, 0)
     pl.semaphore_wait(semaphore, devices - 1)
 
+    share = parts.shape[1] // devices
+
+    def columns(owner):
+        return pl.ds(pl.multiple_of((owner * share // 128) * 128, 128), 128)
+
     def copy_of(step):
         other = (me + step) % devices
         return pltpu.make_async_remote_copy(
-            src_ref=parts.at[other],
+            src_ref=parts.at[:, columns(other)],
             dst_ref=held.at[step],
             send_sem=send_sem.at[step],
             recv_sem=recv_sem.at[step],
@@ -267,7 +272,7 @@
         return carry
 
     lax.fori_loop(1, devices, send, 0)
-    held[0] = parts[me]
+    held[0] = parts[:, columns(me)]
 
     def finish(step, carry):
         copy_of(step).wait()
@@ -283,25 +288,22 @@
     devices = groups * experts
     kinds, width = rows.shape
     share = width // devices
-    packed = rows.reshape(kinds, devices, share).transpose(1, 0, 2).reshape(devices, kinds * share)
-    room = -(-kinds * share // 1024) * 1024
-    packed = jnp.pad(packed, ((0, 0), (0, room - kinds * share))).reshape(
-        devices, room // 128, 128
-    )
-    summed = pl.pallas_call(
+    room = -(-kinds // 8) * 8
+    total = pl.pallas_call(
         partial(total_kernel, groups, experts),
-        out_shape=jax.ShapeDtypeStruct((room // 128, 128), f32),
+        out_shape=jax.ShapeDtypeStruct((room, 128), f32),
         in_specs=[pl.BlockSpec(memory_space=pltpu.VMEM)],
         out_specs=pl.BlockSpec(memory_space=pltpu.VMEM),
         scratch_shapes=[
-            pltpu.VMEM((devices, room // 128, 128), f32),
+            pltpu.VMEM((devices, room, 128), f32),
             pltpu.SemaphoreType.DMA((devices,)),
             pltpu.SemaphoreType.DMA((devices,)),
         ],
         compiler_params=pltpu.CompilerParams(collective_id=1, has_side_effects=True),
         name="total_small",
-    )(packed)
-    return summed.reshape(-1)[: kinds * share].reshape(kinds, share)
+    )(jnp.pad(rows, ((0, room - kinds), (0, 0))))
+    place = (lax.axis_index("dp") * experts + lax.axis_index("expert")) % (128 // share)
+    return lax.dynamic_slice_in_dim(total, place * share, share, 1)[:kinds]
 
 
 def turn(value, cosine, sine):
@@ -600,15 +602,18 @@
     slope_ref,
     pick_ref,
     router_ref,
-    gate_ref,
-    up_ref,
-    down_ref,
+    gate_in,
+    up_in,
+    down_in,
     rows_out,
     hidden_out,
     grad_gate_out,
     grad_up_out,
     out_out,
     grad_out,
+    gate_ref,
+    up_ref,
+    down_ref,
     held,
     pulled,
     hidden,
@@ -632,6 +637,7 @@
     dense_recv,
     load_sem,
     save_sem,
+    intake_sem,
 ):
     group = lax.axis_index("dp")
     mine = lax.axis_index("expert")
@@ -640,6 +646,14 @@
     pair = 2 * rows
     bits = (1, 2, 4)
     peers = {mask: (flips(group, mask, bits), mine) for mask in range(1, 8)}
+    intake = [
+        pltpu.make_async_copy(source, target, intake_sem.at[number])
+        for number, (source, target) in enumerate(
+            ((gate_in, gate_ref), (up_in, up_ref), (down_in, down_ref))
+        )
+    ]
+    for copy in intake:
+        copy.start()
     barrier([peers[mask] for mask in range(1, 8)])
 
     def remote(source, target, send, recv, mask):
@@ -786,6 +800,8 @@
     for which in range(2):
         pull(0, 0, which).start()
     seat.wait()
+    for copy in intake:
+        copy.wait()
 
     def step(chip, carry):
         @pl.when(chip == 0)
@@ -973,9 +989,12 @@
             jax.ShapeDtypeStruct((8, rows, depth), bf16),
             jax.ShapeDtypeStruct((rows, depth + 128), bf16),
         ],
-        in_specs=[ANY, ANY, vmem, vmem, vmem, vmem, vmem],
+        in_specs=[ANY, ANY, vmem, vmem, ANY, ANY, ANY],
         out_specs=[ANY] * 6,
         scratch_shapes=[
+            pltpu.VMEM((width, depth), bf16),
+            pltpu.VMEM((width, depth), bf16),
+            pltpu.VMEM((width, depth), bf16),
             pltpu.VMEM((8 * rows, depth), bf16),
             pltpu.VMEM((4 * rows, width), f32),
             pltpu.VMEM((2 * rows, width), bf16),
@@ -999,6 +1018,7 @@
             pltpu.SemaphoreType.DMA((8,)),
             pltpu.SemaphoreType.DMA((3,)),
             pltpu.SemaphoreType.DMA((10,)),
+            pltpu.SemaphoreType.DMA((3,)),
         ],
         compiler_params=pltpu.CompilerParams(
             collective_id=2, has_side_effects=True, vmem_limit_bytes=61 * 1024 * 1024
@@ -1112,25 +1132,31 @@
 
 
 def back_kernel(
-    grad_ref,
-    rows_ref,
+    grad_in,
+    rows_in,
     place_ref,
     cos_far,
     sin_far,
     cos_near,
     sin_near,
     weight_ref,
-    query_ref,
-    key_ref,
-    value_ref,
-    mixture_ref,
+    query_in,
+    key_in,
+    value_in,
+    mixture_in,
     query_weight,
     back_out,
     key_out,
     value_out,
     output_sum,
-    query_sum,
+    query_part,
     query_out,
+    grad_ref,
+    rows_ref,
+    query_ref,
+    key_ref,
+    value_ref,
+    mixture_ref,
     grad_hold,
     query_hold,
     back_hold,
@@ -1142,25 +1168,22 @@
     key_pass,
     value_pass,
     total_hold,
+    result_hold,
     output_blocks,
     output_near,
     output_far,
     query_blocks,
-    query_near,
-    query_far,
     output_near_send,
     output_near_recv,
     output_sum_send,
     output_sum_recv,
-    query_near_send,
-    query_near_recv,
-    query_sum_send,
-    query_sum_recv,
+    query_save,
     got_send,
     got_recv,
     pass_send,
     pass_recv,
     load_sem,
+    intake_sem,
 ):
     group = lax.axis_index("dp")
     mine = lax.axis_index("expert")
@@ -1169,6 +1192,21 @@
     edge = ((mine + 1) % experts) // 2 == 0
     bits = (1, 2, 4)
     peers = {mask: (flips(group, mask, bits), mine) for mask in (1, 2, 4)}
+    intake = [
+        pltpu.make_async_copy(source, target, intake_sem.at[number])
+        for number, (source, target) in enumerate(
+            (
+                (grad_in, grad_ref),
+                (mixture_in, mixture_ref),
+                (query_in, query_ref),
+                (key_in, key_ref),
+                (value_in, value_ref),
+                (rows_in, rows_ref),
+            )
+        )
+    ]
+    for copy in intake:
+        copy.start()
     barrier(
         [peers[mask] for mask in (1, 2, 4)]
         + [(group, (mine + step) % experts) for step in range(1, experts)]
@@ -1200,20 +1238,17 @@
         (output_near_send, output_near_recv, output_sum_send, output_sum_recv),
         tile,
     )
-    queries_sum = ChipSums(
-        remote,
-        query_blocks,
-        query_near,
-        query_far,
-        (query_near_send, query_near_recv, query_sum_send, query_sum_recv),
-        tile,
-    )
-
     def owner_of(number):
+        near_end = 2 - side
+        far_end = 3 - 3 * side
         return jnp.where(
             number == 0,
-            2 - side,
-            jnp.where(number == 1, 3 - 3 * side, jnp.where(number == 2, 1 + 4 * side - mine, mine)),
+            jnp.where(edge, near_end, far_end),
+            jnp.where(
+                number == 1,
+                jnp.where(edge, far_end, near_end),
+                jnp.where(number == 2, 1 + 4 * side - mine, mine),
+            ),
         )
 
     def chip_of(owner):
@@ -1274,6 +1309,8 @@
         ]
 
     load(0).start()
+    for copy in intake:
+        copy.wait()
     block_slices = blocks_of(experts, rows_all, tokens, tile)
     spots = lax.broadcasted_iota(jnp.int32, (rows_all, seq_len), 1)
 
@@ -1354,14 +1391,12 @@
         def _():
             outputs.across(chip).start()
 
-            @pl.when(step == 1)
+            @pl.when((step == 1) & edge)
             def _():
-                @pl.when(edge)
-                def _():
-                    for copy in hand_on(1 + side):
-                        copy.start()
-
-            @pl.when((step == 3) | (step == 5))
+                for copy in hand_on(1 + side):
+                    copy.start()
+
+            @pl.when(((step == 1) | (step == 5)) & jnp.logical_not(edge))
             def _():
                 for copy in give(owner):
                     copy.start()
@@ -1370,18 +1405,16 @@
 
     lax.fori_loop(0, 8, one, 0)
 
-    def project(block, carry):
-        number = turned_pair(block, group, bits)
-        columns = pl.ds(pl.multiple_of(number * tile, tile), tile)
-        block_at = pl.ds(pl.multiple_of(block * tile, tile), tile)
-        query_blocks[block_at] = lax.dot_general(
-            rows_ref[:, columns], query_out[...], stack, preferred_element_type=f32
+    def keep(number):
+        at = pl.ds(pl.multiple_of(number * tile, tile), tile)
+        return pltpu.make_async_copy(query_blocks.at[at], query_part.at[at], query_save.at[number])
+
+    def project(number, carry):
+        at = pl.ds(pl.multiple_of(number * tile, tile), tile)
+        query_blocks[at] = lax.dot_general(
+            rows_ref[:, at], query_out[...], stack, preferred_element_type=f32
         ).astype(bf16)
-
-        @pl.when(block % 2 == 1)
-        def _():
-            queries_sum.across(block // 2).start()
-
+        keep(number).start()
         return carry
 
     lax.fori_loop(0, 8, project, 0)
@@ -1407,6 +1440,14 @@
             query_out[...], weights[step % 2], contract, preferred_element_type=f32
         ).astype(bf16)
         return carry
+
+    @pl.when(edge)
+    def _():
+        for copy in hand_on(1 + side):
+            copy.wait_send()
+        for owner in (3 - 3 * side, 1 + 4 * side - mine):
+            for copy in give(owner):
+                copy.start()
 
     lax.fori_loop(0, depth // tile, rows_back, 0)
     piece = 32
@@ -1428,16 +1469,26 @@
         for copy in give(2 - side):
             copy.start()
 
-    for chip in range(4):
-        queries_sum.settle(chip)
+    def deliver(sums, result):
+        half_tile = tile // 2
+        for half in range(2):
+
+            def one(step, carry):
+                at = pl.ds(pl.multiple_of(step * piece, piece), piece)
+                source = pl.ds(pl.multiple_of(half * half_tile + step * piece, piece), piece)
+                result_hold[at] = sums.blocks[source].astype(f32)
+                return carry
+
+            lax.fori_loop(0, half_tile // piece, one, 0)
+            copy = pltpu.make_async_copy(
+                result_hold, result.at[pl.ds(half * half_tile, half_tile)], load_sem.at[0]
+            )
+            copy.start()
+            copy.wait()
+
     outputs.cross()
     outputs.close()
-    result = pltpu.make_async_copy(whole(output_blocks, 0, tile), output_sum, load_sem.at[0])
-    result.start()
-    queries_sum.cross()
-    queries_sum.close()
-    second = pltpu.make_async_copy(whole(query_blocks, 0, tile), query_sum, load_sem.at[1])
-    second.start()
+    deliver(outputs, output_sum)
 
     def expected(source):
         far_end = (mine + 2) % experts
@@ -1474,23 +1525,21 @@
         cut = slice(head * HEAD, (head + 1) * HEAD)
         key_out[:, cut] = turn(total_hold[:, cut], cos_near[...], -sin_near[...]).astype(bf16)
 
-    @pl.when(edge)
-    def _():
-        for copy in hand_on(1 + side):
-            copy.wait_send()
-
     @pl.when(jnp.logical_not(edge))
     def _():
         for copy in give(2 - side):
             copy.wait_send()
 
-    for number in (1, 2):
-        for copy in give(owner_of(number)):
+    for owner in (3 - 3 * side, 1 + 4 * side - mine):
+        for copy in give(owner):
             copy.wait_send()
     outputs.drain()
-    queries_sum.drain()
-    result.wait()
-    second.wait()
+
+    def kept(number, carry):
+        keep(number).wait()
+        return carry
+
+    lax.fori_loop(0, 8, kept, 0)
 
 
 def back_call(
@@ -1514,12 +1563,18 @@
             jax.ShapeDtypeStruct((rows, depth), bf16),
             jax.ShapeDtypeStruct((tokens, own), bf16),
             jax.ShapeDtypeStruct((tokens, own), bf16),
-            jax.ShapeDtypeStruct((tile, depth), bf16),
-            jax.ShapeDtypeStruct((tile, depth), bf16),
+            jax.ShapeDtypeStruct((tile, depth), f32),
+            jax.ShapeDtypeStruct((depth, heads_width), bf16),
         ],
-        in_specs=[vmem] * 7 + [ANY] + [vmem] * 4 + [ANY],
+        in_specs=[ANY] * 2 + [vmem] * 5 + [ANY] * 6,
         out_specs=[vmem] * 3 + [ANY] * 2,
         scratch_shapes=[
+            pltpu.VMEM((rows, heads_width), bf16),
+            pltpu.VMEM((rows, depth), bf16),
+            pltpu.VMEM((rows, depth), bf16),
+            pltpu.VMEM((rows, heads_width), bf16),
+            pltpu.VMEM((tokens, heads_width), bf16),
+            pltpu.VMEM((tokens, heads_width), bf16),
             pltpu.VMEM((rows, heads_width), bf16),
             pltpu.VMEM((rows, tile), f32),
             pltpu.VMEM((rows, tile), f32),
@@ -1532,25 +1587,22 @@
             pltpu.VMEM((tokens, own), bf16),
             pltpu.VMEM((tokens, own), bf16),
             pltpu.VMEM((tokens, own), f32),
+            pltpu.VMEM((tile // 2, depth), f32),
             blocks(8),
             blocks(4),
             blocks(3),
             blocks(8),
-            blocks(4),
-            blocks(3),
             dma(4),
             dma(4),
             dma(6),
             dma(6),
-            dma(4),
-            dma(4),
-            dma(6),
-            dma(6),
+            dma(8),
             dma(4, 2),
             dma(4, 2),
             dma(2),
             dma(2),
             dma(2),
+            dma(6),
         ],
         compiler_params=pltpu.CompilerParams(
             collective_id=3, has_side_effects=True, vmem_limit_bytes=61 * 1024 * 1024
@@ -2248,6 +2300,16 @@
 
 
 def last_kernel(
+    rows_in,
+    table_in,
+    key_in,
+    value_in,
+    grad_keys_in,
+    grad_values_in,
+    normed_in,
+    home_out,
+    key_out,
+    value_out,
     rows_back,
     table_ref,
     key_own,
@@ -2255,9 +2317,7 @@
     grad_keys,
     grad_values,
     normed_ref,
-    home_out,
-    key_out,
-    value_out,
+    intake_sem,
     part,
     got,
     pile,
@@ -2284,6 +2344,22 @@
     bits = (1, 2, 4)
     peers = {mask: (flips(group, mask, bits), mine) for mask in (1, 2, 4)}
     others = [(mine + hop) % experts for hop in range(1, experts)]
+    intake = [
+        pltpu.make_async_copy(source, target, intake_sem.at[number])
+        for number, (source, target) in enumerate(
+            (
+                (rows_in, rows_back),
+                (table_in, table_ref),
+                (grad_keys_in, grad_keys),
+                (grad_values_in, grad_values),
+                (key_in, key_own),
+                (value_in, value_own),
+                (normed_in, normed_ref),
+            )
+        )
+    ]
+    for copy in intake:
+        copy.start()
     barrier([peers[mask] for mask in (1, 2, 4)] + [(group, other) for other in others])
 
     def send_to(device, source, target, send, recv):
@@ -2309,10 +2385,16 @@
     )
 
     def owner_of(number):
+        near_end = 2 - side
+        far_end = 3 - 3 * side
         return jnp.where(
             number == 0,
-            2 - side,
-            jnp.where(number == 1, 3 - 3 * side, jnp.where(number == 2, 1 + 4 * side - mine, mine)),
+            jnp.where(edge, near_end, far_end),
+            jnp.where(
+                number == 1,
+                jnp.where(edge, far_end, near_end),
+                jnp.where(number == 2, 1 + 4 * side - mine, mine),
+            ),
         )
 
     def give(owner):
@@ -2332,6 +2414,9 @@
     hand_on = send_to(
         (group, 1 + side), part.at[2 - side], pile, pass_send.at[0], pass_recv.at[0]
     )
+
+    for copy in intake[:-1]:
+        copy.wait()
 
     def one(step, carry):
         owner = owner_of(step)
@@ -2352,7 +2437,7 @@
         def _():
             hand_on.start()
 
-        @pl.when((step == 1) | (step == 2))
+        @pl.when(((step == 0) | (step == 2)) & jnp.logical_not(edge))
         def _():
             give(owner).start()
 
@@ -2375,8 +2460,15 @@
 
         return carry
 
+    intake[-1].wait()
     lax.fori_loop(0, 8, project, 0)
     piece = 32
+
+    @pl.when(edge)
+    def _():
+        hand_on.wait_send()
+        for owner in (3 - 3 * side, 1 + 4 * side - mine):
+            give(owner).start()
 
     def add_rows(target, start, source, other_start, count):
         def add(step, carry):
@@ -2439,22 +2531,19 @@
 
             lax.fori_loop(0, seq_len // piece, add, 0)
 
-    @pl.when(edge)
-    def _():
-        hand_on.wait_send()
-
     @pl.when(jnp.logical_not(edge))
     def _():
         give(2 - side).wait_send()
 
-    for number in (1, 2):
-        give(owner_of(number)).wait_send()
+    for owner in (3 - 3 * side, 1 + 4 * side - mine):
+        give(owner).wait_send()
     for copy in swaps:
         copy.wait_send()
     sums.drain()
 
 
 def last_call(rows_back, table, key_own, value_own, grad_keys, grad_values, normed):
+    rows = rows_back.shape[0]
     tokens, own = grad_keys.shape
     depth = normed.shape[1]
     experts = 4
@@ -2477,9 +2566,17 @@
             jax.ShapeDtypeStruct((share, heads_width), f32),
             jax.ShapeDtypeStruct((share, heads_width), f32),
         ],
-        in_specs=[vmem] * 7,
+        in_specs=[ANY] * 7,
         out_specs=[vmem] * 3,
         scratch_shapes=[
+            pltpu.VMEM((rows, depth), bf16),
+            pltpu.VMEM((rows, tokens), bf16),
+            pltpu.VMEM((depth, own), bf16),
+            pltpu.VMEM((depth, own), bf16),
+            pltpu.VMEM((tokens, own), bf16),
+            pltpu.VMEM((tokens, own), bf16),
+            pltpu.VMEM((tokens, depth), bf16),
+            dma(7),
             pltpu.VMEM((experts, seq_len, depth), bf16),
             pltpu.VMEM((experts, seq_len, depth), bf16),
             pltpu.VMEM((seq_len, depth), bf16),
@@ -2500,6 +2597,9 @@
         ],
         compiler_params=pltpu.CompilerParams(
             collective_id=5, has_side_effects=True, vmem_limit_bytes=56 * 1024 * 1024
+        ),
+        cost_estimate=pl.CostEstimate(
+            flops=40_000_000_000, bytes_accessed=150_000_000, transcendentals=0
         ),
         name="attend_last",
     )(rows_back, table, key_own, value_own, grad_keys, grad_values, normed)
@@ -2595,11 +2695,14 @@
         axis=1,
     ).astype(bf16)
     query_part = jnp.einsum("rd,re->de", rows_flat, grad_query, preferred_element_type=f32)
-    query_sum = lax.psum_scatter(
-        query_part.astype(bf16), "dp", scatter_dimension=0, tiled=True
-    )
     rows_back = jnp.einsum("re,de->rd", grad_query, query_w, preferred_element_type=f32)
-    return rows_back.astype(bf16), grad_keys, grad_values, output_sum, query_sum
+    return (
+        rows_back.astype(bf16),
+        grad_keys,
+        grad_values,
+        output_sum.astype(f32),
+        query_part.astype(bf16),
+    )
 
 
 def exchange(value):
@@ -2797,7 +2900,7 @@
 
     back_moe = exchange(summed_out[0].reshape(experts, capacity, model_width))
     backward = back_call if ready else back_plain
-    rows_back, grad_keys, grad_values, output_out, query_out = backward(
+    rows_back, grad_keys, grad_values, output_out, query_part = backward(
         recv_attn_grad.reshape(expert_rows, model_width),
         rows_flat,
         row_places,
@@ -2810,10 +2913,11 @@
         mixture,
         query_full,
     )
-    rows_back, back_moe = lax.optimization_barrier((rows_back, back_moe))
+    query_out = lax.psum_scatter(query_part, "dp", scatter_dimension=0, tiled=True)
     grad_normed_one, key_grad, value_grad = (last_call if ready else last_plain)(
         rows_back, spread_table, key_own, value_own, grad_keys, grad_values, normed_group
     )
+    grad_normed_one, back_moe = lax.optimization_barrier((grad_normed_one, back_moe))
     spread_moe = jnp.einsum("ect,ecd->etd", table_moe, back_moe, preferred_element_type=f32)
     moe_sum = jnp.sum(dense_moe.T[:, :, None] * spread_moe, axis=0)
     block_out = (live_rows[:, None] * (middle + moe_sum)).astype(bf16)[None]
@@ -2841,7 +2945,7 @@
         key_grad,
         value_grad,
         query_out.astype(f32)[None],
-        output_out.astype(f32)[None],
+        output_out[None],
         gate_grad,
         up_grad,
         down_grad,

time: 613 us -> 617 us (level)
  waiting for transfers between devices: 30.8 us -> 41.7 us
  other arithmetic: 33.3 us -> 25.6 us
    pallas_call x1, Pallas kernels: 53.7 us -> 74.4 us  [last_call(): pl.pallas_call(last_kernel, out_shape=[jax.ShapeDtypeStruct((seq_len, dep...]
    pallas_call x1, Pallas kernels: 100 us -> 83.6 us  [back_call(): pl.pallas_call(back_kernel, out_shape=[jax.ShapeDtypeStruct((rows, depth)...]
    all_to_all x5, waiting for transfers between devices: 17.1 us -> 23.4 us  [exchange(): lax.all_to_all(value, 'expert', split_axis=0, concat_axis=0, tiled=True)]
  transfers between devices with their start and end apart: 7 -> 8, of which waited for: 4 -> 5; matrix products, arithmetic and copies ran while one was open for 18% -> 17% of each run, Pallas kernels for 17% -> 15%
where the time goes in v3:
time: 617 us; the launch traced here: 607 us
  Pallas kernels  411 us (67%)
  matrix products  66.5 us (11%)
  waiting for transfers between devices  41.7 us (7%)
  other arithmetic  25.6 us (4%)
  local copies, waits for them, and re-layouts  24 us (4%)
  starting transfers between devices  23.7 us (4%)
  between operations  14.4 us (2%)
    pallas_call x1, Pallas kernels, start_call(): pl.pallas_call(start_kernel, out_shape=[shaped(small_room, depth), shaped...  127 us
    pallas_call x1, Pallas kernels, ffn_call(): pl.pallas_call(partial(ffn_kernel, rows), out_shape=[jax.ShapeDtypeStruct...  112 us
    pallas_call x1, Pallas kernels, back_call(): pl.pallas_call(back_kernel, out_shape=[jax.ShapeDtypeStruct((rows, depth)...  83.6 us
    pallas_call x1, Pallas kernels, last_call(): pl.pallas_call(last_kernel, out_shape=[jax.ShapeDtypeStruct((seq_len, dep...  74.4 us
    all_to_all x5, waiting for transfers between devices, exchange(): lax.all_to_all(value, 'expert', split_axis=0, concat_axis=0, tiled=True)  23.4 us
    all_to_all x5, starting transfers between devices, exchange(): lax.all_to_all(value, 'expert', split_axis=0, concat_axis=0, tiled=True)  23.2 us
    all_gather x1, waiting for transfers between devices, on_device(): lax.all_gather(given_rows.reshape(expert_rows, model_width), 'dp', axis=0...  15.9 us
    pallas_call x1, Pallas kernels, total_small(): pl.pallas_call(partial(total_kernel, groups, experts), out_shape=jax.Shap...  13.9 us
  transfers between devices with their start and end apart: 8, of which 5 were waited for; matrix products, arithmetic and copies ran while one was open for 17% of the time, Pallas kernels for 15%

profile of v3, /device:TPU:0, one launch (start us, length us, event | category | flops | bytes accessed | tf_op | source)
XLA Modules:
  0.0 607.0 jit_solution(2625906208137997609)
XLA Ops:
  7.2 1.3 copy.55.lengths
  8.6 1.3 copy_bitcast_fusion
  9.9 0.3 fusion.32
  10.2 0.8 pad_maximum_fusion
  10.9 127.4 %attend_start.1 = (bf16[16,2048]{1,0:T(8,128)(2,1)}, f32[64,128]{1,0:T(8,128)}, bf16[288,512]{1,0:T(8,128)(2,1)}, s32[288,1]{1,0:T(8,128)}, f32[288,128]{1,0:T(8...) custom-call(bf16[128,2048]{1,0:T(8,128)(2,1)} %bitcast.138, ...), custom_call_target="tpu_custom_call" | custom-call | flops 99999997952 | bytes 300000000 | tf_op jit(solution)/shard_map/attend_start/pallas_call | solution.py:2106
  138.4 6.0 all-to-all-start
  144.9 0.6 select_reduce_fusion
  145.6 0.5 multiply_multiply_fusion
  146.1 5.4 convert_bitcast_fusion.2
  151.5 2.0 convert_bitcast_fusion.1
  153.5 0.5 slice-done.2
  154.1 0.8 slice-done.3
  154.8 2.0 convert_bitcast_fusion
  156.9 0.7 dynamic-slice_bitcast_fusion.2
  157.6 0.6 dynamic_slice.14
  158.3 0.6 pad.19.router_ref
  158.9 4.2 pad.20.gate_in
  163.1 2.1 pad.21.up_in
  165.2 0.6 copy-done.1
  165.8 2.1 pad.18.down_in
  168.0 0.3 fusion.29
  168.3 0.6 compare_convert_fusion.1
  169.1 1.9 convert_subtract_fusion.pick_ref
  170.9 2.4 all-to-all-done
  173.4 4.1 multiply_reduce_fusion.2
  177.7 1.6 convolution_convert_fusion
  179.2 3.5 all-to-all-start.1
  183.0 15.9 %all-gather.2.cloned.1.call-done = bf16[2304,2048]{1,0:T(8,128)(2,1)} async-done(((bf16[288,2048]{1,0:T(8,128)(2,1)}), bf16[2304,2048]{1,0:T(8,128)(2,1)}) %all-gather.2.cloned.1.call-update) | async-done | bytes 9437200 | tf_op jit(solution)/shard_map/all_gather | solution.py:2790
  198.9 12.8 %fusion.45 = f32[2304,768]{1,0:T(8,128)} fusion(bf16[2304,2048]{1,0:T(8,128)(2,1)} %all-gather.2.cloned.1.call-done, bf16[704,2048]{1,0:T(8,128)(2,1)} %convert_bitcast_fusion.2), kind=kOutput, calls=%fused_computation.126 | convolution fusion | flops 7247757312 | bytes 19398656 | tf_op jit(solution)/shard_map/rd,fd->rf/dot_general | solution.py:2836
  211.7 1.0 copy-done.3
  212.7 111.9 %ffn.1 = (bf16[8,288,2048]{2,1,0:T(8,128)(2,1)}, bf16[8,288,768]{2,1,0:T(8,128)(2,1)}, bf16[8,288,768]{2,1,0:T(8,128)(2,1)}, bf16[8,288,768]{2,1,0:T(8,128)(2,1)...) custom-call(bf16[288,2048]{1,0:T(8,128)(2,1)} %bitcast.144, f32[8,288,768]{2,1,0:T(8,128)} %bitcast.139, ...), custom_call_target="tpu_custom_call" | custom-call | tf_op jit(solution)/shard_map/ffn/pallas_call | solution.py:982
  324.8 0.8 copy-done.4
  325.8 5.0 all-to-all-start.2
  330.8 13.9 %convolution_bitcast_fusion.2 = f32[1,704,2048]{2,1,0:T(8,128)} fusion(bf16[2304,2048]{1,0:T(8,128)(2,1)} %all-gather.2.cloned.1.call-done, bf16[2304,768]{1,0:T(8,128)(2,1)} %bitcast.184), kind=kOutput, calls=%fused_computation.7 | convolution fusion | flops 6643777536 | bytes 18743296 | tf_op jit(solution)/shard_map/rf,rd->fd/dot_general | solution.py:2855
  344.7 11.2 %convolution_bitcast_fusion.1 = f32[1,2048,704]{1,2,0:T(8,128)} fusion(bf16[2304,2048]{1,0:T(8,128)(2,1)} %bitcast.180, bf16[2304,768]{1,0:T(8,128)(2,1)S(1)} %bitcast.183), kind=kOutput, calls=%fused_computation.6 | convolution fusion | flops 6643777536 | bytes 18743296 | tf_op jit(solution)/shard_map/rd,rf->df/dot_general | solution.py:2861
  355.9 5.4 all-to-all-done.2
  361.6 0.5 convolution_bitcast_fusion.3
  362.1 1.0 multiply_reduce_fusion.3
  363.1 1.6 subtract_add_fusion
  364.7 1.6 convolution_convert_fusion.1
  366.2 4.3 all-to-all-start.3
  370.8 12.3 %convolution_bitcast_fusion = f32[1,2048,704]{1,2,0:T(8,128)} fusion(bf16[2304,2048]{1,0:T(8,128)(2,1)} %bitcast.181, bf16[2304,768]{1,0:T(8,128)(2,1)} %bitcast.182), kind=kOutput, calls=%fused_computation.5 | convolution fusion | flops 6643777536 | bytes 18743296 | tf_op jit(solution)/shard_map/rd,rf->df/dot_general | solution.py:2867
  383.1 15.5 %all-to-all-done.3 = bf16[4,72,2048]{2,1,0:T(8,128)(2,1)} async-done(((bf16[4,72,2048]{2,1,0:T(8,128)(2,1)}), bf16[4,72,2048]{2,1,0:T(8,128)(2,1)}, u32[]{:S(2)}, u32[]{:S(2)}) %all-to-all-start.3) | async-done | bytes 1179680 | tf_op jit(solution)/shard_map/all_to_all | solution.py:2709
  398.6 2.4 reduce-scatter.3.cloned.1.call-done
  401.0 0.7 tile.8
  401.7 0.7 tile.20
  402.4 83.6 %attend_back_sums.1 = (bf16[288,2048]{1,0:T(8,128)(2,1)}, bf16[512,512]{1,0:T(8,128)(2,1)}, bf16[512,512]{1,0:T(8,128)(2,1)}, f32[256,2048]{1,0:T(8,128)}, bf16[2048,2048]{1,0:T(8,128)(2,1)}) custom-call(bf16[288,2048]{1,0:T(8,128)(2,1)} %bitcast.47.grad_in, bf16[288,2048]{1,0:T(8,128)(2,1)} %get-tuple-element.69.rows_in, ...), custom_call_target="tpu_custom_call" | custom-call | flops 60000002048 | bytes 200000000 | tf_op jit(solution)/shard_map/attend_back_sums/pallas_call | solution.py:1560
  486.1 2.5 multiply_reduce_fusion
  488.7 1.5 fusion.51
  490.2 0.4 fusion.27
  490.6 4.4 all-to-all-start.4
  495.0 74.4 %attend_last.1 = (f32[128,2048]{1,0:T(8,128)}, f32[64,2048]{1,0:T(8,128)}, f32[64,2048]{1,0:T(8,128)}) custom-call(bf16[288,2048]{1,0:T(8,128)(2,1)} %get-tuple-element.79.rows_in, bf16[288,512]{1,0:T(8,128)(2,1)} %get-tuple-element.80.table_in, bf16[2048,512]{1,0:T(8,128)(2,1)} %get-tuple-element.81.key_in, bf16[2048,512]{1,0:T(8,128)(2,1)} %get-tuple-element.82.value_in, ...), custom_call_target="tpu_custom_call" | custom-call | flops 40000000000 | bytes 150000000 | tf_op jit(solution)/shard_map/attend_last/pallas_call | solution.py:2562
  569.4 3.0 fusion.18
  572.5 0.7 select_maximum_fusion.parts
  573.2 13.9 %total_small.1 = f32[16,128]{1,0:T(8,128)} custom-call(f32[16,2048]{1,0:T(8,128)} %select_maximum_fusion.parts), custom_call_target="tpu_custom_call" | custom-call | tf_op jit(solution)/shard_map/total_small/pallas_call | solution.py:292
  587.2 1.4 dynamic-slice_bitcast_fusion.4
  588.5 1.4 dynamic-slice_bitcast_fusion
  589.9 2.1 multiply_reduce_fusion.1
  592.1 1.0 fusion.20
  593.1 1.3 fusion.23
  594.4 2.9 bitcast_convert_fusion
  597.3 0.8 copy.62
  598.1 0.8 copy.63
  598.9 1.3 copy.64
  (85 shorter events, 2.3 us)
Async XLA Ops:
  7.2 191.7 %all-gather.2.cloned.1.call-start = ((), (), s32[]{:S(2)}) async-start(), calls=%async_computation.7 | async-start | bytes 10616832 | tf_op jit(solution)/shard_map/all_gather | solution.py:2790
  138.4 6.0 copy-start.14
  138.4 6.4 %copy-start = (bf16[1,128,2048]{2,1,0:T(8,128)(2,1)S(1)}, bf16[1,128,2048]{2,1,0:T(8,128)(2,1)}, u32[]{:S(2)}) copy-start(bf16[1,128,2048]{2,1,0:T(8,128)(2,1)} %param.16) | copy-start | bytes 1572868
  138.4 7.7 %copy-start.11 = (bf16[16,2048]{1,0:T(8,128)(2,1)S(1)}, bf16[16,2048]{1,0:T(8,128)(2,1)}, u32[]{:S(2)}) copy-start(bf16[16,2048]{1,0:T(8,128)(2,1)} %get-tuple-element.55) | copy-start | bytes 196612
  138.4 13.1 %slice-start = ((s8[5767168]{0:T(1024)(128)(4,1)}), s8[1572864]{0:T(1024)(128)(4,1)S(1)}, s32[]{:S(2)}) async-start(s8[5767168]{0:T(1024)(128)(4,1)} %bitcast.140), calls=%async_computation.10 | async-start | bytes 3145728
  138.4 34.9 %all-to-all-start = ((bf16[4,72,2048]{2,1,0:T(8,128)(2,1)}), bf16[4,72,2048]{2,1,0:T(8,128)(2,1)}, u32[]{:S(2)}, u32[]{:S(2)}) async-start(bf16[4,72,2048]{2,1,0:T(8,128)(2,1)} %bitcast.149), calls=%async_computation | async-start | bytes 2359296 | tf_op jit(solution)/shard_map/all_to_all | solution.py:2709
  146.1 5.4 slice-start.1
  146.1 8.0 %slice-start.2 = ((s8[5767168]{0:T(1024)(128)(4,1)}), s8[4194304]{0:T(1024)(128)(4,1)S(1)}, s32[]{:S(2)}) async-start(s8[5767168]{0:T(1024)(128)(4,1)} %bitcast.142), calls=%async_computation.12 | async-start | bytes 8388608
  151.5 3.3 slice-start.3
  154.8 2.7 copy-start.16
  158.2 4.8 copy-start.2
  163.1 2.8 copy-start.1
  165.8 7.5 %copy-start.10 = (bf16[288,128]{1,0:T(8,128)(2,1)S(1)}, bf16[288,128]{1,0:T(8,128)(2,1)}, u32[]{:S(2)}) copy-start(bf16[288,128]{1,0:T(8,128)(2,1)} %get-tuple-element.56) | copy-start | bytes 221188
  173.4 4.3 copy-start.9
  179.2 32.4 %all-to-all-start.1 = ((bf16[4,72,2048]{2,1,0:T(8,128)(2,1)}), bf16[4,72,2048]{2,1,0:T(8,128)(2,1)S(1)}, u32[]{:S(2)}, u32[]{:S(2)}) async-start(bf16[4,72,2048]{2,1,0:T(8,128)(2,1)} %convolution_convert_fusion), calls=%async_computation.1 | async-start | bytes 2359296 | tf_op jit(solution)/shard_map/all_to_all | solution.py:2709
  182.8 218.2 %reduce-scatter.3.cloned.1.call-start = ((), (), s32[]{:S(2)}) async-start(), calls=%async_computation.8 | async-start | bytes 10616832 | tf_op jit(solution)/shard_map/reduce_scatter | solution.py:2853
  211.7 1.0 copy-start.3
  324.8 0.8 copy-start.4
  325.8 35.5 %all-to-all-start.2 = ((bf16[4,72,2176]{2,1,0:T(8,128)(2,1)}), bf16[4,72,2176]{2,1,0:T(8,128)(2,1)S(1)}, u32[]{:S(2)}, u32[]{:S(2)}) async-start(bf16[4,72,2176]{2,1,0:T(8,128)(2,1)} %bitcast.146), calls=%async_computation.2 | async-start | bytes 2506752 | tf_op jit(solution)/shard_map/all_to_all | solution.py:2709
  330.8 13.9 %copy-start.17 = (bf16[8,288,768]{2,1,0:T(8,128)(2,1)S(1)}, bf16[8,288,768]{2,1,0:T(8,128)(2,1)}, u32[]{:S(2)}) copy-start(bf16[8,288,768]{2,1,0:T(8,128)(2,1)} %get-tuple-element.64) | copy-start | bytes 10616836
  366.2 32.4 %all-to-all-start.3 = ((bf16[4,72,2048]{2,1,0:T(8,128)(2,1)}), bf16[4,72,2048]{2,1,0:T(8,128)(2,1)}, u32[]{:S(2)}, u32[]{:S(2)}) async-start(bf16[4,72,2048]{2,1,0:T(8,128)(2,1)} %convolution_convert_fusion.1), calls=%async_computation.3 | async-start | bytes 2359296 | tf_op jit(solution)/shard_map/all_to_all | solution.py:2709
  370.5 223.9 %reduce-scatter.5.cloned.1.call-start = ((), (), s32[]{:S(2)}) async-start(), calls=%async_computation.9 | async-start | bytes 9437184 | tf_op jit(solution)/shard_map/reduce_scatter | solution.py:2916
  370.7 30.2 %copy-start.13 = (f32[128,128]{1,0:T(8,128)S(1)}, f32[128,128]{1,0:T(8,128)}, u32[]{:S(2)}) copy-start(f32[128,128]{1,0:T(8,128)} %get-tuple-element.128.cos_home) | copy-start | bytes 196612
  370.7 30.9 %copy-start.12 = (f32[128,128]{1,0:T(8,128)S(1)}, f32[128,128]{1,0:T(8,128)}, u32[]{:S(2)}) copy-start(f32[128,128]{1,0:T(8,128)} %get-tuple-element.129.sin_home) | copy-start | bytes 196612
  490.6 78.8 %all-to-all-start.4 = ((bf16[4,72,2048]{2,1,0:T(8,128)(2,1)}), bf16[4,72,2048]{2,1,0:T(8,128)(2,1)}, u32[]{:S(2)}, u32[]{:S(2)}) async-start(bf16[4,72,2048]{2,1,0:T(8,128)(2,1)} %bitcast.147), calls=%async_computation.5 | async-start | bytes 2359296 | tf_op jit(solution)/shard_map/all_to_all | solution.py:2709
  572.5 20.6 %copy-start.15 = (f32[128]{0:T(128)S(1)}, f32[128]{0:T(128)}, u32[]{:S(2)}) copy-start(f32[128]{0:T(128)} %get-tuple-element.120) | copy-start | bytes 1540
  587.2 5.9 copy-start.5
  593.1 4.2 copy-start.8
  593.1 5.0 copy-start.7
  594.4 4.5 copy-start.6
Sparse Core Ops, SparseCore 0:
  138.6 60.3 all-gather.1
  324.7 76.2 reduce-scatter.2
  486.2 85.1 reduce-scatter.4

commit v4 on v3

--- a/solution.py
+++ b/solution.py
@@ -629,6 +629,8 @@
     dense_hold,
     far_send,
     far_recv,
+    across_send,
+    across_recv,
     near_send,
     near_recv,
     sum_send,
@@ -636,6 +638,7 @@
     dense_send,
     dense_recv,
     load_sem,
+    seat_sem,
     save_sem,
     intake_sem,
 ):
@@ -643,7 +646,9 @@
     mine = lax.axis_index("expert")
     depth = held.shape[1]
     width = hidden.shape[1]
-    pair = 2 * rows
+    part = rows // 2
+    pair = 2 * part
+    split = -(-part // 32) * 16
     bits = (1, 2, 4)
     peers = {mask: (flips(group, mask, bits), mine) for mask in range(1, 8)}
     intake = [
@@ -666,47 +671,83 @@
             device_id_type=MESH,
         )
 
-    def own_half(half):
-        size = rows // 2
-        return own_ref.at[pl.ds(half * size, size)]
+    def cut_of(half):
+        return (0, split) if half == 0 else (split, part - split)
+
+    def seat_of(batch, block):
+        return pl.ds(pl.multiple_of((batch * 8 + block) * part, 16), part)
+
+    def some(batch, block, half):
+        start, size = cut_of(half)
+        return held.at[pl.ds((batch * 8 + block) * part + start, size)]
 
     sends = {}
-    for slot, (mask, half) in enumerate(((2, 0), (4, 1), (2, 1), (4, 0))):
-        sends[mask, half] = remote(
-            own_half(half),
-            halves(held, mask, rows, half),
-            far_send.at[slot],
-            far_recv.at[slot],
-            mask,
-        )
-    sends[6, 0] = remote(
-        halves(held, 2, rows, 0), halves(held, 6, rows, 0), far_send.at[4], far_recv.at[4], 4
-    )
-    sends[6, 1] = remote(
-        halves(held, 4, rows, 1), halves(held, 6, rows, 1), far_send.at[5], far_recv.at[5], 2
-    )
     across = {}
-    for chip in range(4):
-        across[chip] = remote(
-            own_ref if chip == 0 else whole(held, 2 * chip, rows),
-            whole(held, 2 * chip + 1, rows),
-            near_send.at[chip],
-            near_recv.at[chip],
-            1,
-        )
-    sends[2, 0].start()
-    sends[4, 1].start()
-    across[0].start()
-    sends[2, 1].start()
-    sends[4, 0].start()
-    seat = pltpu.make_async_copy(own_ref, whole(held, 0, rows), load_sem.at[2])
-    seat.start()
-
-    def pull(chip, slot, which):
-        block = group_of(2 * chip + which)
-        return pltpu.make_async_copy(
-            slope_ref.at[block], whole(pulled, 2 * slot + which, rows), load_sem.at[which]
-        )
+    for batch in range(2):
+        for slot, (mask, half) in enumerate(((2, 0), (4, 1), (2, 1), (4, 0))):
+            start, size = cut_of(half)
+            sends[batch, mask, half] = remote(
+                own_ref.at[pl.ds(batch * part + start, size)],
+                some(batch, mask, half),
+                far_send.at[batch, slot],
+                far_recv.at[batch, slot],
+                mask,
+            )
+        sends[batch, 6, 0] = remote(
+            some(batch, 2, 0),
+            some(batch, 6, 0),
+            far_send.at[batch, 4],
+            far_recv.at[batch, 4],
+            4,
+        )
+        sends[batch, 6, 1] = remote(
+            some(batch, 4, 1),
+            some(batch, 6, 1),
+            far_send.at[batch, 5],
+            far_recv.at[batch, 5],
+            2,
+        )
+        for chip in range(4):
+            across[batch, chip] = remote(
+                own_ref.at[pl.ds(batch * part, part)]
+                if chip == 0
+                else held.at[seat_of(batch, 2 * chip)],
+                held.at[seat_of(batch, 2 * chip + 1)],
+                across_send.at[batch, chip],
+                across_recv.at[batch, chip],
+                1,
+            )
+
+    def leave(batch):
+        for mask, half in ((2, 0), (4, 1), (2, 1), (4, 0)):
+            sends[batch, mask, half].start()
+
+    def pass_on(batch):
+        sends[batch, 2, 0].wait_recv()
+        sends[batch, 6, 0].start()
+        sends[batch, 4, 1].wait_recv()
+        sends[batch, 6, 1].start()
+        sends[batch, 2, 1].wait_recv()
+        across[batch, 1].start()
+        sends[batch, 4, 0].wait_recv()
+        across[batch, 2].start()
+
+    def finish(batch):
+        sends[batch, 6, 0].wait_recv()
+        sends[batch, 6, 1].wait_recv()
+        across[batch, 3].start()
+
+    leave(0)
+    across[0, 0].start()
+    across[1, 0].start()
+    seats = [
+        pltpu.make_async_copy(
+            own_ref.at[pl.ds(batch * part, part)], held.at[seat_of(batch, 0)], seat_sem.at[batch]
+        )
+        for batch in range(2)
+    ]
+    for seat in seats:
+        seat.start()
 
     def group_of(index):
         result = group
@@ -716,53 +757,57 @@
             result = result + on * turned
         return result
 
-    def saves(chip):
+    def rows_of(step, which):
+        return group_of(2 * (step % 4) + which), pl.ds(
+            pl.multiple_of((step // 4) * part, 16), part
+        )
+
+    def pull(step, which):
+        block, at = rows_of(step, which)
+        slot = 2 * (step % 2) + which
+        return pltpu.make_async_copy(
+            slope_ref.at[block, at],
+            pulled.at[pl.ds(pl.multiple_of(slot * part, 16), part)],
+            load_sem.at[which],
+        )
+
+    def saves(step):
         copies = []
         for which in range(2):
-            block = group_of(2 * chip + which)
+            block, at = rows_of(step, which)
+            own = pl.ds(which * part, part)
             for number, (source, target) in enumerate(
                 (
-                    (whole(held, 2 * chip + which, rows), rows_out.at[block]),
-                    (whole(scaled, which, rows), hidden_out.at[block]),
-                    (whole(grad_gate, which, rows), grad_gate_out.at[block]),
-                    (whole(grad_up, which, rows), grad_up_out.at[block]),
-                    (whole(made, which, rows), out_out.at[block]),
+                    (held.at[seat_of(step // 4, 2 * (step % 4) + which)], rows_out),
+                    (scaled.at[own], hidden_out),
+                    (grad_gate.at[own], grad_gate_out),
+                    (grad_up.at[own], grad_up_out),
+                    (made.at[own], out_out),
                 )
             ):
                 copies.append(
-                    pltpu.make_async_copy(source, target, save_sem.at[5 * which + number])
+                    pltpu.make_async_copy(
+                        source, target.at[block, at], save_sem.at[5 * which + number]
+                    )
                 )
         return copies
 
-    def across_sum(chip):
-        return remote(
-            whole(grads, 2 * chip + 1, rows),
-            whole(near, chip, rows),
-            near_send.at[4 + chip],
-            near_recv.at[4 + chip],
-            1,
-        )
-
-    hops = {}
-    for slot, (key, block, half, mask) in enumerate(
-        (
-            ("x2", 2, 0, 2),
-            ("x6", 6, 0, 2),
-            ("y4", 4, 1, 4),
-            ("y6", 6, 1, 4),
-            ("then_y", 4, 0, 4),
-            ("then_x", 2, 1, 2),
-        )
-    ):
-        size = rows // 2
-        hops[key] = remote(
-            halves(grads, block, rows, half),
-            far.at[pl.ds(slot * size, size)],
-            sum_send.at[slot],
-            sum_recv.at[slot],
-            mask,
-        )
-    far_slots = {"x2": 0, "x6": 1, "y4": 2, "y6": 3, "then_y": 4, "then_x": 5}
+    sums = [
+        ChipSums(
+            remote,
+            grads.at[batch],
+            near.at[batch],
+            far.at[batch],
+            (
+                near_send.at[batch],
+                near_recv.at[batch],
+                sum_send.at[batch],
+                sum_recv.at[batch],
+            ),
+            part,
+        )
+        for batch in range(2)
+    ]
 
     def dense_hop(mask):
         return remote(
@@ -773,94 +818,83 @@
             mask,
         )
 
-    def join(chip):
-        across_sum(chip).wait_recv()
-        block = 2 * chip
-
-        def add(step, carry):
-            at = pl.ds(pl.multiple_of(block * rows + step * 48, 16), 48)
-            other = pl.ds(pl.multiple_of(chip * rows + step * 48, 16), 48)
-            grads[at] = (grads[at].astype(f32) + near[other].astype(f32)).astype(bf16)
-            return carry
-
-        lax.fori_loop(0, rows // 48, add, 0)
-
-    def add_far(block, half, key):
-        size = rows // 2
-        hops[key].wait_recv()
-
-        def add(step, carry):
-            at = pl.ds(pl.multiple_of(block * rows + half * size + step * 48, 16), 48)
-            other = pl.ds(far_slots[key] * size + pl.multiple_of(step * 48, 16), 48)
-            grads[at] = (grads[at].astype(f32) + far[other].astype(f32)).astype(bf16)
-            return carry
-
-        lax.fori_loop(0, size // 48, add, 0)
-
     for which in range(2):
-        pull(0, 0, which).start()
-    seat.wait()
+        pull(0, which).start()
+    for seat in seats:
+        seat.wait()
     for copy in intake:
         copy.wait()
 
-    def step(chip, carry):
-        @pl.when(chip == 0)
+    def one(step, carry):
+        batch = step // 4
+        chip = step % 4
+
+        @pl.when(step == 0)
         def _():
-            across[0].wait_recv()
-
-        @pl.when(chip == 1)
+            across[0, 0].wait_recv()
+
+        @pl.when(step == 1)
         def _():
-            sends[2, 0].wait_recv()
-            sends[6, 0].start()
-            sends[4, 1].wait_recv()
-            sends[6, 1].start()
-            sends[2, 1].wait_recv()
-            across[1].start()
-            sends[4, 0].wait_recv()
-            across[2].start()
-            across[1].wait_recv()
-
-        @pl.when(chip == 2)
+            pass_on(0)
+            across[0, 1].wait_recv()
+
+        @pl.when(step == 2)
         def _():
-            sends[6, 0].wait_recv()
-            sends[6, 1].wait_recv()
-            across[3].start()
-            across[2].wait_recv()
-
-        @pl.when(chip == 3)
+            finish(0)
+            leave(1)
+            across[0, 2].wait_recv()
+
+        @pl.when(step == 3)
         def _():
-            across[3].wait_recv()
-
-        slot = chip % 2
+            across[0, 3].wait_recv()
+
+        @pl.when(step == 4)
+        def _():
+            across[1, 0].wait_recv()
+
+        @pl.when(step == 5)
+        def _():
+            pass_on(1)
+            across[1, 1].wait_recv()
+
+        @pl.when(step == 6)
+        def _():
+            finish(1)
+            across[1, 2].wait_recv()
+
+        @pl.when(step == 7)
+        def _():
+            across[1, 3].wait_recv()
+
         for which in range(2):
-            pull(chip, slot, which).wait()
-
-        @pl.when(chip < 3)
+            pull(step, which).wait()
+
+        @pl.when(step < 7)
         def _():
             for which in range(2):
-                pull(chip + 1, 1 - slot, which).start()
-
-        @pl.when(chip > 0)
+                pull(step + 1, which).start()
+
+        @pl.when(step > 0)
         def _():
-            for copy in saves(chip - 1):
+            for copy in saves(step - 1):
                 copy.wait()
 
-        base = pl.multiple_of(chip * pair, pair)
-        at = pl.ds(base, pair)
+        at = pl.ds(pl.multiple_of((batch * 8 + 2 * chip) * part, pair), pair)
+        grads_at = pl.ds(pl.multiple_of(2 * chip * part, pair), pair)
+        loads = pl.ds(pl.multiple_of((step % 2) * pair, pair), pair)
         logits = lax.dot_general(
             held[at], router_ref[...], (((1,), (1,)), ((), ())), preferred_element_type=f32
         )
         apart = []
         for which in range(2):
             block = group_of(2 * chip + which)
-            picks = pick_ref[pl.ds(pl.multiple_of(block * rows, rows), rows)]
+            picks = pick_ref[pl.ds(pl.multiple_of(block * rows + batch * part, 8), part)]
             apart.append(
                 jnp.sum(
-                    logits[which * rows : (which + 1) * rows] * picks, axis=-1, keepdims=True
+                    logits[which * part : (which + 1) * part] * picks, axis=-1, keepdims=True
                 )
             )
         weight = 1.0 / (1.0 + jnp.exp(jnp.concatenate(apart, axis=0)))
-        loads = pl.ds(pl.multiple_of(slot * pair, pair), pair)
         tile = width
         wide = 1024
         partial_dense = jnp.zeros((pair, 128), f32)
@@ -892,87 +926,98 @@
         partial_dense = lax.fori_loop(0, width // tile, units, partial_dense)
         ones = jnp.ones((8, 128), f32)
         for which in range(2):
-            dense[2 * chip + which] = lax.dot_general(
+            dense[2 * chip + which, pl.ds(pl.multiple_of(batch * 8, 8), 8)] = lax.dot_general(
                 ones,
-                partial_dense[which * rows : (which + 1) * rows],
+                partial_dense[which * part : (which + 1) * part],
                 (((1,), (1,)), ((), ())),
                 precision=highest,
                 preferred_element_type=f32,
             )
 
-        @pl.when(chip == 1)
-        def _():
-            join(0)
-
-        @pl.when(chip == 2)
-        def _():
-            join(1)
-            hops["x2"].start()
-
-        @pl.when(chip == 3)
-        def _():
-            join(2)
-            hops["y4"].start()
+        for number in range(2):
+
+            @pl.when((step > 4 * number) & (step <= 4 * number + 4))
+            def _():
+                sums[number].settle((step - 1) % 4)
 
         def columns(number, carry):
             cut = pl.ds(pl.multiple_of(number * wide, wide), wide)
             made[:, cut] = jnp.dot(
                 hidden[...], down_ref[:, cut], preferred_element_type=f32
             ).astype(bf16)
-            grads[at, cut] = (
+            grads[batch, grads_at, cut] = (
                 jnp.dot(grad_gate[...], gate_ref[:, cut], preferred_element_type=f32)
                 + jnp.dot(grad_up[...], up_ref[:, cut], preferred_element_type=f32)
             ).astype(bf16)
             return carry
 
         lax.fori_loop(0, depth // wide, columns, 0)
-        across_sum(chip).start()
-        for copy in saves(chip):
+        for number in range(2):
+
+            @pl.when(batch == number)
+            def _():
+                sums[number].across(chip).start()
+
+        for copy in saves(step):
             copy.start()
+
+        @pl.when(step == 6)
+        def _():
+            sums[0].cross()
+
         return carry
 
-    lax.fori_loop(0, 4, step, 0)
-    join(3)
-    hops["x6"].start()
-    hops["y6"].start()
+    lax.fori_loop(0, 8, one, 0)
+    sums[1].settle(3)
     for mask in range(1, 8):
         dense_hop(mask).start()
-    add_far(0, 0, "x2")
-    add_far(0, 1, "y4")
-    add_far(4, 0, "x6")
-    hops["then_y"].start()
-    add_far(2, 1, "y6")
-    hops["then_x"].start()
+    sums[0].close()
     total = dense[0]
     for mask in range(1, 8):
         dense_hop(mask).wait_recv()
         total = total + dense_far[mask]
-    for copy in saves(3):
+    for copy in saves(7):
         copy.wait()
     pick = (lax.broadcasted_iota(jnp.int32, (8, 128), 0) == 0).astype(f32)
-    column = lax.dot_general(
-        total, pick, (((0,), (0,)), ((), ())), precision=highest, preferred_element_type=f32
+    column = jnp.concatenate(
+        [
+            lax.dot_general(
+                total[batch * 8 : (batch + 1) * 8],
+                pick,
+                (((0,), (0,)), ((), ())),
+                precision=highest,
+                preferred_element_type=f32,
+            )
+            for batch in range(2)
+        ],
+        axis=0,
     )
     upper = column.astype(bf16)
     lower = (column - upper.astype(f32)).astype(bf16)
     lane = lax.broadcasted_iota(jnp.int32, column.shape, 1)
     dense_hold[...] = jnp.where(lane == 0, upper, jnp.where(lane == 1, lower, 0.0)).astype(bf16)
-    add_far(0, 0, "then_y")
-    add_far(0, 1, "then_x")
-    tail = pltpu.make_async_copy(dense_hold, grad_out.at[:, pl.ds(depth, 128)], load_sem.at[0])
-    tail.start()
-    last = pltpu.make_async_copy(
-        whole(grads, 0, rows), grad_out.at[:, pl.ds(0, depth)], load_sem.at[2]
-    )
-    last.start()
-    for copy in list(sends.values()) + list(across.values()) + list(hops.values()):
+    last = [pltpu.make_async_copy(dense_hold, grad_out.at[:, pl.ds(depth, 128)], load_sem.at[0])]
+    for batch in range(2):
+        last.append(
+            pltpu.make_async_copy(
+                grads.at[batch, pl.ds(0, part)],
+                grad_out.at[pl.ds(batch * part, part), pl.ds(0, depth)],
+                seat_sem.at[batch],
+            )
+        )
+    last[0].start()
+    last[1].start()
+    sums[1].cross()
+    sums[1].close()
+    last[2].start()
+    for copy in list(sends.values()) + list(across.values()):
         copy.wait_send()
-    for chip in range(4):
-        across_sum(chip).wait_send()
+    for batch in range(2):
+        sums[batch].drain()
     for mask in range(1, 8):
         dense_hop(mask).wait_send()
-    last.wait()
-    tail.wait()
+    for copy in last:
+        copy.wait()
 
 
 def ffn_call(own, slopes, picks, router, gate, up, down):
@@ -996,27 +1041,30 @@
             pltpu.VMEM((width, depth), bf16),
             pltpu.VMEM((width, depth), bf16),
             pltpu.VMEM((8 * rows, depth), bf16),
-            pltpu.VMEM((4 * rows, width), f32),
-            pltpu.VMEM((2 * rows, width), bf16),
-            pltpu.VMEM((2 * rows, width), bf16),
-            pltpu.VMEM((2 * rows, width), bf16),
-            pltpu.VMEM((2 * rows, width), bf16),
-            pltpu.VMEM((2 * rows, depth), bf16),
-            pltpu.VMEM((8 * rows, depth), bf16),
-            pltpu.VMEM((4 * rows, depth), bf16),
-            pltpu.VMEM((3 * rows, depth), bf16),
-            pltpu.VMEM((8, 8, rows), f32),
-            pltpu.VMEM((8, 8, rows), f32),
+            pltpu.VMEM((2 * rows, width), f32),
+            pltpu.VMEM((rows, width), bf16),
+            pltpu.VMEM((rows, width), bf16),
+            pltpu.VMEM((rows, width), bf16),
+            pltpu.VMEM((rows, width), bf16),
+            pltpu.VMEM((rows, depth), bf16),
+            pltpu.VMEM((2, 4 * rows, depth), bf16),
+            pltpu.VMEM((2, 2 * rows, depth), bf16),
+            pltpu.VMEM((2, 3 * rows // 2, depth), bf16),
+            pltpu.VMEM((8, 16, rows // 2), f32),
+            pltpu.VMEM((8, 16, rows // 2), f32),
             pltpu.VMEM((rows, 128), bf16),
-            pltpu.SemaphoreType.DMA((6,)),
-            pltpu.SemaphoreType.DMA((6,)),
+            pltpu.SemaphoreType.DMA((2, 6)),
+            pltpu.SemaphoreType.DMA((2, 6)),
+            pltpu.SemaphoreType.DMA((2, 4)),
+            pltpu.SemaphoreType.DMA((2, 4)),
+            pltpu.SemaphoreType.DMA((2, 4)),
+            pltpu.SemaphoreType.DMA((2, 4)),
+            pltpu.SemaphoreType.DMA((2, 6)),
+            pltpu.SemaphoreType.DMA((2, 6)),
             pltpu.SemaphoreType.DMA((8,)),
             pltpu.SemaphoreType.DMA((8,)),
-            pltpu.SemaphoreType.DMA((6,)),
-            pltpu.SemaphoreType.DMA((6,)),
-            pltpu.SemaphoreType.DMA((8,)),
-            pltpu.SemaphoreType.DMA((8,)),
-            pltpu.SemaphoreType.DMA((3,)),
+            pltpu.SemaphoreType.DMA((2,)),
+            pltpu.SemaphoreType.DMA((2,)),
             pltpu.SemaphoreType.DMA((10,)),
             pltpu.SemaphoreType.DMA((3,)),
         ],
@@ -1033,7 +1081,8 @@
         self.remote = remote
         self.near_send, self.near_recv, self.sum_send, self.sum_recv = sems
         self.hops = {}
-        size = rows // 2
+        self.split = -(-rows // 32) * 16
+        place = 0
         for slot, (key, block, half, mask) in enumerate(
             (
                 ("x2", 2, 0, 2),
@@ -1044,16 +1093,21 @@
                 ("then_x", 2, 1, 2),
             )
         ):
+            start, size = self.half(half)
             self.hops[key] = (
                 remote(
-                    halves(blocks, block, rows, half),
-                    far.at[pl.ds(slot * size, size)],
+                    blocks.at[pl.ds(block * rows + start, size)],
+                    far.at[pl.ds(place, size)],
                     self.sum_send.at[slot],
                     self.sum_recv.at[slot],
                     mask,
                 ),
-                slot * size,
-            )
+                place,
+            )
+            place += size
+
+    def half(self, number):
+        return (0, self.split) if number == 0 else (self.split, self.rows - self.split)
 
     def across(self, chip):
         return self.remote(
@@ -1065,7 +1119,7 @@
         )
 
     def add(self, start, other, other_start, count):
-        piece = 48 if count % 48 == 0 else 32
+        piece = next(size for size in (48, 32, 16) if count % size == 0)
 
         def one(step, carry):
             at = pl.ds(pl.multiple_of(start + step * piece, 16), piece)
@@ -1099,10 +1153,10 @@
             self.begin("y6")
 
     def add_far(self, block, half, key):
-        size = self.rows // 2
+        start, size = self.half(half)
         copy, place = self.hops[key]
         copy.wait_recv()
-        self.add(block * self.rows + half * size, self.far, place, size)
+        self.add(block * self.rows + start, self.far, place, size)
 
     def cross(self):
         self.add_far(4, 0, "x6")
@@ -2898,7 +2952,6 @@
         (recv_attn_grad, up_grad, summed_out)
     )
 
-    back_moe = exchange(summed_out[0].reshape(experts, capacity, model_width))
     backward = back_call if ready else back_plain
     rows_back, grad_keys, grad_values, output_out, query_part = backward(
         recv_attn_grad.reshape(expert_rows, model_width),
@@ -2917,7 +2970,8 @@
     grad_normed_one, key_grad, value_grad = (last_call if ready else last_plain)(
         rows_back, spread_table, key_own, value_own, grad_keys, grad_values, normed_group
     )
-    grad_normed_one, back_moe = lax.optimization_barrier((grad_normed_one, back_moe))
+    grad_normed_one, summed_out = lax.optimization_barrier((grad_normed_one, summed_out))
+    back_moe = exchange(summed_out[0].reshape(experts, capacity, model_width))
     spread_moe = jnp.einsum("ect,ecd->etd", table_moe, back_moe, preferred_element_type=f32)
     moe_sum = jnp.sum(dense_moe.T[:, :, None] * spread_moe, axis=0)
     block_out = (live_rows[:, None] * (middle + moe_sum)).astype(bf16)[None]

time: 617 us -> 613 us (level)
  Pallas kernels: 411 us -> 404 us
    pallas_call x1, Pallas kernels: 13.9 us -> 30.1 us  [total_small(): pl.pallas_call(partial(total_kernel, groups, experts), out_shape=jax.Shap...]
    pallas_call x1, Pallas kernels: 74.4 us -> 61 us  [last_call(): pl.pallas_call(last_kernel, out_shape=[jax.ShapeDtypeStruct((seq_len, dep...]
    pallas_call x1, Pallas kernels: 112 us -> 102 us  [ffn_call(): pl.pallas_call(partial(ffn_kernel, rows), out_shape=[jax.ShapeDtypeStruct...]
where the time goes in v4:
time: 613 us; the launch traced here: 604 us
  Pallas kernels  404 us (66%)
  matrix products  66.1 us (11%)
  waiting for transfers between devices  42.5 us (7%)
  other arithmetic  26.7 us (4%)
  starting transfers between devices  26.2 us (4%)
  local copies, waits for them, and re-layouts  24 us (4%)
  between operations  14.7 us (2%)
    pallas_call x1, Pallas kernels, start_call(): pl.pallas_call(start_kernel, out_shape=[shaped(small_room, depth), shaped...  127 us
    pallas_call x1, Pallas kernels, ffn_call(): pl.pallas_call(partial(ffn_kernel, rows), out_shape=[jax.ShapeDtypeStruct...  102 us
    pallas_call x1, Pallas kernels, back_call(): pl.pallas_call(back_kernel, out_shape=[jax.ShapeDtypeStruct((rows, depth)...  83.6 us
    pallas_call x1, Pallas kernels, last_call(): pl.pallas_call(last_kernel, out_shape=[jax.ShapeDtypeStruct((seq_len, dep...  61 us
    pallas_call x1, Pallas kernels, total_small(): pl.pallas_call(partial(total_kernel, groups, experts), out_shape=jax.Shap...  30.1 us
    all_to_all x5, starting transfers between devices, exchange(): lax.all_to_all(value, 'expert', split_axis=0, concat_axis=0, tiled=True)  25.7 us
    all_to_all x5, waiting for transfers between devices, exchange(): lax.all_to_all(value, 'expert', split_axis=0, concat_axis=0, tiled=True)  23 us
    all_gather x1, waiting for transfers between devices, on_device(): lax.all_gather(given_rows.reshape(expert_rows, model_width), 'dp', axis=0...  15.9 us
  transfers between devices with their start and end apart: 8, of which 5 were waited for; matrix products, arithmetic and copies ran while one was open for 17% of the time, Pallas kernels for 15%

profile of v4, /device:TPU:0, one launch (start us, length us, event | category | flops | bytes accessed | tf_op | source)
XLA Modules:
  0.0 604.0 jit_solution(11797924267062780819)
XLA Ops:
  7.2 1.3 copy.55.lengths
  8.6 1.3 copy_bitcast_fusion
  9.9 0.3 fusion.32
  10.2 0.8 pad_maximum_fusion
  10.9 127.4 %attend_start.1 = (bf16[16,2048]{1,0:T(8,128)(2,1)}, f32[64,128]{1,0:T(8,128)}, bf16[288,512]{1,0:T(8,128)(2,1)}, s32[288,1]{1,0:T(8,128)}, f32[288,128]{1,0:T(8...) custom-call(bf16[128,2048]{1,0:T(8,128)(2,1)} %bitcast.138, ...), custom_call_target="tpu_custom_call" | custom-call | flops 99999997952 | bytes 300000000 | tf_op jit(solution)/shard_map/attend_start/pallas_call | solution.py:2160
  138.4 6.0 all-to-all-start
  144.9 0.6 select_reduce_fusion
  145.6 0.5 multiply_multiply_fusion
  146.1 5.4 convert_bitcast_fusion.2
  151.5 2.0 convert_bitcast_fusion.1
  153.6 0.5 slice-done.2
  154.1 0.8 slice-done.3
  154.8 2.0 convert_bitcast_fusion
  156.9 0.7 dynamic-slice_bitcast_fusion.2
  157.6 0.6 dynamic_slice.14
  158.3 0.6 pad.19.router_ref
  158.9 4.2 pad.20.gate_in
  163.1 2.1 pad.21.up_in
  165.2 0.6 copy-done.1
  165.9 2.1 pad.18.down_in
  168.0 0.3 fusion.29
  168.4 0.6 compare_convert_fusion.1
  169.1 1.9 convert_subtract_fusion.pick_ref
  171.0 2.4 all-to-all-done
  173.3 4.1 multiply_reduce_fusion.2
  177.7 1.6 convolution_convert_fusion
  179.2 3.5 all-to-all-start.1
  183.0 15.9 %all-gather.2.cloned.1.call-done = bf16[2304,2048]{1,0:T(8,128)(2,1)} async-done(((bf16[288,2048]{1,0:T(8,128)(2,1)}), bf16[2304,2048]{1,0:T(8,128)(2,1)}) %all-gather.2.cloned.1.call-update) | async-done | bytes 9437200 | tf_op jit(solution)/shard_map/all_gather | solution.py:2844
  198.9 12.8 %fusion.45 = f32[2304,768]{1,0:T(8,128)} fusion(bf16[2304,2048]{1,0:T(8,128)(2,1)} %all-gather.2.cloned.1.call-done, bf16[704,2048]{1,0:T(8,128)(2,1)} %convert_bitcast_fusion.2), kind=kOutput, calls=%fused_computation.126 | convolution fusion | flops 7247757312 | bytes 19398656 | tf_op jit(solution)/shard_map/rd,fd->rf/dot_general | solution.py:2890
  211.7 1.0 copy-done.3
  212.7 101.7 %ffn.1 = (bf16[8,288,2048]{2,1,0:T(8,128)(2,1)}, bf16[8,288,768]{2,1,0:T(8,128)(2,1)}, bf16[8,288,768]{2,1,0:T(8,128)(2,1)}, bf16[8,288,768]{2,1,0:T(8,128)(2,1)...) custom-call(bf16[288,2048]{1,0:T(8,128)(2,1)} %bitcast.144, f32[8,288,768]{2,1,0:T(8,128)} %bitcast.139, ...), custom_call_target="tpu_custom_call" | custom-call | tf_op jit(solution)/shard_map/ffn/pallas_call | solution.py:1027
  314.6 0.8 copy-done.4
  315.6 4.8 all-to-all-start.2
  320.5 13.6 %convolution_bitcast_fusion.2 = f32[1,704,2048]{2,1,0:T(8,128)} fusion(bf16[2304,2048]{1,0:T(8,128)(2,1)} %all-gather.2.cloned.1.call-done, bf16[2304,768]{1,0:T(8,128)(2,1)} %bitcast.184), kind=kOutput, calls=%fused_computation.7 | convolution fusion | flops 6643777536 | bytes 18743296 | tf_op jit(solution)/shard_map/rf,rd->fd/dot_general | solution.py:2909
  334.1 11.2 %convolution_bitcast_fusion.1 = f32[1,2048,704]{1,2,0:T(8,128)} fusion(bf16[2304,2048]{1,0:T(8,128)(2,1)} %bitcast.180, bf16[2304,768]{1,0:T(8,128)(2,1)S(1)} %bitcast.183), kind=kOutput, calls=%fused_computation.6 | convolution fusion | flops 6643777536 | bytes 18743296 | tf_op jit(solution)/shard_map/rd,rf->df/dot_general | solution.py:2915
  345.3 5.1 all-to-all-done.2
  350.6 0.5 convolution_bitcast_fusion.3
  351.0 1.0 multiply_reduce_fusion.3
  352.0 1.5 subtract_add_fusion
  353.5 1.6 convolution_convert_fusion.1
  355.1 4.3 all-to-all-start.3
  359.7 12.2 %convolution_bitcast_fusion = f32[1,2048,704]{1,2,0:T(8,128)} fusion(bf16[2304,2048]{1,0:T(8,128)(2,1)} %bitcast.181, bf16[2304,768]{1,0:T(8,128)(2,1)} %bitcast.182), kind=kOutput, calls=%fused_computation.5 | convolution fusion | flops 6643777536 | bytes 18743296 | tf_op jit(solution)/shard_map/rd,rf->df/dot_general | solution.py:2921
  371.9 15.6 %all-to-all-done.3 = bf16[4,72,2048]{2,1,0:T(8,128)(2,1)} async-done(((bf16[4,72,2048]{2,1,0:T(8,128)(2,1)}), bf16[4,72,2048]{2,1,0:T(8,128)(2,1)}, u32[]{:S(2)}, u32[]{:S(2)}) %all-to-all-start.3) | async-done | bytes 1179680 | tf_op jit(solution)/shard_map/all_to_all | solution.py:2763
  387.5 3.5 reduce-scatter.3.cloned.1.call-done
  391.0 0.7 tile.8
  391.7 0.7 tile.20
  392.5 83.6 %attend_back_sums.1 = (bf16[288,2048]{1,0:T(8,128)(2,1)}, bf16[512,512]{1,0:T(8,128)(2,1)}, bf16[512,512]{1,0:T(8,128)(2,1)}, f32[256,2048]{1,0:T(8,128)}, bf16[2048,2048]{1,0:T(8,128)(2,1)}) custom-call(bf16[288,2048]{1,0:T(8,128)(2,1)} %bitcast.47.grad_in, bf16[288,2048]{1,0:T(8,128)(2,1)} %get-tuple-element.69.rows_in, ...), custom_call_target="tpu_custom_call" | custom-call | flops 60000002048 | bytes 200000000 | tf_op jit(solution)/shard_map/attend_back_sums/pallas_call | solution.py:1614
  476.1 2.5 multiply_reduce_fusion
  478.7 1.5 fusion.51
  480.3 61.0 %attend_last.1 = (f32[128,2048]{1,0:T(8,128)}, f32[64,2048]{1,0:T(8,128)}, f32[64,2048]{1,0:T(8,128)}) custom-call(bf16[288,2048]{1,0:T(8,128)(2,1)} %get-tuple-element.79.rows_in, bf16[288,512]{1,0:T(8,128)(2,1)} %get-tuple-element.80.table_in, bf16[2048,512]{1,0:T(8,128)(2,1)} %get-tuple-element.81.key_in, bf16[2048,512]{1,0:T(8,128)(2,1)} %get-tuple-element.82.value_in, ...), custom_call_target="tpu_custom_call" | custom-call | flops 40000000000 | bytes 150000000 | tf_op jit(solution)/shard_map/attend_last/pallas_call | solution.py:2616
  541.3 7.1 %all-to-all-start.4 = ((bf16[4,72,2048]{2,1,0:T(8,128)(2,1)}), bf16[4,72,2048]{2,1,0:T(8,128)(2,1)}, u32[]{:S(2)}, u32[]{:S(2)}) async-start(bf16[4,72,2048]{2,1,0:T(8,128)(2,1)} %bitcast.147), calls=%async_computation.5 | async-start | bytes 2359296 | tf_op jit(solution)/shard_map/all_to_all | solution.py:2763
  548.4 0.4 fusion.27
  548.8 3.1 fusion.18
  551.9 0.7 select_maximum_fusion.parts
  552.6 30.1 %total_small.1 = f32[16,128]{1,0:T(8,128)} custom-call(f32[16,2048]{1,0:T(8,128)} %select_maximum_fusion.parts), custom_call_target="tpu_custom_call" | custom-call | tf_op jit(solution)/shard_map/total_small/pallas_call | solution.py:292
  582.7 1.4 dynamic-slice_bitcast_fusion.4
  584.1 1.4 dynamic-slice_bitcast_fusion
  585.5 2.5 fusion.23
  588.0 2.1 multiply_reduce_fusion.1
  590.1 1.0 fusion.20
  591.2 2.9 bitcast_convert_fusion
  594.1 0.8 copy.62
  594.9 0.8 copy.63
  595.7 1.3 copy.64
  (91 shorter events, 2.4 us)
Async XLA Ops:
  7.2 191.8 %all-gather.2.cloned.1.call-start = ((), (), s32[]{:S(2)}) async-start(), calls=%async_computation.7 | async-start | bytes 10616832 | tf_op jit(solution)/shard_map/all_gather | solution.py:2844
  138.4 6.0 copy-start.15
  138.4 6.4 %copy-start = (bf16[1,128,2048]{2,1,0:T(8,128)(2,1)S(1)}, bf16[1,128,2048]{2,1,0:T(8,128)(2,1)}, u32[]{:S(2)}) copy-start(bf16[1,128,2048]{2,1,0:T(8,128)(2,1)} %param.16) | copy-start | bytes 1572868
  138.4 7.7 %copy-start.10 = (bf16[16,2048]{1,0:T(8,128)(2,1)S(1)}, bf16[16,2048]{1,0:T(8,128)(2,1)}, u32[]{:S(2)}) copy-start(bf16[16,2048]{1,0:T(8,128)(2,1)} %get-tuple-element.55) | copy-start | bytes 196612
  138.4 13.1 %slice-start = ((s8[5767168]{0:T(1024)(128)(4,1)}), s8[1572864]{0:T(1024)(128)(4,1)S(1)}, s32[]{:S(2)}) async-start(s8[5767168]{0:T(1024)(128)(4,1)} %bitcast.140), calls=%async_computation.10 | async-start | bytes 3145728
  138.4 34.9 %all-to-all-start = ((bf16[4,72,2048]{2,1,0:T(8,128)(2,1)}), bf16[4,72,2048]{2,1,0:T(8,128)(2,1)}, u32[]{:S(2)}, u32[]{:S(2)}) async-start(bf16[4,72,2048]{2,1,0:T(8,128)(2,1)} %bitcast.149), calls=%async_computation | async-start | bytes 2359296 | tf_op jit(solution)/shard_map/all_to_all | solution.py:2763
  146.1 21.9 %copy-start.16 = (f32[128]{0:T(128)}, f32[128]{0:T(128)S(1)}, u32[]{:S(2)}) copy-start(f32[128]{0:T(128)S(1)} %get-tuple-element.121) | copy-start | bytes 1540
  146.1 21.9 %copy-start.13 = (f32[1,2048]{1,0:T(1,128)}, f32[1,2048]{1,0:T(1,128)S(1)}, u32[]{:S(2)}) copy-start(f32[1,2048]{1,0:T(1,128)S(1)} %get-tuple-element.110) | copy-start | bytes 24580
  146.1 5.4 slice-start.1
  146.1 8.0 %slice-start.2 = ((s8[5767168]{0:T(1024)(128)(4,1)}), s8[4194304]{0:T(1024)(128)(4,1)S(1)}, s32[]{:S(2)}) async-start(s8[5767168]{0:T(1024)(128)(4,1)} %bitcast.142), calls=%async_computation.12 | async-start | bytes 8388608
  151.5 3.3 slice-start.3
  154.8 2.7 copy-start.19
  158.3 4.8 copy-start.2
  163.1 2.8 copy-start.1
  165.9 7.5 %copy-start.9 = (bf16[288,128]{1,0:T(8,128)(2,1)S(1)}, bf16[288,128]{1,0:T(8,128)(2,1)}, u32[]{:S(2)}) copy-start(bf16[288,128]{1,0:T(8,128)(2,1)} %get-tuple-element.56) | copy-start | bytes 221188
  173.3 4.3 copy-start.8
  179.2 32.5 %all-to-all-start.1 = ((bf16[4,72,2048]{2,1,0:T(8,128)(2,1)}), bf16[4,72,2048]{2,1,0:T(8,128)(2,1)S(1)}, u32[]{:S(2)}, u32[]{:S(2)}) async-start(bf16[4,72,2048]{2,1,0:T(8,128)(2,1)} %convolution_convert_fusion), calls=%async_computation.1 | async-start | bytes 2359296 | tf_op jit(solution)/shard_map/all_to_all | solution.py:2763
  182.8 208.2 %reduce-scatter.3.cloned.1.call-start = ((), (), s32[]{:S(2)}) async-start(), calls=%async_computation.8 | async-start | bytes 10616832 | tf_op jit(solution)/shard_map/reduce_scatter | solution.py:2907
  211.7 1.0 copy-start.3
  314.6 0.8 copy-start.4
  315.6 34.7 %all-to-all-start.2 = ((bf16[4,72,2176]{2,1,0:T(8,128)(2,1)}), bf16[4,72,2176]{2,1,0:T(8,128)(2,1)S(1)}, u32[]{:S(2)}, u32[]{:S(2)}) async-start(bf16[4,72,2176]{2,1,0:T(8,128)(2,1)} %bitcast.146), calls=%async_computation.2 | async-start | bytes 2506752 | tf_op jit(solution)/shard_map/all_to_all | solution.py:2763
  320.5 13.6 %copy-start.20 = (bf16[8,288,768]{2,1,0:T(8,128)(2,1)S(1)}, bf16[8,288,768]{2,1,0:T(8,128)(2,1)}, u32[]{:S(2)}) copy-start(bf16[8,288,768]{2,1,0:T(8,128)(2,1)} %get-tuple-element.64) | copy-start | bytes 10616836
  355.1 32.4 %all-to-all-start.3 = ((bf16[4,72,2048]{2,1,0:T(8,128)(2,1)}), bf16[4,72,2048]{2,1,0:T(8,128)(2,1)}, u32[]{:S(2)}, u32[]{:S(2)}) async-start(bf16[4,72,2048]{2,1,0:T(8,128)(2,1)} %convolution_convert_fusion.1), calls=%async_computation.3 | async-start | bytes 2359296 | tf_op jit(solution)/shard_map/all_to_all | solution.py:2763
  359.4 231.8 %reduce-scatter.5.cloned.1.call-start = ((), (), s32[]{:S(2)}) async-start(), calls=%async_computation.9 | async-start | bytes 9437184 | tf_op jit(solution)/shard_map/reduce_scatter | solution.py:2969
  359.7 31.3 %copy-start.12 = (f32[128,128]{1,0:T(8,128)S(1)}, f32[128,128]{1,0:T(8,128)}, u32[]{:S(2)}) copy-start(f32[128,128]{1,0:T(8,128)} %get-tuple-element.128.cos_home) | copy-start | bytes 196612
  359.7 32.0 %copy-start.11 = (f32[128,128]{1,0:T(8,128)S(1)}, f32[128,128]{1,0:T(8,128)}, u32[]{:S(2)}) copy-start(f32[128,128]{1,0:T(8,128)} %get-tuple-element.129.sin_home) | copy-start | bytes 196612
  480.3 68.1 %copy-start.14 = (f32[1,2048]{1,0:T(1,128)S(1)}, f32[1,2048]{1,0:T(1,128)}, u32[]{:S(2)}) copy-start(f32[1,2048]{1,0:T(1,128)} %copy-done.13) | copy-start | bytes 24580
  480.3 68.1 %copy-start.17 = (f32[128]{0:T(128)S(1)}, f32[128]{0:T(128)}, u32[]{:S(2)}) copy-start(f32[128]{0:T(128)} %copy-done.16) | copy-start | bytes 1540
  541.3 44.2 %copy-start.18 = (f32[128]{0:T(128)S(1)}, f32[128]{0:T(128)}, u32[]{:S(2)}) copy-start(f32[128]{0:T(128)} %get-tuple-element.120) | copy-start | bytes 1540
  541.3 46.7 %all-to-all-start.4 = ((bf16[4,72,2048]{2,1,0:T(8,128)(2,1)}), bf16[4,72,2048]{2,1,0:T(8,128)(2,1)}, u32[]{:S(2)}, u32[]{:S(2)}) async-start(bf16[4,72,2048]{2,1,0:T(8,128)(2,1)} %bitcast.147), calls=%async_computation.5 | async-start | bytes 2359296 | tf_op jit(solution)/shard_map/all_to_all | solution.py:2763
  590.1 4.0 copy-start.7
  590.1 4.8 copy-start.6
  591.2 4.5 copy-start.5
Sparse Core Ops, SparseCore 0:
  138.6 60.3 all-gather.1
  314.5 76.4 reduce-scatter.2
  476.2 81.8 reduce-scatter.4
